TPU v7x, 256 devices: a whole 4x4x8 slice. The times are simulated.
256 devices in a mesh: freq: 4 (over x_hi, core), order: 64 (over z, y, x_lo).
Axes of the slice: x: 4 (x_hi: 2, x_lo: 2; x = x_hi * 2 + x_lo), y: 4, z: 8, core: 2. Of those that a mesh axis runs over, the one named last changes fastest.
Arguments:
- harmonics: bfloat16 [32, 128, 2, 4096], P(None, 'order'), may hold values from -6 to 6
- legendre: bfloat16 [128, 4096, 512], P('order'), may hold values from -0.09375 to 0.09375
- beam_window: float32 [4, 4096], replicated, may hold values from 0.2 to 1
- order_ids: int32 [128], replicated, may hold values from 0 to 4095, as said below
- noise_weight: float32 [4, 512, 8192], P('freq', 'order'), may hold values from 0.3 to 3
Outputs:
- applied: float32 [32, 128, 2, 4096], P('freq', 'order')
Inputs may be any that keep to these rules, and one draw needn't show every extreme that they name: `order_ids`: all distinct; slots 2k and 2k + 1 hold the orders m and 4095 - m for some m < 2048; one pair holds the orders 0 and 4095.
All inputs are finite; a program needn't handle non-finite values.
Results may differ from a plain program's by a relative error of at most 0.0027.
Values may be sent and summed in bfloat16 or wider, within the bound.
No kernel may reach another device: no remote copies, remote signals or barrier semaphores. Data moves between devices by JAX's collectives and lax.ppermute only.
A program may use at most 64 MiB of HBM per device.

v0:
```python
import math

import jax
import jax.numpy as jnp
from jax import lax
from jax.sharding import PartitionSpec as P

ORD_DEV = 2


def make_table(order_ids, nlon):
    steps = jnp.arange(nlon, dtype=jnp.int32)
    turns = order_ids[:, None] * steps[None, :] % nlon
    angle = turns.astype(jnp.float32) * (2.0 * math.pi / nlon)
    factor = jnp.where(order_ids == 0, 1.0, 2.0).astype(jnp.float32)[:, None]
    return jnp.stack([factor * jnp.cos(angle), -factor * jnp.sin(angle)], 1).astype(jnp.bfloat16)


def on_device(harmonics, legendre, beam_window, order_ids, noise_weight):
    degrees = harmonics.shape[3]
    nlon = noise_weight.shape[2]
    orders_all = order_ids.shape[0]
    first_slot = lax.axis_index("order") * ORD_DEV
    local_ids = lax.dynamic_slice_in_dim(order_ids, first_slot, ORD_DEV, 0)
    live_mask = (jnp.arange(degrees, dtype=jnp.int32)[None, :] >= local_ids[:, None]).astype(
        jnp.float32
    )
    own_beam = lax.dynamic_index_in_dim(beam_window, lax.axis_index("freq"), 0, keepdims=False)
    own_shaping = (own_beam[None, :] * live_mask)[None, :, None, :]
    smoothed = (harmonics.astype(jnp.float32) * own_shaping).astype(jnp.bfloat16)
    columns = jnp.einsum(
        "bocl,olr->bocr", smoothed, legendre, preferred_element_type=jnp.float32
    ).astype(jnp.bfloat16)
    dft_table = make_table(order_ids, nlon)
    fwd_scale = 1.0 / math.sqrt(2.0 * orders_all)
    back_scale = 1.0 / math.sqrt(1.0 * nlon)
    pixel_weights = noise_weight[0]
    field = (
        jnp.einsum(
            "bocr,ocj->brj",
            lax.all_to_all(columns, "order", split_axis=3, concat_axis=1, tiled=True),
            dft_table,
            preferred_element_type=jnp.float32,
        )
        * fwd_scale
    )
    weighted = (field * pixel_weights[None]).astype(jnp.bfloat16)
    summed = jnp.einsum("brj,ocj->bocr", weighted, dft_table, preferred_element_type=jnp.float32)
    band_terms = (summed * back_scale).astype(jnp.bfloat16)
    returned = lax.all_to_all(band_terms, "order", split_axis=1, concat_axis=3, tiled=True)
    projected = (
        jnp.einsum("bocr,olr->bocl", returned, legendre, preferred_element_type=jnp.float32)
        * own_shaping
    )
    return lax.psum_scatter(projected, "freq", scatter_dimension=0, tiled=True)


def solution(mesh):
    return jax.shard_map(
        on_device,
        mesh=mesh,
        in_specs=(
            P(None, "order", None, None),
            P("order", None, None),
            P(),
            P(),
            P("freq", "order", None),
        ),
        out_specs=P("freq", "order", None, None),
        check_vma=False,
    )
```

profile of v0, /device:TPU:1, one launch (start us, length us, event | category | flops | bytes accessed | tf_op | source)
XLA Modules:
  0.0 132.2 jit_solution(3402265347176146127)
XLA Ops:
  6.5 0.0 copy-start
  6.5 0.8 dynamic_slice.7
  7.3 0.1 copy-done
  7.4 0.1 compare_select_fusion
  7.5 2.3 %multiply_convert_fusion.2 = bf16[32,2,2,4096]{3,2,1,0:T(2,128)(2,1)S(1)} fusion(bf16[32,2,2,4096]{3,2,1,0:T(2,128)(2,1)} %param.5, f32[2,4096]{1,0:T(2,128)S(1)} %compare_select_fusion), kind=kLoop, calls=%fused_computation.25 | loop fusion | flops 1572864 | bytes 2129920 | tf_op jit(solution)/shard_map/convert_element_type | solution.py:30
  9.8 0.0 copy-start.2
  9.8 5.1 %fusion.37 = bf16[32,2,2,512]{3,0,2,1:T(8,128)(2,1)S(1)} fusion(bf16[2,4096,512]{2,1,0:T(8,128)(2,1)} %param.6, bf16[32,2,2,4096]{3,2,1,0:T(2,128)(2,1)S(1)} %multiply_convert_fusion.2), kind=kOutput, calls=%fused_computation.29 | convolution fusion | flops 536936448 | bytes 9568256 | tf_op jit(solution)/shard_map/bocl,olr->bocr/dot_general | solution.py:31
  14.9 0.0 copy-start.1
  14.9 0.4 copy.17
  15.3 1.1 reshape.174
  16.4 13.6 %all-to-all-start = ((bf16[64,2,512]{2,1,0:T(2,128)(2,1)}), bf16[64,2,512]{2,1,0:T(2,128)(2,1)S(1)}, u32[]{:S(2)}, u32[]{:S(2)}) async-start(bf16[64,2,512]{2,1,0:T(2,128)(2,1)} %reshape.174), calls=%async_computation | async-start | bytes 262144 | tf_op jit(solution)/shard_map/all_to_all | solution.py:41
  29.9 0.0 reduce-scatter.2.cloned.1.call-start
  30.0 0.0 copy-done.2
  30.0 19.1 %multiply_convert_fusion.1 = (bf16[128,1,8192]{2,0,1:T(8,128)(2,1)S(1)}, bf16[128,1,8192]{2,0,1:T(8,128)(2,1)}) fusion(s32[128]{0:T(128)S(1)} %copy-done.2, f32[128]{0:T(128)S(1)} %get-tuple-element.7, f32[128]{0:T(128)S(1)} %get-tuple-element.8), kind=kLoop, calls=%fused_computation.21 | loop fusion | flops 18874368 | bytes 4195840 | tf_op jit(solution)/shard_map/convert
  49.1 0.0 copy-done.1
  49.1 0.0 all-to-all-done
  49.1 0.3 reshape.175
  49.4 0.1 copy.39
  49.5 0.1 copy.19
  49.6 4.8 %fusion.40 = bf16[32,128,2,8]{1,0,3,2:T(8,128)(2,1)S(1)} fusion(f32[8,8192]{1,0:T(8,128)S(1)} %multiply_bitcast_fusion, bf16[128,1,8192]{2,0,1:T(8,128)(2,1)} %get-tuple-element.6, bf16[128,1,8192]{2,0,1:T(8,128)(2,1)S(1)} %get-tuple-element.5, bf16[32,128,2,8]{0,3,2,1:T(8,128)(2,1)S(1)} %bitcast.93), kind=kOutput, calls=%fused_computation.30 | convolution fusion | flops 2162294784 | bytes 4718592 | tf_op jit(solution)/shard_map/brj,ocj->bocr/dot_general | solution.py:48
  54.4 0.4 copy.21
  54.8 0.4 reshape.176
  55.2 20.3 %all_to_all.36 = bf16[64,2,512]{2,1,0:T(2,128)(2,1)S(1)} all-to-all(bf16[64,2,512]{2,1,0:T(2,128)(2,1)S(1)} %reshape.176), channel_id=1, replica_groups=mesh['freq'=4,'order'=64] {'order'}, dimensions={0} | all-to-all | bytes 262144 | tf_op jit(solution)/shard_map/all_to_all | solution.py:50
  75.5 0.3 reshape.177
  75.8 7.4 %fusion.10 = f32[32,2,2,4096]{3,0,2,1:T(8,128)} fusion(bf16[2,4096,512]{2,1,0:T(8,128)(2,1)} %param.6, f32[2,4096]{1,0:T(2,128)S(1)} %compare_select_fusion, bf16[32,2,2,64,8]{0,4,2,1,3:T(8,128)(2,1)S(1)} %bitcast.92), kind=kOutput, calls=%fused_computation.12 | convolution fusion | flops 537395200 | bytes 10649600 | tf_op jit(solution)/shard_map/bocr,olr->bocl/dot_general | solution.py:52
  83.2 0.0 reduce-scatter.2.cloned.1.call-update
  83.2 39.9 %reduce-scatter.2.cloned.1.call-done = f32[8,2,2,4096]{3,0,2,1:T(8,128)} async-done(((f32[32,2,2,4096]{3,0,2,1:T(8,128)}), f32[8,2,2,4096]{3,0,2,1:T(8,128)}) %reduce-scatter.2.cloned.1.call-update) | async-done | bytes 524304 | tf_op jit(solution)/shard_map/reduce_scatter | solution.py:55
  123.1 2.2 %copy.24 = f32[8,2,2,4096]{3,2,1,0:T(2,128)} copy(f32[8,2,2,4096]{3,0,2,1:T(8,128)} %reduce-scatter.2.cloned.1.call-done) | data formatting | bytes 1048576 | tf_op jit(solution)/shard_map/reduce_scatter | solution.py:55
  (3 shorter events, 0.0 us)
Async XLA Ops:
  6.5 0.8 copy-start
  9.8 20.2 %copy-start.2 = (s32[128]{0:T(128)S(1)}, s32[128]{0:T(128)}, u32[]{:S(2)}) copy-start(s32[128]{0:T(128)} %param.8) | copy-start | bytes 1540
  14.9 34.2 %copy-start.1 = (f32[1,8,8192]{2,1,0:T(8,128)S(1)}, f32[1,8,8192]{2,1,0:T(8,128)}, u32[]{:S(2)}) copy-start(f32[1,8,8192]{2,1,0:T(8,128)} %param.9) | copy-start | bytes 786436
  16.4 32.8 %all-to-all-start = ((bf16[64,2,512]{2,1,0:T(2,128)(2,1)}), bf16[64,2,512]{2,1,0:T(2,128)(2,1)S(1)}, u32[]{:S(2)}, u32[]{:S(2)}) async-start(bf16[64,2,512]{2,1,0:T(2,128)(2,1)} %reshape.174), calls=%async_computation | async-start | bytes 262144 | tf_op jit(solution)/shard_map/all_to_all | solution.py:41
  29.9 93.2 %reduce-scatter.2.cloned.1.call-start = ((), (), s32[]{:S(2)}) async-start(), calls=%async_computation.3 | async-start | bytes 2621440 | tf_op jit(solution)/shard_map/reduce_scatter | solution.py:55
Sparse Core Ops, SparseCore 0:
  83.3 39.7 reduce-scatter.1
where the time goes:
time: 133 us; the launch traced here: 132 us
  waiting for transfers between devices  39.9 us (30%)
  other arithmetic  21.5 us (16%)
  blocking collectives  20.3 us (15%)
  matrix products  17.3 us (13%)
  starting transfers between devices  13.6 us (10%)
  between operations  13.5 us (10%)
  local copies, waits for them, and re-layouts  6.13 us (5%)
    reduce_scatter x1, waiting for transfers between devices, on_device(): return lax.psum_scatter(projected, 'freq', scatter_dimension=0, tiled=True)  39.9 us
    all_to_all x1, blocking collectives, on_device(): lax.all_to_all(band_terms, 'order', split_axis=1, concat_axis=3, tiled=True)  20.3 us
    another operation x1, other arithmetic  19.1 us
    all_to_all x1, starting transfers between devices, on_device(): lax.all_to_all(columns, 'order', split_axis=3, concat_axis=1, tiled=True)  13.6 us
    dot_general x1, matrix products, on_device(): jnp.einsum('bocr,olr->bocl', returned, legendre, preferred_element_type=j...  7.42 us
    dot_general x1, matrix products, on_device(): jnp.einsum('bocl,olr->bocr', smoothed, legendre, preferred_element_type=j...  5.05 us
    dot_general x1, matrix products, on_device(): jnp.einsum('brj,ocj->bocr', weighted, dft_table, preferred_element_type=j...  4.78 us
  transfers between devices with their start and end apart: 2, of which 1 were waited for; matrix products, arithmetic and copies ran while one was open for 14% of the time, Pallas kernels for 0%

commit v1 on v0

--- a/solution.py
+++ b/solution.py
@@ -9,17 +9,28 @@
 
 
 def make_table(order_ids, nlon):
-    steps = jnp.arange(nlon, dtype=jnp.int32)
-    turns = order_ids[:, None] * steps[None, :] % nlon
-    angle = turns.astype(jnp.float32) * (2.0 * math.pi / nlon)
+    fine = 128
+    coarse = nlon // fine
+    unit = 2.0 * math.pi / nlon
+    a_turns = order_ids[:, None] * (fine * jnp.arange(coarse, dtype=jnp.int32))[None, :] % nlon
+    b_turns = order_ids[:, None] * jnp.arange(fine, dtype=jnp.int32)[None, :] % nlon
+    a = a_turns.astype(jnp.float32) * unit
+    b = b_turns.astype(jnp.float32) * unit
     factor = jnp.where(order_ids == 0, 1.0, 2.0).astype(jnp.float32)[:, None]
-    return jnp.stack([factor * jnp.cos(angle), -factor * jnp.sin(angle)], 1).astype(jnp.bfloat16)
+    ca, sa = (factor * jnp.cos(a))[:, :, None], (factor * jnp.sin(a))[:, :, None]
+    cb, sb = jnp.cos(b)[:, None, :], jnp.sin(b)[:, None, :]
+    cos = (ca * cb - sa * sb).astype(jnp.bfloat16).reshape(-1, nlon)
+    sin = (-(sa * cb + ca * sb)).astype(jnp.bfloat16).reshape(-1, nlon)
+    return jnp.stack([cos, sin], 1)
 
 
 def on_device(harmonics, legendre, beam_window, order_ids, noise_weight):
+    maps = harmonics.shape[0]
     degrees = harmonics.shape[3]
+    lats = legendre.shape[2]
     nlon = noise_weight.shape[2]
     orders_all = order_ids.shape[0]
+    groups = beam_window.shape[0]
     first_slot = lax.axis_index("order") * ORD_DEV
     local_ids = lax.dynamic_slice_in_dim(order_ids, first_slot, ORD_DEV, 0)
     live_mask = (jnp.arange(degrees, dtype=jnp.int32)[None, :] >= local_ids[:, None]).astype(
@@ -47,12 +58,18 @@
     weighted = (field * pixel_weights[None]).astype(jnp.bfloat16)
     summed = jnp.einsum("brj,ocj->bocr", weighted, dft_table, preferred_element_type=jnp.float32)
     band_terms = (summed * back_scale).astype(jnp.bfloat16)
-    returned = lax.all_to_all(band_terms, "order", split_axis=1, concat_axis=3, tiled=True)
-    projected = (
-        jnp.einsum("bocr,olr->bocl", returned, legendre, preferred_element_type=jnp.float32)
-        * own_shaping
-    )
-    return lax.psum_scatter(projected, "freq", scatter_dimension=0, tiled=True)
+    own_maps = maps // groups
+    order_devs = orders_all // ORD_DEV
+    rows = lats // order_devs
+    send = band_terms.reshape(groups, own_maps, order_devs, ORD_DEV, 2, rows)
+    send = send.transpose(0, 2, 3, 4, 1, 5).reshape(groups * order_devs, 2, -1)
+    got = lax.all_to_all(send, ("freq", "order"), split_axis=0, concat_axis=0, tiled=True)
+    got = got.reshape(groups, order_devs, ORD_DEV, 2, own_maps, rows)
+    got = got.transpose(2, 0, 3, 4, 1, 5).reshape(ORD_DEV, groups, 2, own_maps, lats)
+    projected = jnp.einsum("ofcbr,olr->ofcbl", got, legendre, preferred_element_type=jnp.float32)
+    shaping = beam_window[None, :, :] * live_mask[:, None, :]
+    total = jnp.sum(projected * shaping[:, :, None, None, :], axis=1)
+    return total.transpose(2, 0, 1, 3)
 
 
 def solution(mesh):

time: 133 us -> 89 us (0.67)
  waiting for transfers between devices: 39.9 us -> 12.6 us
  blocking collectives: 20.3 us -> 0 us
  local copies, waits for them, and re-layouts: 6.13 us -> 26.4 us
  other arithmetic: 21.5 us -> 6.65 us
  between operations: 13.5 us -> 0.25 us
  starting transfers between devices: 13.6 us -> 26.6 us
    reduce_scatter x1 -> x0, waiting for transfers between devices: 39.9 us -> none  [on_device(): return lax.psum_scatter(projected, 'freq', scatter_dimension=0, tiled=True)]
    all_to_all x1 -> x0, blocking collectives: 20.3 us -> none  [on_device(): lax.all_to_all(band_terms, 'order', split_axis=1, concat_axis=3, tiled=True)]
    another operation x1 -> x0, other arithmetic: 19.1 us -> none
    all_to_all x0 -> x1, starting transfers between devices: none -> 13 us  [on_device(): lax.all_to_all(send, ('freq', 'order'), split_axis=0, concat_axis=0, tile...]
    all_to_all x0 -> x1, waiting for transfers between devices: none -> 12.6 us  [on_device(): lax.all_to_all(send, ('freq', 'order'), split_axis=0, concat_axis=0, tile...]
    convert_element_type x0 -> x2, local copies, waits for them, and re-layouts: none -> 6.45 us  [the longest x1 4.16 us: make_table(): cos = (ca * cb - sa * sb).astype(jnp.bfloat16).reshape(-1, nlon)]
    reshape x0 -> x5, local copies, waits for them, and re-layouts: none -> 4.96 us  [the longest x1 2.95 us: on_device(): got.transpose(2, 0, 3, 4, 1, 5).reshape(ORD_DEV, groups, 2, own_maps, lats)]
    transpose x0 -> x3, local copies, waits for them, and re-layouts: none -> 4.7 us  [the longest x1 2.51 us: on_device(): send = send.transpose(0, 2, 3, 4, 1, 5).reshape(groups * order_devs, 2, -1)]
  transfers between devices with their start and end apart: 2 -> 2, of which waited for: 1 -> 1; matrix products, arithmetic and copies ran while one was open for 14% -> 19% of each run, Pallas kernels for 0% -> 0%
where the time goes in v1:
time: 89 us; the launch traced here: 88.6 us
  starting transfers between devices  26.6 us (30%)
  local copies, waits for them, and re-layouts  26.4 us (30%)
  matrix products  16.1 us (18%)
  waiting for transfers between devices  12.6 us (14%)
  other arithmetic  6.65 us (7%)
    all_to_all x1, starting transfers between devices, on_device(): lax.all_to_all(columns, 'order', split_axis=3, concat_axis=1, tiled=True)  13.6 us
    all_to_all x1, starting transfers between devices, on_device(): lax.all_to_all(send, ('freq', 'order'), split_axis=0, concat_axis=0, tile...  13 us
    all_to_all x1, waiting for transfers between devices, on_device(): lax.all_to_all(send, ('freq', 'order'), split_axis=0, concat_axis=0, tile...  12.6 us
    dot_general x1, matrix products, on_device(): jnp.einsum('ofcbr,olr->ofcbl', got, legendre, preferred_element_type=jnp....  6.05 us
    dot_general x1, matrix products, on_device(): jnp.einsum('bocl,olr->bocr', smoothed, legendre, preferred_element_type=j...  5.05 us
    unnamed x11, local copies, waits for them, and re-layouts  4.54 us
    convert_element_type x1, local copies, waits for them, and re-layouts, make_table(): cos = (ca * cb - sa * sb).astype(jnp.bfloat16).reshape(-1, nlon)  4.16 us
    dot_general x1, matrix products, on_device(): jnp.einsum('bocr,ocj->brj', lax.all_to_all(columns, 'order', split_axis=3...  3.72 us
  transfers between devices with their start and end apart: 2, of which 1 were waited for; matrix products, arithmetic and copies ran while one was open for 19% of the time, Pallas kernels for 0%

profile of v1, /device:TPU:1, one launch (start us, length us, event | category | flops | bytes accessed | tf_op | source)
XLA Modules:
  0.0 88.6 jit_solution(12213753365926483351)
XLA Ops:
  0.0 0.7 dynamic_slice.7
  0.7 0.9 constant_dynamic-slice_fusion
  1.6 0.1 fusion.43
  1.7 2.3 %multiply_convert_fusion = bf16[32,2,2,4096]{3,2,1,0:T(2,128)(2,1)S(1)} fusion(bf16[32,2,2,4096]{3,2,1,0:T(2,128)(2,1)} %param.5, f32[2,4096]{1,0:T(2,128)S(1)} %fusion.43), kind=kLoop, calls=%fused_computation.14 | loop fusion | flops 1572864 | bytes 2129920 | tf_op jit(solution)/shard_map/convert_element_type | solution.py:41
  4.0 5.1 %fusion.25 = bf16[32,2,2,512]{3,0,2,1:T(8,128)(2,1)S(1)} fusion(bf16[2,4096,512]{2,1,0:T(8,128)(2,1)} %param.6, bf16[32,2,2,4096]{3,2,1,0:T(2,128)(2,1)S(1)} %multiply_convert_fusion), kind=kOutput, calls=%fused_computation.19 | convolution fusion | flops 536936448 | bytes 9568256 | tf_op jit(solution)/shard_map/bocl,olr->bocr/dot_general | solution.py:42
  9.1 0.4 copy.14
  9.5 1.1 %reshape.328 = bf16[64,2,512]{2,1,0:T(2,128)(2,1)} reshape(bf16[512,2,2,32]{3,2,1,0:T(2,128)(2,1)S(1)} %bitcast.73) | data formatting | bytes 262144
  10.5 13.6 %all-to-all-start = ((bf16[64,2,512]{2,1,0:T(2,128)(2,1)}), bf16[64,2,512]{2,1,0:T(2,128)(2,1)S(1)}, u32[]{:S(2)}, u32[]{:S(2)}) async-start(bf16[64,2,512]{2,1,0:T(2,128)(2,1)} %reshape.328), calls=%async_computation | async-start | bytes 262144 | tf_op jit(solution)/shard_map/all_to_all | solution.py:52
  24.1 0.3 fusion.45
  24.5 0.3 cosine_multiply_fusion
  24.8 3.5 %negate_convert_fusion = (bf16[128,64,128]{2,1,0:T(8,128)(2,1)S(1)}, bf16[128,64,128]{2,1,0:T(8,128)(2,1)}) fusion(f32[128,128]{1,0:T(8,128)S(1)} %get-tuple-element.10, f32[128,64]{1,0:T(8,128)S(1)} %get-tuple-element.8, f32[128,128]{1,0:T(8,128)S(1)} %get-tuple-element.9, f32[128,64]{1,0:T(8,128)S(1)} %get-tuple-element.7), kind=kLoop, calls=%fused_computation.12 | loop fusion | flops 9437184 | bytes 4390912 | tf_op jit(solution)/shard_map/convert_element_type | solution.py:23
  28.3 4.2 %convert_element_type.77 = bf16[128,1,8192]{2,0,1:T(8,128)(2,1)} reshape(bf16[128,64,128]{2,1,0:T(8,128)(2,1)} %get-tuple-element.6) | data formatting | bytes 4194304 | tf_op jit(solution)/shard_map/convert_element_type | solution.py:22
  32.5 3.2 %constant_dynamic-update-slice_fusion.1 = bf16[128,2,8192]{2,0,1:T(8,128)(2,1)} fusion(bf16[128,1,8192]{2,0,1:T(8,128)(2,1)} %convert_element_type.77), kind=kLoop, calls=%fused_computation.51 | loop fusion | bytes 4194304
  35.6 2.3 %convert_element_type.79 = bf16[128,1,8192]{2,0,1:T(8,128)(2,1)} reshape(bf16[128,64,128]{2,1,0:T(8,128)(2,1)S(1)} %get-tuple-element.5) | data formatting | bytes 4194304 | tf_op jit(solution)/shard_map/convert_element_type | solution.py:23
  37.9 3.1 %constant_dynamic-update-slice_fusion = bf16[128,2,8192]{2,0,1:T(8,128)(2,1)} fusion(bf16[128,2,8192]{2,0,1:T(8,128)(2,1)} %constant_dynamic-update-slice_fusion.1, bf16[128,1,8192]{2,0,1:T(8,128)(2,1)} %convert_element_type.79), kind=kLoop, calls=%fused_computation.50 | loop fusion | bytes 4194304 | tf_op jit(solution)/shard_map/stack | solution.py:24
  41.1 0.3 reshape.329
  41.5 0.1 copy.16
  41.6 3.7 %fusion.2 = bf16[32,8,8192,1]{2,0,1,3:T(8,128)(2,1)S(1)} fusion(bf16[128,2,8192]{2,0,1:T(8,128)(2,1)} %constant_dynamic-update-slice_fusion, f32[8,8192]{1,0:T(8,128)S(1)} %multiply_bitcast_fusion, bf16[32,128,2,8]{0,3,2,1:T(8,128)(2,1)S(1)} %bitcast.77), kind=kOutput, calls=%fused_computation.3 | convolution fusion | flops 1077936128 | bytes 8781824 | tf_op jit(solution)/shard_map/bocr,ocj->brj/dot_general | solution.py:50
  45.3 1.3 %fusion.28 = bf16[32,128,2,8]{1,0,3,2:T(8,128)(2,1)S(1)} fusion(bf16[32,8,8192,1]{2,0,1,3:T(8,128)(2,1)S(1)} %fusion.2, bf16[128,2,8192]{2,0,1:T(8,128)(2,1)S(1)} %copy-done), kind=kOutput, calls=%fused_computation.20 | convolution fusion | flops 1073872896 | bytes 8519680 | tf_op jit(solution)/shard_map/brj,ocj->bocr/dot_general | solution.py:59
  46.6 0.4 copy.18
  47.0 0.9 reshape.319
  47.9 2.5 %copy.19 = bf16[4,64,2,2,8,8]{1,0,5,4,3,2:T(4,128)(2,1)S(1)} copy(bf16[4,64,2,2,8,8]{4,0,5,3,2,1:T(4,128)(2,1)S(1)} %bitcast.72) | data formatting | bytes 262144 | tf_op jit(solution)/shard_map/transpose | solution.py:65
  50.4 0.2 reshape.320
  50.6 0.8 copy.20
  51.4 13.0 %all-to-all-start.1 = ((bf16[256,2,128]{2,1,0:T(2,128)(2,1)}), bf16[256,2,128]{2,1,0:T(2,128)(2,1)S(1)}, u32[]{:S(2)}, u32[]{:S(2)}) async-start(bf16[256,2,128]{2,1,0:T(2,128)(2,1)} %copy.20), calls=%async_computation.1 | async-start | bytes 262144 | tf_op jit(solution)/shard_map/all_to_all | solution.py:66
  64.5 12.6 %all-to-all-done.1 = bf16[256,2,128]{2,1,0:T(2,128)(2,1)S(1)} async-done(((bf16[256,2,128]{2,1,0:T(2,128)(2,1)}), bf16[256,2,128]{2,1,0:T(2,128)(2,1)S(1)}, u32[]{:S(2)}, u32[]{:S(2)}) %all-to-all-start.1) | async-done | bytes 131104 | tf_op jit(solution)/shard_map/all_to_all | solution.py:66
  77.1 0.1 copy.21
  77.2 0.2 reshape.321
  77.3 1.0 %copy.22 = bf16[2,4,2,8,64,8]{5,4,3,2,1,0:T(8,128)(2,1)S(1)} copy(bf16[2,4,2,8,64,8]{4,1,5,3,2,0:T(4,128)(2,1)S(1)} %bitcast.76) | data formatting | bytes 262144 | tf_op jit(solution)/shard_map/transpose | solution.py:68
  78.3 3.0 %reshape.322 = bf16[2,4,2,8,512]{4,3,2,1,0:T(8,128)(2,1)S(1)} reshape(bf16[2,4,2,8,64,8]{5,4,3,2,1,0:T(8,128)(2,1)S(1)} %copy.22) | data formatting | bytes 262144 | tf_op jit(solution)/shard_map/reshape | solution.py:68
  81.3 6.0 %fusion.13 = f32[2,2,8,4096]{3,2,1,0:T(8,128)S(1)} fusion(bf16[2,4,2,8,512]{4,3,2,1,0:T(8,128)(2,1)S(1)} %reshape.322, bf16[2,4096,512]{2,1,0:T(8,128)(2,1)} %param.6, f32[2,4,4096]{2,1,0:T(4,128)S(1)} %broadcast_multiply_fusion), kind=kOutput, calls=%fused_computation.15 | convolution fusion | flops 537788416 | bytes 9175040 | tf_op jit(solution)/shard_map/ofcbr,olr->ofcbl/dot_general | solution.py:69
  87.4 1.2 %copy.23 = f32[8,2,2,4096]{3,2,1,0:T(2,128)} copy(f32[8,2,2,4096]{3,0,2,1:T(8,128)S(1)} %bitcast.78) | data formatting | bytes 1048576 | tf_op jit(solution)/shard_map/transpose | solution.py:72
  (15 shorter events, 0.2 us)
Async XLA Ops:
  4.0 20.1 %copy-start.3 = (s32[128]{0:T(128)S(1)}, s32[128]{0:T(128)}, u32[]{:S(2)}) copy-start(s32[128]{0:T(128)} %param.8) | copy-start | bytes 1540
  10.5 30.6 %all-to-all-start = ((bf16[64,2,512]{2,1,0:T(2,128)(2,1)}), bf16[64,2,512]{2,1,0:T(2,128)(2,1)S(1)}, u32[]{:S(2)}, u32[]{:S(2)}) async-start(bf16[64,2,512]{2,1,0:T(2,128)(2,1)} %reshape.328), calls=%async_computation | async-start | bytes 262144 | tf_op jit(solution)/shard_map/all_to_all | solution.py:52
  32.5 5.5 %copy-start.1 = (f32[1,8,8192]{2,1,0:T(8,128)S(1)}, f32[1,8,8192]{2,1,0:T(8,128)}, u32[]{:S(2)}) copy-start(f32[1,8,8192]{2,1,0:T(8,128)} %param.9) | copy-start | bytes 786436
  41.6 3.7 %copy-start = (bf16[128,2,8192]{2,0,1:T(8,128)(2,1)S(1)}, bf16[128,2,8192]{2,0,1:T(8,128)(2,1)}, u32[]{:S(2)}) copy-start(bf16[128,2,8192]{2,0,1:T(8,128)(2,1)} %constant_dynamic-update-slice_fusion) | copy-start | bytes 12582916
  46.6 17.9 %copy-start.2 = (f32[4,4096]{1,0:T(4,128)S(1)}, f32[4,4096]{1,0:T(4,128)}, u32[]{:S(2)}) copy-start(f32[4,4096]{1,0:T(4,128)} %param.7) | copy-start | bytes 196612
  51.4 25.6 %all-to-all-start.1 = ((bf16[256,2,128]{2,1,0:T(2,128)(2,1)}), bf16[256,2,128]{2,1,0:T(2,128)(2,1)S(1)}, u32[]{:S(2)}, u32[]{:S(2)}) async-start(bf16[256,2,128]{2,1,0:T(2,128)(2,1)} %copy.20), calls=%async_computation.1 | async-start | bytes 262144 | tf_op jit(solution)/shard_map/all_to_all | solution.py:66

commit v2 on v0

v2 whole, which is shorter than its diff:
```python
import math

import jax
import jax.numpy as jnp
from jax import lax
from jax.experimental import pallas as pl
from jax.experimental.pallas import tpu as pltpu
from jax.sharding import PartitionSpec as P

ORD_DEV = 2
LANES = 128
F32 = jnp.float32
BF16 = jnp.bfloat16


def lane_ids(shape):
    return lax.broadcasted_iota(jnp.int32, shape, len(shape) - 1)


def swap_halves(a, b):
    low = lane_ids(a.shape) < LANES // 2
    first = jnp.where(low, a, pltpu.roll(b, LANES // 2, a.ndim - 1))
    second = jnp.where(low, pltpu.roll(a, LANES // 2, a.ndim - 1), b)
    return first, second


def forward_kernel(parts, ids_ref, beam_ref, harm_ref, leg_ref, out_ref, leg_v, wide, lhs, sems):
    degrees, lats = leg_ref.shape[1], leg_ref.shape[2]
    maps = out_ref.shape[1] // (2 * ORD_DEV)
    tiles = degrees // LANES
    step = degrees // parts
    copies = []
    for o in range(ORD_DEV):
        for p in range(parts):
            copy = pltpu.make_async_copy(
                leg_ref.at[o, pl.ds(p * step, step), :],
                leg_v.at[o, pl.ds(p * step, step), :],
                sems.at[o * parts + p],
            )
            copy.start()
            copies.append(copy)
    slot = lax.axis_index("order") * ORD_DEV
    group = lax.axis_index("freq")
    wide[...] = harm_ref[...].astype(F32)
    beam = beam_ref[pl.ds(group, 1), :]
    degree = lane_ids((1, degrees))
    sums = []
    for o in range(ORD_DEV):
        shaping = jnp.where(degree >= ids_ref[slot + o], beam, 0.0)
        total = jnp.zeros((2 * maps, lats), F32)
        for p in range(parts):
            for t in range(p * tiles // parts, (p + 1) * tiles // parts):
                cols = pl.ds(t * LANES, LANES)
                for c in range(2):
                    rows = wide[pl.ds((o * tiles + t) * 2 + c, maps, stride=ORD_DEV * tiles * 2), :]
                    lhs[pl.ds(c * maps, maps), cols] = (
                        rows * shaping[:, t * LANES : (t + 1) * LANES]
                    ).astype(BF16)
            copies[o * parts + p].wait()
            total += jnp.dot(
                lhs[:, pl.ds(p * step, step)],
                leg_v[o, pl.ds(p * step, step), :],
                preferred_element_type=F32,
            )
        sums.append(total)
    both = jnp.concatenate(sums, 0)
    out_ref[...] = both.T.astype(BF16)


def forward(order_ids, beam, harm, legendre, maps, parts=4):
    degrees, lats = legendre.shape[1:]
    return pl.pallas_call(
        lambda *refs: forward_kernel(parts, *refs),
        name="forward",
        out_shape=jax.ShapeDtypeStruct((lats, ORD_DEV * 2 * maps), BF16),
        in_specs=[
            pl.BlockSpec(memory_space=pltpu.SMEM),
            pl.BlockSpec(memory_space=pltpu.VMEM),
            pl.BlockSpec(memory_space=pltpu.VMEM),
            pl.BlockSpec(memory_space=pl.ANY),
        ],
        out_specs=pl.BlockSpec(memory_space=pltpu.VMEM),
        scratch_shapes=[
            pltpu.VMEM(legendre.shape, BF16),
            pltpu.VMEM(harm.shape, F32),
            pltpu.VMEM((2 * maps, degrees), BF16),
            pltpu.SemaphoreType.DMA((ORD_DEV * parts,)),
        ],
    )(order_ids, beam, harm, legendre)


def table_kernel(coarse_ref, mid_ref, fine_ref, out_ref, base):
    rows = coarse_ref.shape[1]
    mids, coarses = mid_ref.shape[2], coarse_ref.shape[2]
    fc, fs = fine_ref[0], fine_ref[1]
    for q in range(mids):
        mc, ms = mid_ref[0, :, q : q + 1], mid_ref[1, :, q : q + 1]
        cols = slice(q * LANES, (q + 1) * LANES)
        base[0, :, cols] = mc * fc - ms * fs
        base[1, :, cols] = ms * fc + mc * fs
    half = rows // ORD_DEV
    span = mids * LANES
    for p in range(coarses):
        cc, cs = coarse_ref[0, :, p : p + 1], coarse_ref[1, :, p : p + 1]
        cos = (cc * base[0] - cs * base[1]).astype(BF16)
        sin = (-(cs * base[0] + cc * base[1])).astype(BF16)
        for o in range(ORD_DEV):
            part = slice(o * half, (o + 1) * half)
            out_ref[pl.ds(o * rows, half), pl.ds(p * span, span)] = cos[part]
            out_ref[pl.ds(o * rows + half, half), pl.ds(p * span, span)] = sin[part]


def make_table(order_ids, nlon):
    ids = order_ids.reshape(-1, ORD_DEV).T.reshape(-1, 1)
    mids = 8
    coarses = nlon // (mids * LANES)
    unit = 2.0 * math.pi / nlon

    def pair(step, count, factor):
        turns = ids * (step * jnp.arange(count, dtype=jnp.int32))[None, :] % nlon
        angle = turns.astype(F32) * unit
        return jnp.stack([factor * jnp.cos(angle), factor * jnp.sin(angle)])

    factor = jnp.where(ids == 0, 1.0, 2.0).astype(F32)
    coarse = pair(mids * LANES, coarses, factor)
    mid = pair(LANES, mids, 1.0)
    fine = pair(1, LANES, 1.0)
    rows = ids.shape[0]
    return pl.pallas_call(
        table_kernel,
        name="table",
        out_shape=jax.ShapeDtypeStruct((2 * rows, nlon), BF16),
        in_specs=[pl.BlockSpec(memory_space=pltpu.VMEM)] * 3,
        out_specs=pl.BlockSpec(memory_space=pltpu.VMEM),
        scratch_shapes=[pltpu.VMEM((2, rows, mids * LANES), F32)],
    )(coarse, mid, fine)


def pixel_kernel(groups, chunk, scales, got_ref, table_ref, weight_ref, out_ref, wide, lhs, mixed):
    fwd_scale, back_scale = scales
    rows = weight_ref.shape[0]
    pairs = got_ref.shape[0] // rows
    maps = got_ref.shape[1] // (2 * ORD_DEV)
    nlon = table_ref.shape[1]
    wide[...] = got_ref[...].astype(F32)
    for r in range(0, rows, 2):
        stacked = jnp.concatenate(
            [wide[pl.ds(r + i, pairs, stride=rows), :] for i in range(2)], 0
        )
        turned = stacked.T
        for o in range(ORD_DEV):
            cos = turned[(2 * o) * maps : (2 * o + 1) * maps]
            sin = turned[(2 * o + 1) * maps : (2 * o + 2) * maps]
            for i, half in enumerate(swap_halves(cos, sin)):
                lhs[pl.ds((r + i) * maps, maps), pl.ds(o * LANES, LANES)] = half.astype(BF16)
    total = jnp.zeros((rows * maps, 2 * LANES), F32)
    for j in range(nlon // chunk):
        cols = pl.ds(j * chunk, chunk)
        part = table_ref[:, cols]
        field = jnp.dot(lhs[...], part, preferred_element_type=F32)
        weight = weight_ref[:, cols] * fwd_scale
        weighted = jnp.concatenate(
            [
                (field[r * maps : (r + 1) * maps] * weight[r : r + 1]).astype(BF16)
                for r in range(rows)
            ],
            0,
        )
        total += lax.dot_general(
            weighted, part, (((1,), (1,)), ((), ())), preferred_element_type=F32
        )
    total = total * back_scale
    own = maps // groups
    low_rows = rows // 2
    for f in range(groups):
        pieces = []
        for low in range(low_rows):
            for o in range(ORD_DEV):
                at = [(high * low_rows + low) * maps + f * own for high in range(2)]
                pieces += list(
                    swap_halves(
                        *[total[a : a + own, o * LANES : (o + 1) * LANES] for a in at]
                    )
                )
        turned = jnp.concatenate(pieces, 0).T
        for high in range(2):
            mixed[pl.ds(f * 2 * pairs + high, pairs, stride=2), :] = turned[
                high * pairs : (high + 1) * pairs
            ]
    out_ref[...] = mixed[...].astype(BF16)


def pixels(got, table, weight, groups, scales, chunk=512):
    return pl.pallas_call(
        lambda *refs: pixel_kernel(groups, chunk, scales, *refs),
        name="pixels",
        out_shape=jax.ShapeDtypeStruct(got.shape, BF16),
        in_specs=[pl.BlockSpec(memory_space=pltpu.VMEM)] * 3,
        out_specs=pl.BlockSpec(memory_space=pltpu.VMEM),
        scratch_shapes=[
            pltpu.VMEM(got.shape, F32),
            pltpu.VMEM((got.shape[0] // 2, 2 * LANES), BF16),
            pltpu.VMEM(got.shape, F32),
        ],
    )(got, table, weight)


def backward_kernel(parts, ids_ref, beam_ref, got_ref, leg_ref, out_ref, leg_v, mixed, sems):
    degrees, lats = leg_ref.shape[1], leg_ref.shape[2]
    groups = beam_ref.shape[0]
    tiles = degrees // LANES
    step = degrees // parts
    copies = []
    for o in range(ORD_DEV):
        for p in range(parts):
            copy = pltpu.make_async_copy(
                leg_ref.at[o, pl.ds(p * step, step), :],
                leg_v.at[o, pl.ds(p * step, step), :],
                sems.at[o * parts + p],
            )
            copy.start()
            copies.append(copy)
    slot = lax.axis_index("order") * ORD_DEV
    span = got_ref.shape[0] // groups
    width = LANES // groups
    lows = lats // span
    own = width // (2 * ORD_DEV)
    blocks = [got_ref[pl.ds(f * span, span), :].astype(F32) for f in range(groups)]
    lane_group = lane_ids((span, LANES)) // width
    turned = [
        [v if k == 0 else pltpu.roll(v, k * width, 1) for k in range(groups)] for v in blocks
    ]
    for low in range(lows):
        merged = turned[0][(0 - low) % groups]
        for f in range(1, groups):
            merged = jnp.where(lane_group == f, turned[f][(f - low) % groups], merged)
        mixed[pl.ds(low, span, stride=lows), :] = merged
    rows = mixed[...].T.astype(BF16)
    degree = lane_ids((1, degrees))
    for o in range(ORD_DEV):
        lhs = jnp.concatenate(
            [
                rows[f * width + o * 2 * own : f * width + (o + 1) * 2 * own]
                for f in range(groups)
            ],
            0,
        )
        for p in range(parts):
            copies[o * parts + p].wait()
            cols = slice(p * step, (p + 1) * step)
            terms = lax.dot_general(
                lhs,
                leg_v[o, pl.ds(p * step, step), :],
                (((1,), (1,)), ((), ())),
                preferred_element_type=F32,
            )
            live = degree[:, cols] >= ids_ref[slot + o]
            total = jnp.zeros((2 * own, step), F32)
            for f in range(groups):
                shaping = jnp.where(live, beam_ref[f : f + 1, cols], 0.0)
                total += terms[f * 2 * own : (f + 1) * 2 * own] * shaping
            for t in range(tiles // parts):
                for c in range(2):
                    at = o * tiles * 2 + (p * tiles // parts + t) * 2 + c
                    out_ref[pl.ds(at, own, stride=ORD_DEV * tiles * 2), :] = total[
                        c * own : (c + 1) * own, t * LANES : (t + 1) * LANES
                    ]


def backward(order_ids, beam, got, legendre, own, parts=4):
    degrees = legendre.shape[1]
    return pl.pallas_call(
        lambda *refs: backward_kernel(parts, *refs),
        name="backward",
        out_shape=jax.ShapeDtypeStruct((own * ORD_DEV * 2 * degrees // LANES, LANES), F32),
        in_specs=[
            pl.BlockSpec(memory_space=pltpu.SMEM),
            pl.BlockSpec(memory_space=pltpu.VMEM),
            pl.BlockSpec(memory_space=pltpu.VMEM),
            pl.BlockSpec(memory_space=pl.ANY),
        ],
        out_specs=pl.BlockSpec(memory_space=pltpu.VMEM),
        scratch_shapes=[
            pltpu.VMEM(legendre.shape, BF16),
            pltpu.VMEM((legendre.shape[2], LANES), F32),
            pltpu.SemaphoreType.DMA((ORD_DEV * parts,)),
        ],
    )(order_ids, beam, got, legendre)


def on_device(harmonics, legendre, beam_window, order_ids, noise_weight):
    maps, _, _, degrees = harmonics.shape
    lats = legendre.shape[2]
    nlon = noise_weight.shape[2]
    orders_all = order_ids.shape[0]
    groups = beam_window.shape[0]
    tiles = degrees // LANES
    own = maps // groups
    pairs = orders_all // ORD_DEV
    scales = (1.0 / math.sqrt(2.0 * orders_all), 1.0 / math.sqrt(1.0 * nlon))
    harm = harmonics.reshape(maps, ORD_DEV, 2, tiles, LANES).transpose(0, 1, 3, 2, 4)
    harm = harm.reshape(-1, LANES)
    columns = forward(order_ids, beam_window, harm, legendre, maps)
    columns = columns.reshape(pairs, lats // pairs, -1)
    got = lax.all_to_all(columns, "order", split_axis=0, concat_axis=0, tiled=True)
    table = make_table(order_ids, nlon)
    terms = pixels(got.reshape(lats, -1), table, noise_weight[0], groups, scales)
    terms = terms.reshape(groups * pairs, -1, LANES)
    back = lax.all_to_all(terms, ("freq", "order"), split_axis=0, concat_axis=0, tiled=True)
    out = backward(order_ids, beam_window, back.reshape(-1, LANES), legendre, own)
    out = out.reshape(own, ORD_DEV, tiles, 2, LANES).transpose(0, 1, 3, 2, 4)
    return out.reshape(own, ORD_DEV, 2, degrees)


def solution(mesh):
    return jax.shard_map(
        on_device,
        mesh=mesh,
        in_specs=(
            P(None, "order", None, None),
            P("order", None, None),
            P(),
            P(),
            P("freq", "order", None),
        ),
        out_specs=P("freq", "order", None, None),
        check_vma=False,
    )
```

time: 133 us -> 66.9 us (0.50)
  waiting for transfers between devices: 39.9 us -> 2.27 us
  Pallas kernels: 0 us -> 23.5 us
  other arithmetic: 21.5 us -> 1.16 us
  matrix products: 17.3 us -> 0 us
  between operations: 13.5 us -> 0.08 us
  local copies, waits for them, and re-layouts: 6.13 us -> 2.51 us
  blocking collectives: 20.3 us -> 23.6 us
    reduce_scatter x1 -> x0, waiting for transfers between devices: 39.9 us -> none  [on_device(): return lax.psum_scatter(projected, 'freq', scatter_dimension=0, tiled=True)]
    pallas_call x0 -> x4, Pallas kernels: none -> 23.5 us  [the longest x1 6.72 us: backward(): pl.pallas_call(lambda *refs: backward_kernel(parts, *refs), name='backwar...]
    another operation x1 -> x2, other arithmetic: 19.1 us -> 0.68 us  [pair(): return jnp.stack([factor * jnp.cos(angle), factor * jnp.sin(angle)])]
    dot_general x3 -> x0, matrix products: 17.3 us -> none  [the longest x1 7.42 us: on_device(): jnp.einsum('bocr,olr->bocl', returned, legendre, preferred_element_type=j...]
    all_to_all x1, blocking collectives: 20.3 us -> 23.6 us  [on_device(): lax.all_to_all(terms, ('freq', 'order'), split_axis=0, concat_axis=0, til...]
    convert_element_type x1 -> x0, other arithmetic: 2.31 us -> none  [on_device(): (harmonics.astype(jnp.float32) * own_shaping).astype(jnp.bfloat16)]
    all_to_all x1, waiting for transfers between devices: 0.01 us -> 2.27 us  [on_device(): lax.all_to_all(columns, 'order', split_axis=0, concat_axis=0, tiled=True)]
    reduce_scatter x1 -> x0, local copies, waits for them, and re-layouts: 2.24 us -> none  [on_device(): return lax.psum_scatter(projected, 'freq', scatter_dimension=0, tiled=True)]
  transfers between devices with their start and end apart: 2 -> 1, of which waited for: 1 -> 1; matrix products, arithmetic and copies ran while one was open for 14% -> 5% of each run, Pallas kernels for 0% -> 7%
where the time goes in v2:
time: 66.9 us; the launch traced here: 66.7 us
  blocking collectives  23.6 us (35%)
  Pallas kernels  23.5 us (35%)
  starting transfers between devices  13.6 us (20%)
  local copies, waits for them, and re-layouts  2.51 us (4%)
  waiting for transfers between devices  2.27 us (3%)
  other arithmetic  1.16 us (2%)
    all_to_all x1, blocking collectives, on_device(): lax.all_to_all(terms, ('freq', 'order'), split_axis=0, concat_axis=0, til...  23.6 us
    all_to_all x1, starting transfers between devices, on_device(): lax.all_to_all(columns, 'order', split_axis=0, concat_axis=0, tiled=True)  13.6 us
    pallas_call x1, Pallas kernels, backward(): pl.pallas_call(lambda *refs: backward_kernel(parts, *refs), name='backwar...  6.72 us
    pallas_call x1, Pallas kernels, forward(): pl.pallas_call(lambda *refs: forward_kernel(parts, *refs), name='forward'...  6.35 us
    pallas_call x1, Pallas kernels, pixels(): pl.pallas_call(lambda *refs: pixel_kernel(groups, chunk, scales, *refs),...  5.91 us
    pallas_call x1, Pallas kernels, make_table(): pl.pallas_call(table_kernel, name='table', out_shape=jax.ShapeDtypeStruct...  4.55 us
    all_to_all x1, waiting for transfers between devices, on_device(): lax.all_to_all(columns, 'order', split_axis=0, concat_axis=0, tiled=True)  2.27 us
    another operation x2, local copies, waits for them, and re-layouts, pair(): return jnp.stack([factor * jnp.cos(angle), factor * jnp.sin(angle)])  1.57 us
  transfers between devices with their start and end apart: 1, of which 1 were waited for; matrix products, arithmetic and copies ran while one was open for 5% of the time, Pallas kernels for 7%

profile of v2, /device:TPU:1, one launch (start us, length us, event | category | flops | bytes accessed | tf_op | source)
XLA Modules:
  0.0 66.7 jit_solution(14410135533065718832)
XLA Ops:
  0.0 0.0 copy-start.1
  0.0 6.3 %forward.1 = bf16[512,128]{1,0:T(8,128)(2,1)} custom-call(s32[128]{0:T(128)} %refs_0_.3, f32[4,4096]{1,0:T(4,128)} %refs_1_.3, bf16[4096,128]{1,0:T(8,128)(2,1)} %bitcast.16, bf16[2,4096,512]{2,1,0:T(8,128)(2,1)} %refs_3_.3), custom_call_target="tpu_custom_call" | custom-call | tf_op jit(solution)/shard_map/forward/pallas_call | solution.py:72
  6.4 13.6 %all-to-all-start = ((bf16[64,8,128]{2,1,0:T(8,128)(2,1)}), bf16[64,8,128]{2,1,0:T(8,128)(2,1)S(1)}, u32[]{:S(2)}, u32[]{:S(2)}) async-start(bf16[64,8,128]{2,1,0:T(8,128)(2,1)} %bitcast.17), calls=%async_computation | async-start | bytes 262144 | tf_op jit(solution)/shard_map/all_to_all | solution.py:305
  20.0 0.0 copy-done.1
  20.0 0.1 reshape.503
  20.1 0.1 copy.13
  20.2 0.1 reshape.504
  20.3 0.1 fusion.15
  20.4 0.8 %copy.14.coarse_ref = f32[2,128,8]{2,1,0:T(8,128)} copy(f32[2,128,8]{1,2,0:T(8,128)S(1)} %get-tuple-element.13) | data formatting | bytes 16384 | tf_op jit(solution)/shard_map/stack | solution.py:122
  21.2 0.8 %copy.15.mid_ref = f32[2,128,8]{2,1,0:T(8,128)} copy(f32[2,128,8]{1,2,0:T(8,128)S(1)} %get-tuple-element.14) | data formatting | bytes 16384 | tf_op jit(solution)/shard_map/stack | solution.py:122
  22.0 0.3 fusion.7
  22.3 0.7 %pad_maximum_fusion.fine_ref = f32[2,128,128]{2,1,0:T(8,128)} fusion(f32[1,128,128]{2,1,0:T(8,128)S(1)} %get-tuple-element.10, f32[1,128,128]{2,1,0:T(8,128)S(1)} %get-tuple-element.9), kind=kLoop, calls=%fused_computation | loop fusion | flops 32768 | bytes 262144 | tf_op jit(solution)/shard_map/stack | solution.py:122
  23.0 4.6 %table.1.refs_1_ = bf16[256,8192]{1,0:T(8,128)(2,1)} custom-call(f32[2,128,8]{2,1,0:T(8,128)} %copy.14.coarse_ref, f32[2,128,8]{2,1,0:T(8,128)} %copy.15.mid_ref, f32[2,128,128]{2,1,0:T(8,128)} %pad_maximum_fusion.fine_ref), custom_call_target="tpu_custom_call" | custom-call | tf_op jit(solution)/shard_map/table/pallas_call | solution.py:129
  27.6 2.3 %all-to-all-done = bf16[64,8,128]{2,1,0:T(8,128)(2,1)S(1)} async-done(((bf16[64,8,128]{2,1,0:T(8,128)(2,1)}), bf16[64,8,128]{2,1,0:T(8,128)(2,1)S(1)}, u32[]{:S(2)}, u32[]{:S(2)}) %all-to-all-start) | async-done | bytes 131104 | tf_op jit(solution)/shard_map/all_to_all | solution.py:305
  29.9 0.0 copy-start
  29.9 0.7 copy-done
  30.5 5.9 %pixels.1 = bf16[512,128]{1,0:T(8,128)(2,1)} custom-call(bf16[512,128]{1,0:T(8,128)(2,1)} %bitcast.19, bf16[256,8192]{1,0:T(8,128)(2,1)} %table.1.refs_1_, f32[8,8192]{1,0:T(8,128)} %bitcast.21), custom_call_target="tpu_custom_call" | custom-call | tf_op jit(solution)/shard_map/pixels/pallas_call | solution.py:194
  36.4 23.6 %all_to_all.10 = bf16[256,2,128]{2,1,0:T(2,128)(2,1)} all-to-all(bf16[256,2,128]{2,1,0:T(2,128)(2,1)} %bitcast.20), channel_id=1, replica_groups=mesh['freq'=4,'order'=64] {'freq','order'}, dimensions={0} | all-to-all | bytes 262144 | tf_op jit(solution)/shard_map/all_to_all | solution.py:309
  60.0 6.7 %backward.1 = f32[1024,128]{1,0:T(8,128)} custom-call(s32[128]{0:T(128)} %refs_0_.3, f32[4,4096]{1,0:T(4,128)} %refs_1_.3, bf16[512,128]{1,0:T(8,128)(2,1)} %bitcast.18, bf16[2,4096,512]{2,1,0:T(8,128)(2,1)} %refs_3_.3), custom_call_target="tpu_custom_call" | custom-call | tf_op jit(solution)/shard_map/backward/pallas_call | solution.py:272
  (4 shorter events, 0.0 us)
Async XLA Ops:
  0.0 20.0 %copy-start.1 = (s32[128]{0:T(128)S(1)}, s32[128]{0:T(128)}, u32[]{:S(2)}) copy-start(s32[128]{0:T(128)} %refs_0_.3) | copy-start | bytes 1540
  6.4 23.5 %all-to-all-start = ((bf16[64,8,128]{2,1,0:T(8,128)(2,1)}), bf16[64,8,128]{2,1,0:T(8,128)(2,1)S(1)}, u32[]{:S(2)}, u32[]{:S(2)}) async-start(bf16[64,8,128]{2,1,0:T(8,128)(2,1)} %bitcast.17), calls=%async_computation | async-start | bytes 262144 | tf_op jit(solution)/shard_map/all_to_all | solution.py:305
  29.9 0.7 copy-start

commit v3 on v2

v3 whole, which is shorter than its diff:
```python
import math

import jax
import jax.numpy as jnp
from jax import lax
from jax.experimental import pallas as pl
from jax.experimental.pallas import tpu as pltpu
from jax.sharding import PartitionSpec as P

ORD_DEV = 2
LANES = 128
F32 = jnp.float32
BF16 = jnp.bfloat16


def limits(mib):
    return pltpu.CompilerParams(vmem_limit_bytes=mib << 20)


def on_chip(value):
    return pltpu.with_memory_space_constraint(value, pltpu.VMEM)


def off_chip(value):
    return pltpu.with_memory_space_constraint(value, pltpu.HBM)


def lane_ids(shape):
    return lax.broadcasted_iota(jnp.int32, shape, len(shape) - 1)


def swap_halves(a, b):
    low = lane_ids(a.shape) < LANES // 2
    first = jnp.where(low, a, pltpu.roll(b, LANES // 2, a.ndim - 1))
    second = jnp.where(low, pltpu.roll(a, LANES // 2, a.ndim - 1), b)
    return first, second


def forward_kernel(
    parts, ids_hbm, beam_ref, harm_ref, leg_ref, out_ref, leg_v, beam_v, harm_v, wide, lhs, ids_ref, sems
):
    degrees, lats = leg_ref.shape[1], leg_ref.shape[2]
    maps = harm_ref.shape[0]
    tiles = degrees // LANES
    step = lats // parts
    slot = lax.axis_index("order") * ORD_DEV
    group = lax.axis_index("freq")
    beam_copy = pltpu.make_async_copy(beam_ref, beam_v, sems.at[ORD_DEV * (parts + 1)])
    beam_copy.start()
    ids_copy = pltpu.make_async_copy(ids_hbm, ids_ref, sems.at[ORD_DEV * (parts + 1) + 1])
    ids_copy.start()
    harm_copies, leg_copies = [], []
    for o in range(ORD_DEV):
        base = o * (parts + 1)
        copy = pltpu.make_async_copy(harm_ref.at[:, o], harm_v.at[:, o], sems.at[base])
        copy.start()
        harm_copies.append(copy)
        for p in range(parts):
            cols = pl.ds(p * step, step)
            copy = pltpu.make_async_copy(
                leg_ref.at[o, :, cols], leg_v.at[o, :, cols], sems.at[base + 1 + p]
            )
            copy.start()
            leg_copies.append(copy)
    ids_copy.wait()
    beam_copy.wait()
    beam = beam_v[pl.ds(group, 1), :]
    degree = lane_ids((1, degrees))

    def prepare(o):
        harm_copies[o].wait()
        rows = 2 * tiles
        for b in range(maps):
            wide[o, pl.ds(b * rows, rows), :] = harm_v[b, o].astype(F32)
        shaping = jnp.where(degree >= ids_ref[slot + o], beam, 0.0)
        for t in range(tiles):
            cols = pl.ds(t * LANES, LANES)
            for c in range(2):
                values = wide[o, pl.ds(t * 2 + c, maps, stride=rows), :]
                lhs[o, pl.ds(c * maps, maps), cols] = (
                    values * shaping[:, t * LANES : (t + 1) * LANES]
                ).astype(BF16)

    prepare(0)
    for o in range(ORD_DEV):
        for p in range(parts):
            cols = pl.ds(p * step, step)
            leg_copies[o * parts + p].wait()
            sums = jnp.dot(lhs[o], leg_v[o, :, cols], preferred_element_type=F32)
            out_ref[cols, pl.ds(o * 2 * maps, 2 * maps)] = sums.T.astype(BF16)
            if o == 0 and p == 0:
                prepare(1)


def forward(order_ids, beam, harm, legendre, parts=2):
    degrees, lats = legendre.shape[1:]
    maps = harm.shape[0]
    return pl.pallas_call(
        lambda *refs: forward_kernel(parts, *refs),
        name="forward",
        out_shape=jax.ShapeDtypeStruct((lats, ORD_DEV * 2 * maps), BF16),
        in_specs=[pl.BlockSpec(memory_space=pl.ANY)] * 4,
        out_specs=pl.BlockSpec(memory_space=pltpu.VMEM),
        scratch_shapes=[
            pltpu.VMEM(legendre.shape, BF16),
            pltpu.VMEM(beam.shape, F32),
            pltpu.VMEM(harm.shape, BF16),
            pltpu.VMEM((ORD_DEV, maps * harm.shape[2], LANES), F32),
            pltpu.VMEM((ORD_DEV, 2 * maps, degrees), BF16),
            pltpu.SMEM(order_ids.shape, jnp.int32),
            pltpu.SemaphoreType.DMA((ORD_DEV * (parts + 1) + 2,)),
        ],
        compiler_params=limits(24),
    )(off_chip(order_ids), off_chip(beam), off_chip(harm), off_chip(legendre))


def table_kernel(nlon, ids_ref, out_ref, sign_ref, slots, small, fine):
    rows = ids_ref.shape[1]
    half = rows // ORD_DEV
    mids = 8
    span = mids * LANES
    coarses = out_ref.shape[1] // span
    unit = 2.0 * math.pi / nlon
    slots[...] = jnp.broadcast_to(ids_ref[...].astype(F32), (rows, rows)).T
    lane = lane_ids((half, LANES))
    steps = jnp.where(lane < LANES // 2, lane * LANES, (lane - LANES // 2) * span)
    for o in range(ORD_DEV):
        wide_ids = slots[pl.ds(o, half, stride=ORD_DEV), :]
        ids = wide_ids.astype(jnp.int32)
        factor = jnp.where((ids == 0) | (lane < LANES // 2), 1.0, 2.0)
        angle = ((ids * steps) & (nlon - 1)).astype(F32) * unit
        part = pl.ds(o * half, half)
        small[0, part, :] = factor * jnp.cos(angle)
        small[1, part, :] = factor * jnp.sin(angle)
        angle = ((ids * lane) & (nlon - 1)).astype(F32) * unit
        fine[0, part, :] = jnp.cos(angle)
        fine[1, part, :] = jnp.sin(angle)
        across = jnp.concatenate([wide_ids, wide_ids], 0).T[0:8]
        odd = across.astype(jnp.int32) & 1
        sign_ref[pl.ds(o * 8, 8), :] = (1 - 2 * odd).astype(F32)
    block = 16
    for r in range(0, rows, block):
        part = pl.ds(r, block)
        sc, ss = small[0, part, :], small[1, part, :]
        fc, fs = fine[0, part, :], fine[1, part, :]
        cos, sin = [], []
        for q in range(mids):
            mc, ms = sc[:, q : q + 1], ss[:, q : q + 1]
            cos.append(mc * fc - ms * fs)
            sin.append(ms * fc + mc * fs)
        at = (r // half) * rows + r % half
        for p in range(coarses):
            lead = LANES // 2 + p
            cc, cs = sc[:, lead : lead + 1], ss[:, lead : lead + 1]
            for q in range(mids):
                cols = pl.ds(p * span + q * LANES, LANES)
                out_ref[pl.ds(at, block), cols] = (cc * cos[q] - cs * sin[q]).astype(BF16)
                out_ref[pl.ds(at + half, block), cols] = (-(cs * cos[q] + cc * sin[q])).astype(BF16)


def make_table(order_ids, nlon):
    rows = order_ids.shape[0]
    return pl.pallas_call(
        lambda *refs: table_kernel(nlon, *refs),
        name="table",
        out_shape=(pltpu.VMEM((2 * rows, nlon // 2), BF16), pltpu.VMEM((8 * ORD_DEV, LANES), F32)),
        in_specs=[pl.BlockSpec(memory_space=pltpu.VMEM)],
        out_specs=(pl.BlockSpec(memory_space=pltpu.VMEM),) * 2,
        scratch_shapes=[
            pltpu.VMEM((rows, rows), F32),
            pltpu.VMEM((2, rows, LANES), F32),
            pltpu.VMEM((2, rows, LANES), F32),
        ],
        compiler_params=limits(8),
    )(order_ids.reshape(1, -1))


def pixel_kernel(
    groups, chunk, scales, got_ref, table_ref, sign_ref, weight_ref, leg_ref, out_ref, leg_v, wide, lhs, mixed, sem
):
    leg_copy = pltpu.make_async_copy(leg_ref, leg_v, sem)
    leg_copy.start()
    fwd_scale, back_scale = scales
    rows = weight_ref.shape[0]
    pairs = got_ref.shape[0] // rows
    maps = got_ref.shape[1] // (2 * ORD_DEV)
    size = rows * maps
    half = table_ref.shape[1]
    wide[...] = got_ref[...].astype(F32)
    signs = [sign_ref[pl.ds(o * 8, 1), :] for o in range(ORD_DEV)]
    for r in range(0, rows, 2):
        stacked = jnp.concatenate(
            [wide[pl.ds(r + i, pairs, stride=rows), :] for i in range(2)], 0
        )
        turned = stacked.T
        for o in range(ORD_DEV):
            cos = turned[(2 * o) * maps : (2 * o + 1) * maps]
            sin = turned[(2 * o + 1) * maps : (2 * o + 2) * maps]
            for i, part in enumerate(swap_halves(cos, sin)):
                cols = pl.ds(o * LANES, LANES)
                lhs[pl.ds((r + i) * maps, maps), cols] = part.astype(BF16)
                lhs[pl.ds(size + (r + i) * maps, maps), cols] = (part * signs[o]).astype(BF16)
    total = jnp.zeros((2 * size, 2 * LANES), F32)
    for j in range(half // chunk):
        cols = pl.ds(j * chunk, chunk)
        part = table_ref[:, cols]
        field = jnp.dot(lhs[...], part, preferred_element_type=F32)
        pieces = []
        for h in range(2):
            weight = weight_ref[:, pl.ds(h * half + j * chunk, chunk)] * fwd_scale
            for r in range(rows):
                at = h * size + r * maps
                pieces.append((field[at : at + maps] * weight[r : r + 1]).astype(BF16))
        total += lax.dot_general(
            jnp.concatenate(pieces, 0), part, (((1,), (1,)), ((), ())), preferred_element_type=F32
        )
    sign = jnp.concatenate(signs, 1)
    total = (total[:size] + total[size:] * sign) * back_scale
    own = maps // groups
    low_rows = rows // 2
    for f in range(groups):
        pieces = []
        for low in range(low_rows):
            for o in range(ORD_DEV):
                at = [(high * low_rows + low) * maps + f * own for high in range(2)]
                pieces += list(
                    swap_halves(
                        *[total[a : a + own, o * LANES : (o + 1) * LANES] for a in at]
                    )
                )
        turned = jnp.concatenate(pieces, 0).T
        for high in range(2):
            mixed[pl.ds(f * 2 * pairs + high, pairs, stride=2), :] = turned[
                high * pairs : (high + 1) * pairs
            ]
    out_ref[...] = mixed[...].astype(BF16)
    leg_copy.wait()


def pixels(got, table, signs, weight, legendre, groups, scales, chunk=512):
    return pl.pallas_call(
        lambda *refs: pixel_kernel(groups, chunk, scales, *refs),
        name="pixels",
        out_shape=(pltpu.VMEM(got.shape, BF16), pltpu.VMEM(legendre.shape, BF16)),
        in_specs=[pl.BlockSpec(memory_space=pltpu.VMEM)] * 4 + [pl.BlockSpec(memory_space=pl.ANY)],
        out_specs=(pl.BlockSpec(memory_space=pltpu.VMEM),) * 2,
        scratch_shapes=[
            pltpu.VMEM(got.shape, F32),
            pltpu.VMEM((got.shape[0], 2 * LANES), BF16),
            pltpu.VMEM(got.shape, F32),
            pltpu.SemaphoreType.DMA,
        ],
        compiler_params=limits(8),
    )(on_chip(got), table, signs, on_chip(weight), off_chip(legendre))


def backward_kernel(parts, ids_ref, beam_ref, got_ref, leg_ref, out_ref, mixed):
    degrees, lats = leg_ref.shape[1], leg_ref.shape[2]
    groups = beam_ref.shape[0]
    tiles = degrees // LANES
    step = degrees // parts
    slot = lax.axis_index("order") * ORD_DEV
    span = got_ref.shape[0] // groups
    width = LANES // groups
    lows = lats // span
    own = width // (2 * ORD_DEV)
    blocks = [got_ref[pl.ds(f * span, span), :].astype(F32) for f in range(groups)]
    lane_group = lane_ids((span, LANES)) // width
    turned = [
        [v if k == 0 else pltpu.roll(v, k * width, 1) for k in range(groups)] for v in blocks
    ]
    for low in range(lows):
        merged = turned[0][(0 - low) % groups]
        for f in range(1, groups):
            merged = jnp.where(lane_group == f, turned[f][(f - low) % groups], merged)
        mixed[pl.ds(low, span, stride=lows), :] = merged
    rows = mixed[...].T.astype(BF16)
    degree = lane_ids((1, degrees))
    for o in range(ORD_DEV):
        lhs = jnp.concatenate(
            [
                rows[f * width + o * 2 * own : f * width + (o + 1) * 2 * own]
                for f in range(groups)
            ],
            0,
        )
        for p in range(parts):
            cols = slice(p * step, (p + 1) * step)
            terms = lax.dot_general(
                lhs,
                leg_ref[o, pl.ds(p * step, step), :],
                (((1,), (1,)), ((), ())),
                preferred_element_type=F32,
            )
            live = degree[:, cols] >= ids_ref[slot + o]
            total = jnp.zeros((2 * own, step), F32)
            for f in range(groups):
                shaping = jnp.where(live, beam_ref[f : f + 1, cols], 0.0)
                total += terms[f * 2 * own : (f + 1) * 2 * own] * shaping
            for t in range(tiles // parts):
                for c in range(2):
                    at = o * tiles * 2 + (p * tiles // parts + t) * 2 + c
                    out_ref[pl.ds(at, own, stride=ORD_DEV * tiles * 2), :] = total[
                        c * own : (c + 1) * own, t * LANES : (t + 1) * LANES
                    ]


def backward(order_ids, beam, got, legendre, own, parts=4):
    degrees = legendre.shape[1]
    return pl.pallas_call(
        lambda *refs: backward_kernel(parts, *refs),
        name="backward",
        out_shape=jax.ShapeDtypeStruct((own * ORD_DEV * 2 * degrees // LANES, LANES), F32),
        in_specs=[
            pl.BlockSpec(memory_space=pltpu.SMEM),
            pl.BlockSpec(memory_space=pltpu.VMEM),
            pl.BlockSpec(memory_space=pltpu.VMEM),
            pl.BlockSpec(memory_space=pltpu.VMEM),
        ],
        out_specs=pl.BlockSpec(memory_space=pltpu.VMEM),
        scratch_shapes=[
            pltpu.VMEM((legendre.shape[2], LANES), F32),
        ],
        compiler_params=limits(8),
    )(order_ids, on_chip(beam), on_chip(got), legendre)


def on_device(harmonics, legendre, beam_window, order_ids, noise_weight):
    maps, _, _, degrees = harmonics.shape
    lats = legendre.shape[2]
    nlon = noise_weight.shape[2]
    orders_all = order_ids.shape[0]
    groups = beam_window.shape[0]
    tiles = degrees // LANES
    own = maps // groups
    pairs = orders_all // ORD_DEV
    scales = (1.0 / math.sqrt(2.0 * orders_all), 1.0 / math.sqrt(1.0 * nlon))
    harm = harmonics.reshape(maps, ORD_DEV, 2, tiles, LANES).transpose(0, 1, 3, 2, 4)
    harm = harm.reshape(maps, ORD_DEV, -1, LANES)
    columns = forward(order_ids, beam_window, harm, legendre)
    columns = columns.reshape(pairs, lats // pairs, -1)
    got = lax.all_to_all(columns, "order", split_axis=0, concat_axis=0, tiled=True)
    table, signs = make_table(order_ids, nlon)
    terms, legendre = pixels(
        got.reshape(lats, -1), table, signs, noise_weight[0], legendre, groups, scales
    )
    terms = terms.reshape(groups * pairs, -1, LANES)
    back = lax.all_to_all(terms, ("freq", "order"), split_axis=0, concat_axis=0, tiled=True)
    out = backward(order_ids, beam_window, back.reshape(-1, LANES), legendre, own)
    out = out.reshape(own, ORD_DEV, tiles, 2, LANES).transpose(0, 1, 3, 2, 4)
    return out.reshape(own, ORD_DEV, 2, degrees)


def solution(mesh):
    return jax.shard_map(
        on_device,
        mesh=mesh,
        in_specs=(
            P(None, "order", None, None),
            P("order", None, None),
            P(),
            P(),
            P("freq", "order", None),
        ),
        out_specs=P("freq", "order", None, None),
        check_vma=False,
    )
```

time: 66.9 us -> 58.5 us (0.87)
  Pallas kernels: 23.5 us -> 15.8 us
  waiting for transfers between devices: 2.27 us -> 8.41 us
  blocking collectives: 23.6 us -> 20.4 us
  local copies, waits for them, and re-layouts: 2.51 us -> 0.01 us
  other arithmetic: 1.16 us -> 0 us
    all_to_all x1, waiting for transfers between devices: 2.27 us -> 8.41 us  [on_device(): lax.all_to_all(columns, 'order', split_axis=0, concat_axis=0, tiled=True)]
    all_to_all x1, blocking collectives: 23.6 us -> 20.4 us  [on_device(): lax.all_to_all(terms, ('freq', 'order'), split_axis=0, concat_axis=0, til...]
    pallas_call x1, Pallas kernels: 4.55 us -> 1.46 us  [make_table(): pl.pallas_call(lambda *refs: table_kernel(nlon, *refs), name='table', out...]
    pallas_call x1, Pallas kernels: 5.91 us -> 3.39 us  [pixels(): pl.pallas_call(lambda *refs: pixel_kernel(groups, chunk, scales, *refs),...]
    pallas_call x1, Pallas kernels: 6.72 us -> 4.24 us  [backward(): pl.pallas_call(lambda *refs: backward_kernel(parts, *refs), name='backwar...]
    another operation x2 -> x0, local copies, waits for them, and re-layouts: 1.57 us -> none  [pair(): return jnp.stack([factor * jnp.cos(angle), factor * jnp.sin(angle)])]
    another operation x2 -> x0, other arithmetic: 0.68 us -> none  [pair(): return jnp.stack([factor * jnp.cos(angle), factor * jnp.sin(angle)])]
  transfers between devices with their start and end apart: 1 -> 1, of which waited for: 1 -> 1; matrix products, arithmetic and copies ran while one was open for 5% -> 0% of each run, Pallas kernels for 7% -> 3%
where the time goes in v3:
time: 58.5 us; the launch traced here: 58.3 us
  blocking collectives  20.4 us (35%)
  Pallas kernels  15.8 us (27%)
  starting transfers between devices  13.6 us (23%)
  waiting for transfers between devices  8.41 us (14%)
    all_to_all x1, blocking collectives, on_device(): lax.all_to_all(terms, ('freq', 'order'), split_axis=0, concat_axis=0, til...  20.4 us
    all_to_all x1, starting transfers between devices, on_device(): lax.all_to_all(columns, 'order', split_axis=0, concat_axis=0, tiled=True)  13.6 us
    all_to_all x1, waiting for transfers between devices, on_device(): lax.all_to_all(columns, 'order', split_axis=0, concat_axis=0, tiled=True)  8.41 us
    pallas_call x1, Pallas kernels, forward(): pl.pallas_call(lambda *refs: forward_kernel(parts, *refs), name='forward'...  6.69 us
    pallas_call x1, Pallas kernels, backward(): pl.pallas_call(lambda *refs: backward_kernel(parts, *refs), name='backwar...  4.24 us
    pallas_call x1, Pallas kernels, pixels(): pl.pallas_call(lambda *refs: pixel_kernel(groups, chunk, scales, *refs),...  3.39 us
    pallas_call x1, Pallas kernels, make_table(): pl.pallas_call(lambda *refs: table_kernel(nlon, *refs), name='table', out...  1.46 us
  transfers between devices with their start and end apart: 1, of which 1 were waited for; matrix products, arithmetic and copies ran while one was open for 0% of the time, Pallas kernels for 3%

profile of v3, /device:TPU:1, one launch (start us, length us, event | category | flops | bytes accessed | tf_op | source)
XLA Modules:
  0.0 58.3 jit_solution(3228516351859945310)
XLA Ops:
  0.0 0.0 copy-start.2
  0.0 0.0 copy-start.1
  0.0 0.0 copy-start
  0.0 6.7 %forward.1 = bf16[512,128]{1,0:T(8,128)(2,1)} custom-call(s32[128]{0:T(128)} %refs_0_.3, f32[4,4096]{1,0:T(4,128)} %refs_1_.3, bf16[32,2,64,128]{3,2,1,0:T(8,128)(2,1)} %bitcast.21, bf16[2,4096,512]{2,1,0:T(8,128)(2,1)} %refs_4_.1), custom_call_target="tpu_custom_call" | custom-call | tf_op jit(solution)/shard_map/forward/pallas_call | solution.py:98
  6.7 13.6 %all-to-all-start = ((bf16[64,8,128]{2,1,0:T(8,128)(2,1)}), bf16[64,8,128]{2,1,0:T(8,128)(2,1)S(1)}, u32[]{:S(2)}, u32[]{:S(2)}) async-start(bf16[64,8,128]{2,1,0:T(8,128)(2,1)} %bitcast.3), calls=%async_computation | async-start | bytes 262144 | tf_op jit(solution)/shard_map/all_to_all | solution.py:342
  20.3 0.0 copy-done.2
  20.3 1.5 %table.1 = (bf16[256,4096]{1,0:T(8,128)(2,1)S(1)}, f32[16,128]{1,0:T(8,128)S(1)}) custom-call(s32[1,128]{1,0:T(1,128)S(1)} %bitcast.20), custom_call_target="tpu_custom_call" | custom-call | tf_op jit(solution)/shard_map/table/pallas_call | solution.py:163
  21.8 8.4 %all-to-all-done = bf16[64,8,128]{2,1,0:T(8,128)(2,1)S(1)} async-done(((bf16[64,8,128]{2,1,0:T(8,128)(2,1)}), bf16[64,8,128]{2,1,0:T(8,128)(2,1)S(1)}, u32[]{:S(2)}, u32[]{:S(2)}) %all-to-all-start) | async-done | bytes 131104 | tf_op jit(solution)/shard_map/all_to_all | solution.py:342
  30.2 0.0 copy-done.1
  30.2 3.4 %pixels.1 = (bf16[512,128]{1,0:T(8,128)(2,1)S(1)}, bf16[2,4096,512]{2,1,0:T(8,128)(2,1)S(1)}) custom-call(bf16[512,128]{1,0:T(8,128)(2,1)S(1)} %bitcast.16, bf16[256,4096]{1,0:T(8,128)(2,1)S(1)} %get-tuple-element.9.refs_1_, f32[16,128]{1,0:T(8,128)S(1)} %get-tuple-element.10.refs_2_, f32[8,8192]{1,0:T(8,128)S(1)} %bitcast.18, bf16[2,4096,512]{2,1,0:T(8,128)(2,1)} %refs_4_.1), custom_call_target="tpu_custom_call" | custom-call | tf_op jit(solution)/shard_map/pixels/pallas_call | solution.py:241
  33.6 20.4 %all_to_all.10 = bf16[256,2,128]{2,1,0:T(2,128)(2,1)S(1)} all-to-all(bf16[256,2,128]{2,1,0:T(2,128)(2,1)S(1)} %bitcast.19), channel_id=1, replica_groups=mesh['freq'=4,'order'=64] {'freq','order'}, dimensions={0} | all-to-all | bytes 262144 | tf_op jit(solution)/shard_map/all_to_all | solution.py:348
  54.0 0.0 copy-done
  54.0 4.2 %backward.1 = f32[1024,128]{1,0:T(8,128)} custom-call(s32[128]{0:T(128)S(1)} %copy-done.2, f32[4,4096]{1,0:T(4,128)S(1)} %copy-done, bf16[512,128]{1,0:T(8,128)(2,1)S(1)} %bitcast.17, bf16[2,4096,512]{2,1,0:T(8,128)(2,1)S(1)} %get-tuple-element.12.refs_3_), custom_call_target="tpu_custom_call" | custom-call | tf_op jit(solution)/shard_map/backward/pallas_call | solution.py:310
Async XLA Ops:
  0.0 20.3 %copy-start.2 = (s32[128]{0:T(128)S(1)}, s32[128]{0:T(128)}, u32[]{:S(2)}) copy-start(s32[128]{0:T(128)} %refs_0_.3) | copy-start | bytes 1540
  0.0 30.2 %copy-start.1 = (f32[1,8,8192]{2,1,0:T(8,128)S(1)}, f32[1,8,8192]{2,1,0:T(8,128)}, u32[]{:S(2)}) copy-start(f32[1,8,8192]{2,1,0:T(8,128)} %param.9) | copy-start | bytes 786436
  0.0 54.0 %copy-start = (f32[4,4096]{1,0:T(4,128)S(1)}, f32[4,4096]{1,0:T(4,128)}, u32[]{:S(2)}) copy-start(f32[4,4096]{1,0:T(4,128)} %refs_1_.3) | copy-start | bytes 196612
  6.7 23.5 %all-to-all-start = ((bf16[64,8,128]{2,1,0:T(8,128)(2,1)}), bf16[64,8,128]{2,1,0:T(8,128)(2,1)S(1)}, u32[]{:S(2)}, u32[]{:S(2)}) async-start(bf16[64,8,128]{2,1,0:T(8,128)(2,1)} %bitcast.3), calls=%async_computation | async-start | bytes 262144 | tf_op jit(solution)/shard_map/all_to_all | solution.py:342

commit v4 on v3

v4 whole, which is shorter than its diff:
```python
import math

import jax
import jax.numpy as jnp
from jax import lax
from jax.experimental import pallas as pl
from jax.experimental.pallas import tpu as pltpu
from jax.sharding import PartitionSpec as P

ORD_DEV = 2
LANES = 128
F32 = jnp.float32
BF16 = jnp.bfloat16


def limits(mib):
    return pltpu.CompilerParams(vmem_limit_bytes=mib << 20)


def on_chip(value):
    return pltpu.with_memory_space_constraint(value, pltpu.VMEM)


def off_chip(value):
    return pltpu.with_memory_space_constraint(value, pltpu.HBM)


def lane_ids(shape):
    return lax.broadcasted_iota(jnp.int32, shape, len(shape) - 1)


def swap_halves(a, b):
    low = lane_ids(a.shape) < LANES // 2
    first = jnp.where(low, a, pltpu.roll(b, LANES // 2, a.ndim - 1))
    second = jnp.where(low, pltpu.roll(a, LANES // 2, a.ndim - 1), b)
    return first, second


def table_angles(nlon, ids_row, sign_ref, slots, small, fine, mids):
    rows = ids_row.shape[1]
    half = rows // ORD_DEV
    unit = 2.0 * math.pi / nlon
    slots[...] = jnp.broadcast_to(ids_row.astype(F32), (rows, rows)).T
    lane = lane_ids((half, LANES))
    steps = jnp.where(lane < LANES // 2, lane * LANES, (lane - LANES // 2) * (mids * LANES))
    for o in range(ORD_DEV):
        wide_ids = slots[pl.ds(o, half, stride=ORD_DEV), :]
        ids = wide_ids.astype(jnp.int32)
        factor = jnp.where((ids == 0) | (lane < LANES // 2), 1.0, 2.0)
        angle = ((ids * steps) & (nlon - 1)).astype(F32) * unit
        part = pl.ds(o * half, half)
        small[0, part, :] = factor * jnp.cos(angle)
        small[1, part, :] = factor * jnp.sin(angle)
        angle = ((ids * lane) & (nlon - 1)).astype(F32) * unit
        fine[0, part, :] = jnp.cos(angle)
        fine[1, part, :] = jnp.sin(angle)
        across = jnp.concatenate([wide_ids, wide_ids], 0).T[0:8]
        odd = across.astype(jnp.int32) & 1
        sign_ref[pl.ds(o * 8, 8), :] = (1 - 2 * odd).astype(F32)


def table_rows(out_ref, small, fine, mids, blocks):
    rows = small.shape[1]
    half = rows // ORD_DEV
    span = mids * LANES
    coarses = out_ref.shape[1] // span
    block = 16
    shape = (block, LANES)
    for r in blocks:
        part = pl.ds(r, block)
        sc, ss = small[0, part, :], small[1, part, :]
        fc, fs = fine[0, part, :], fine[1, part, :]
        at = (r // half) * rows + r % half
        lead = []
        for p in range(coarses):
            k = LANES // 2 + p
            cs = jnp.broadcast_to(ss[:, k : k + 1], shape)
            lead.append((jnp.broadcast_to(sc[:, k : k + 1], shape), cs))
        for q in range(mids):
            mc = jnp.broadcast_to(sc[:, q : q + 1], shape)
            ms = jnp.broadcast_to(ss[:, q : q + 1], shape)
            cos = mc * fc - ms * fs
            sin = ms * fc + mc * fs
            for p in range(coarses):
                cc, cs = lead[p]
                cols = pl.ds(p * span + q * LANES, LANES)
                out_ref[pl.ds(at, block), cols] = (cc * cos - cs * sin).astype(BF16)
                out_ref[pl.ds(at + half, block), cols] = (-(cs * cos) - cc * sin).astype(BF16)


def live_steps(ids_ref, slot, tiles):
    first = [ids_ref[slot + o] // LANES for o in range(ORD_DEV)]
    count = tiles - first[0]
    steps = []
    for i in range(tiles + 1):
        later = i >= count
        order = jnp.where(later, 1, 0)
        steps.append((order, jnp.where(later, first[1] + i - count, first[0] + i)))
    return steps


def forward_kernel(
    nlon,
    cuts,
    ids_hbm,
    ids_row_hbm,
    beam_ref,
    harm_ref,
    leg_ref,
    out_ref,
    leg_v,
    table_ref,
    sign_ref,
    ids_row,
    beam_v,
    own_beam,
    harm_v,
    wide,
    lhs,
    slots,
    small,
    fine,
    ids_ref,
    sems,
    leg_sems,
):
    degrees = leg_ref.shape[1]
    maps = harm_ref.shape[0]
    tiles = degrees // LANES
    rows = 2 * tiles
    mids = 8
    slot = lax.axis_index("order") * ORD_DEV
    group = lax.axis_index("freq")
    copies = [
        pltpu.make_async_copy(ids_hbm, ids_ref, sems.at[0]),
        pltpu.make_async_copy(ids_row_hbm, ids_row, sems.at[1]),
        pltpu.make_async_copy(beam_ref, beam_v, sems.at[2]),
        pltpu.make_async_copy(harm_ref, harm_v, sems.at[3]),
    ]
    for copy in copies:
        copy.start()
    copies[0].wait()
    steps = live_steps(ids_ref, slot, tiles)
    leg_copies = []
    for i, (order, tile) in enumerate(steps):
        copy = pltpu.make_async_copy(
            leg_ref.at[order, pl.ds(pl.multiple_of(tile * LANES, LANES), LANES), :],
            leg_v.at[pl.ds(i * LANES, LANES), :],
            leg_sems.at[i],
        )
        copy.start()
        leg_copies.append(copy)
    copies[1].wait()
    table_angles(nlon, ids_row[...], sign_ref, slots, small, fine, mids)
    copies[2].wait()
    own_beam[...] = beam_v[pl.ds(group, 1), :]
    copies[3].wait()
    for b in range(maps):
        for o in range(ORD_DEV):
            wide[pl.ds((b * ORD_DEV + o) * rows, rows), :] = harm_v[b, o].astype(F32)
    lane = lane_ids((1, LANES))
    blank = jnp.zeros((2 * maps, LANES), BF16)
    for i, (order, tile) in enumerate(steps):
        start = pl.multiple_of(tile * LANES, LANES)
        live = lane + start >= ids_ref[slot + order]
        shaping = jnp.where(live, own_beam[:, pl.ds(start, LANES)], 0.0)
        at = pl.multiple_of(order * (2 * maps), 2 * maps)
        cols = pl.ds(i * LANES, LANES)
        lhs[pl.ds(2 * maps - at, 2 * maps), cols] = blank
        for c in range(2):
            values = wide[pl.ds(order * rows + tile * 2 + c, maps, stride=ORD_DEV * rows), :]
            lhs[pl.ds(at + c * maps, maps), cols] = (values * shaping).astype(BF16)
    table_rows(table_ref, small, fine, mids, range(0, small.shape[1], 16))
    total = None
    for lo, hi in zip(cuts[:-1], cuts[1:]):
        for copy in leg_copies[lo:hi]:
            copy.wait()
        span = pl.ds(lo * LANES, (hi - lo) * LANES)
        part = jnp.dot(lhs[:, span], leg_v[span, :], preferred_element_type=F32)
        total = part if total is None else total + part
    out_ref[...] = total.T.astype(BF16)


def forward(order_ids, beam, harm, legendre, nlon):
    degrees, lats = legendre.shape[1:]
    maps = harm.shape[0]
    orders = order_ids.shape[0]
    ids_row = order_ids.reshape(1, -1)
    steps = degrees // LANES + 1
    cuts = (0, steps)
    return pl.pallas_call(
        lambda *refs: forward_kernel(nlon, cuts, *refs),
        name="forward",
        out_shape=(
            pltpu.VMEM((lats, ORD_DEV * 2 * maps), BF16),
            pltpu.VMEM((steps * LANES, lats), BF16),
            pltpu.VMEM((2 * orders, nlon // 2), BF16),
            pltpu.VMEM((8 * ORD_DEV, LANES), F32),
        ),
        in_specs=[pl.BlockSpec(memory_space=pl.ANY)] * 5,
        out_specs=(pl.BlockSpec(memory_space=pltpu.VMEM),) * 4,
        scratch_shapes=[
            pltpu.VMEM(ids_row.shape, jnp.int32),
            pltpu.VMEM(beam.shape, F32),
            pltpu.VMEM((1, degrees), F32),
            pltpu.VMEM(harm.shape, BF16),
            pltpu.VMEM((maps * ORD_DEV * harm.shape[2], LANES), F32),
            pltpu.VMEM((ORD_DEV * 2 * maps, steps * LANES), BF16),
            pltpu.VMEM((orders, orders), F32),
            pltpu.VMEM((2, orders, LANES), F32),
            pltpu.VMEM((2, orders, LANES), F32),
            pltpu.SMEM(order_ids.shape, jnp.int32),
            pltpu.SemaphoreType.DMA((4,)),
            pltpu.SemaphoreType.DMA((steps,)),
        ],
        compiler_params=limits(16),
    )(*[off_chip(v) for v in (order_ids, ids_row, beam, harm, legendre)])


def pixel_kernel(
    groups, chunk, scales, got_ref, table_ref, sign_ref, weight_ref, out_ref, wide, lhs, mixed
):
    fwd_scale, back_scale = scales
    rows = weight_ref.shape[0]
    pairs = got_ref.shape[0] // rows
    maps = got_ref.shape[1] // (2 * ORD_DEV)
    size = rows * maps
    half = table_ref.shape[1]
    wide[...] = got_ref[...].astype(F32)
    signs = [sign_ref[pl.ds(o * 8, 1), :] for o in range(ORD_DEV)]
    for r in range(0, rows, 2):
        stacked = jnp.concatenate(
            [wide[pl.ds(r + i, pairs, stride=rows), :] for i in range(2)], 0
        )
        turned = stacked.T
        for o in range(ORD_DEV):
            cos = turned[(2 * o) * maps : (2 * o + 1) * maps]
            sin = turned[(2 * o + 1) * maps : (2 * o + 2) * maps]
            for i, part in enumerate(swap_halves(cos, sin)):
                cols = pl.ds(o * LANES, LANES)
                lhs[pl.ds((r + i) * maps, maps), cols] = part.astype(BF16)
                lhs[pl.ds(size + (r + i) * maps, maps), cols] = (part * signs[o]).astype(BF16)
    total = jnp.zeros((2 * size, 2 * LANES), F32)
    for j in range(half // chunk):
        cols = pl.ds(j * chunk, chunk)
        part = table_ref[:, cols]
        field = jnp.dot(lhs[...], part, preferred_element_type=F32)
        pieces = []
        for h in range(2):
            weight = weight_ref[:, pl.ds(h * half + j * chunk, chunk)] * fwd_scale
            for r in range(rows):
                at = h * size + r * maps
                pieces.append((field[at : at + maps] * weight[r : r + 1]).astype(BF16))
        total += lax.dot_general(
            jnp.concatenate(pieces, 0), part, (((1,), (1,)), ((), ())), preferred_element_type=F32
        )
    sign = jnp.concatenate(signs, 1)
    total = (total[:size] + total[size:] * sign) * back_scale
    own = maps // groups
    low_rows = rows // 2
    for f in range(groups):
        pieces = []
        for low in range(low_rows):
            for o in range(ORD_DEV):
                at = [(high * low_rows + low) * maps + f * own for high in range(2)]
                pieces += list(
                    swap_halves(
                        *[total[a : a + own, o * LANES : (o + 1) * LANES] for a in at]
                    )
                )
        turned = jnp.concatenate(pieces, 0).T
        for high in range(2):
            mixed[pl.ds(f * 2 * pairs + high, pairs, stride=2), :] = turned[
                high * pairs : (high + 1) * pairs
            ]
    out_ref[...] = mixed[...].astype(BF16)


def pixels(got, table, signs, weight, groups, scales, chunk=256):
    return pl.pallas_call(
        lambda *refs: pixel_kernel(groups, chunk, scales, *refs),
        name="pixels",
        out_shape=pltpu.VMEM(got.shape, BF16),
        in_specs=[pl.BlockSpec(memory_space=pltpu.VMEM)] * 4,
        out_specs=pl.BlockSpec(memory_space=pltpu.VMEM),
        scratch_shapes=[
            pltpu.VMEM(got.shape, F32),
            pltpu.VMEM((got.shape[0], 2 * LANES), BF16),
            pltpu.VMEM(got.shape, F32),
        ],
        compiler_params=limits(8),
    )(on_chip(got), table, signs, on_chip(weight))


def backward_kernel(cuts, ids_ref, beam_ref, got_ref, leg_ref, out_ref, mixed, terms):
    lats = leg_ref.shape[1]
    groups, degrees = beam_ref.shape
    tiles = degrees // LANES
    slot = lax.axis_index("order") * ORD_DEV
    span = got_ref.shape[0] // groups
    width = LANES // groups
    lows = lats // span
    own = width // (2 * ORD_DEV)
    blocks = [got_ref[pl.ds(f * span, span), :].astype(F32) for f in range(groups)]
    lane_group = lane_ids((span, LANES)) // width
    turned = [
        [v if k == 0 else pltpu.roll(v, k * width, 1) for k in range(groups)] for v in blocks
    ]
    for low in range(lows):
        merged = turned[0][(0 - low) % groups]
        for f in range(1, groups):
            merged = jnp.where(lane_group == f, turned[f][(f - low) % groups], merged)
        mixed[pl.ds(low, span, stride=lows), :] = merged
    rows = mixed[...].T.astype(BF16)
    lhs = jnp.concatenate(
        [
            rows[f * width + o * 2 * own : f * width + (o + 1) * 2 * own]
            for o in range(ORD_DEV)
            for f in range(groups)
        ],
        0,
    )
    out_ref[...] = jnp.zeros_like(out_ref)
    lane = lane_ids((1, LANES))
    steps = live_steps(ids_ref, slot, tiles)
    half = groups * 2 * own
    for lo, hi in zip(cuts[:-1], cuts[1:]):
        cols = pl.ds(lo * LANES, (hi - lo) * LANES)
        terms[:, cols] = lax.dot_general(
            lhs, leg_ref[cols, :], (((1,), (1,)), ((), ())), preferred_element_type=F32
        )
        for i in range(lo, hi):
            order, tile = steps[i]
            start = pl.multiple_of(tile * LANES, LANES)
            live = lane + start >= ids_ref[slot + order]
            part = terms[pl.ds(pl.multiple_of(order * half, half), half), pl.ds(i * LANES, LANES)]
            total = jnp.zeros((2 * own, LANES), F32)
            for f in range(groups):
                shaping = jnp.where(live, beam_ref[f : f + 1, pl.ds(start, LANES)], 0.0)
                total += part[f * 2 * own : (f + 1) * 2 * own] * shaping
            for c in range(2):
                out_ref[:, order * 2 * tiles + tile * 2 + c, :] = total[c * own : (c + 1) * own]


def backward(order_ids, beam, got, legendre, own):
    degrees = beam.shape[1]
    shape = (own, ORD_DEV * 2 * degrees // LANES, LANES)
    cuts = (0, 33)
    return pl.pallas_call(
        lambda *refs: backward_kernel(cuts, *refs),
        name="backward",
        out_shape=jax.ShapeDtypeStruct(shape, F32),
        in_specs=[pl.BlockSpec(memory_space=pltpu.SMEM)] + [pl.BlockSpec(memory_space=pltpu.VMEM)] * 3,
        out_specs=pl.BlockSpec(memory_space=pltpu.VMEM),
        scratch_shapes=[
            pltpu.VMEM((legendre.shape[1], LANES), F32),
            pltpu.VMEM((LANES, legendre.shape[0]), F32),
        ],
        compiler_params=limits(8),
    )(order_ids, on_chip(beam), on_chip(got), legendre)


def on_device(harmonics, legendre, beam_window, order_ids, noise_weight):
    maps, _, _, degrees = harmonics.shape
    lats = legendre.shape[2]
    nlon = noise_weight.shape[2]
    orders_all = order_ids.shape[0]
    groups = beam_window.shape[0]
    tiles = degrees // LANES
    own = maps // groups
    pairs = orders_all // ORD_DEV
    scales = (1.0 / math.sqrt(2.0 * orders_all), 1.0 / math.sqrt(1.0 * nlon))
    harm = harmonics.reshape(maps, ORD_DEV, 2, tiles, LANES).transpose(0, 1, 3, 2, 4)
    harm = harm.reshape(maps, ORD_DEV, -1, LANES)
    columns, legendre, table, signs = forward(order_ids, beam_window, harm, legendre, nlon)
    columns = columns.reshape(pairs, lats // pairs, -1)
    got = lax.all_to_all(columns, "order", split_axis=0, concat_axis=0, tiled=True)
    terms = pixels(got.reshape(lats, -1), table, signs, noise_weight[0], groups, scales)
    terms = terms.reshape(groups * pairs, -1, LANES)
    back = lax.all_to_all(terms, ("freq", "order"), split_axis=0, concat_axis=0, tiled=True)
    out = backward(order_ids, beam_window, back.reshape(-1, LANES), legendre, own)
    out = out.reshape(own, ORD_DEV, tiles, 2, LANES).transpose(0, 1, 3, 2, 4)
    return out.reshape(own, ORD_DEV, 2, degrees)


def solution(mesh):
    return jax.shard_map(
        on_device,
        mesh=mesh,
        in_specs=(
            P(None, "order", None, None),
            P("order", None, None),
            P(),
            P(),
            P("freq", "order", None),
        ),
        out_specs=P("freq", "order", None, None),
        check_vma=False,
    )
```

time: 58.5 us -> 54.5 us (0.932)
  blocking collectives: 20.4 us -> 43.7 us
  starting transfers between devices: 13.6 us -> 0 us
  waiting for transfers between devices: 8.41 us -> 0 us
  Pallas kernels: 15.8 us -> 10.6 us
    all_to_all x0 -> x1, blocking collectives: none -> 23.2 us  [on_device(): lax.all_to_all(columns, 'order', split_axis=0, concat_axis=0, tiled=True)]
    all_to_all x1 -> x0, starting transfers between devices: 13.6 us -> none  [on_device(): lax.all_to_all(columns, 'order', split_axis=0, concat_axis=0, tiled=True)]
    all_to_all x1 -> x0, waiting for transfers between devices: 8.41 us -> none  [on_device(): lax.all_to_all(columns, 'order', split_axis=0, concat_axis=0, tiled=True)]
    pallas_call x3 -> x2, Pallas kernels: 12.4 us -> 7.69 us  [the longest x1 4.47 us: forward(): pl.pallas_call(lambda *refs: forward_kernel(nlon, cuts, *refs), name='for...]
  transfers between devices with their start and end apart: 1 -> 0, of which waited for: 1 -> 0; matrix products, arithmetic and copies ran while one was open for 0% -> 0% of each run, Pallas kernels for 3% -> 0%
where the time goes in v4:
time: 54.5 us; the launch traced here: 54.3 us
  blocking collectives  43.7 us (80%)
  Pallas kernels  10.6 us (19%)
    all_to_all x1, blocking collectives, on_device(): lax.all_to_all(columns, 'order', split_axis=0, concat_axis=0, tiled=True)  23.2 us
    all_to_all x1, blocking collectives, on_device(): lax.all_to_all(terms, ('freq', 'order'), split_axis=0, concat_axis=0, til...  20.5 us
    pallas_call x1, Pallas kernels, forward(): pl.pallas_call(lambda *refs: forward_kernel(nlon, cuts, *refs), name='for...  4.47 us
    pallas_call x1, Pallas kernels, backward(): pl.pallas_call(lambda *refs: backward_kernel(cuts, *refs), name='backward...  3.22 us
    pallas_call x1, Pallas kernels, pixels(): pl.pallas_call(lambda *refs: pixel_kernel(groups, chunk, scales, *refs),...  2.92 us

profile of v4, /device:TPU:1, one launch (start us, length us, event | category | flops | bytes accessed | tf_op | source)
XLA Modules:
  0.0 54.3 jit_solution(10817437403679273989)
XLA Ops:
  0.0 0.0 copy-start
  0.0 0.0 copy-start.1
  0.0 0.0 copy-start.2
  0.0 4.5 %forward.1 = (bf16[512,128]{1,0:T(8,128)(2,1)S(1)}, bf16[4224,512]{1,0:T(8,128)(2,1)S(1)}, bf16[256,4096]{1,0:T(8,128)(2,1)S(1)}, f32[16,128]{1,0:T(8,128)S(1)}) custom-call(s32[128]{0:T(128)} %refs_0_.3, s32[1,128]{1,0:T(1,128)} %bitcast.21, f32[4,4096]{1,0:T(4,128)} %refs_1_.1, bf16[32,2,64,128]{3,2,1,0:T(8,128)(2,1)} %bitcast.22, ...), custom_call_target="tpu_custom_call" | custom-call | tf_op jit(solution)/shard_map/forward/pallas_call | solution.py:191
  4.5 23.2 %all_to_all.10 = bf16[64,8,128]{2,1,0:T(8,128)(2,1)S(1)} all-to-all(bf16[64,8,128]{2,1,0:T(8,128)(2,1)S(1)} %bitcast.20), channel_id=1, replica_groups=mesh['freq'=4,'order'=64] {'order'}, dimensions={0} | all-to-all | bytes 262144 | tf_op jit(solution)/shard_map/all_to_all | solution.py:377
  27.7 0.0 copy-done
  27.7 2.9 %pixels.1 = bf16[512,128]{1,0:T(8,128)(2,1)S(1)} custom-call(bf16[512,128]{1,0:T(8,128)(2,1)S(1)} %bitcast.16, bf16[256,4096]{1,0:T(8,128)(2,1)S(1)} %get-tuple-element.10.refs_1_, f32[16,128]{1,0:T(8,128)S(1)} %get-tuple-element.11.refs_2_, f32[8,8192]{1,0:T(8,128)S(1)} %bitcast.19), custom_call_target="tpu_custom_call" | custom-call | tf_op jit(solution)/shard_map/pixels/pallas_call | solution.py:280
  30.6 20.5 %all_to_all.11 = bf16[256,2,128]{2,1,0:T(2,128)(2,1)S(1)} all-to-all(bf16[256,2,128]{2,1,0:T(2,128)(2,1)S(1)} %bitcast.17), channel_id=1, replica_groups=mesh['freq'=4,'order'=64] {'freq','order'}, dimensions={0} | all-to-all | bytes 262144 | tf_op jit(solution)/shard_map/all_to_all | solution.py:380
  51.1 0.0 copy-done.1
  51.1 0.0 copy-done.2
  51.1 3.2 %backward.1 = f32[8,128,128]{2,1,0:T(8,128)} custom-call(s32[128]{0:T(128)S(1)} %copy-done.2, f32[4,4096]{1,0:T(4,128)S(1)} %copy-done.1, bf16[512,128]{1,0:T(8,128)(2,1)S(1)} %bitcast.18, bf16[4224,512]{1,0:T(8,128)(2,1)S(1)} %get-tuple-element.12.refs_3_), custom_call_target="tpu_custom_call" | custom-call | tf_op jit(solution)/shard_map/backward/pallas_call | solution.py:349
Async XLA Ops:
  0.0 27.7 %copy-start = (f32[1,8,8192]{2,1,0:T(8,128)S(1)}, f32[1,8,8192]{2,1,0:T(8,128)}, u32[]{:S(2)}) copy-start(f32[1,8,8192]{2,1,0:T(8,128)} %param.9) | copy-start | bytes 786436
  0.0 51.1 %copy-start.1 = (f32[4,4096]{1,0:T(4,128)S(1)}, f32[4,4096]{1,0:T(4,128)}, u32[]{:S(2)}) copy-start(f32[4,4096]{1,0:T(4,128)} %refs_1_.1) | copy-start | bytes 196612
  0.0 51.1 %copy-start.2 = (s32[128]{0:T(128)S(1)}, s32[128]{0:T(128)}, u32[]{:S(2)}) copy-start(s32[128]{0:T(128)} %refs_0_.3) | copy-start | bytes 1540

commit v5 on v4

--- a/solution.py
+++ b/solution.py
@@ -88,20 +88,42 @@
                 out_ref[pl.ds(at + half, block), cols] = (-(cs * cos) - cc * sin).astype(BF16)
 
 
-def live_steps(ids_ref, slot, tiles):
-    first = [ids_ref[slot + o] // LANES for o in range(ORD_DEV)]
-    count = tiles - first[0]
+TILE = 2 * LANES
+
+
+def lower_slot(ids_ref, slot):
+    return jnp.where(ids_ref[slot] < ids_ref[slot + 1], 0, 1)
+
+
+def live_steps(ids_ref, slot, degrees):
+    tiles = degrees // TILE
+    low = lower_slot(ids_ref, slot)
+    first_low = ids_ref[slot + low] // TILE
+    first_high = ids_ref[slot + 1 - low] // TILE
+    count = tiles // 2 - first_low
+    steps = [(low, degrees // 2 + k * TILE) for k in range(tiles // 2)]
+    for k in range(tiles // 2 + 1):
+        later = k >= count
+        tile = jnp.where(later, first_high + k - count, first_low + k)
+        steps.append((jnp.where(later, 1 - low, low), pl.multiple_of(tile * TILE, TILE)))
+    return steps
+
+
+def dead_steps(ids_ref, slot, degrees):
+    tiles = degrees // TILE
+    low = lower_slot(ids_ref, slot)
+    count = ids_ref[slot + low] // TILE
     steps = []
-    for i in range(tiles + 1):
-        later = i >= count
-        order = jnp.where(later, 1, 0)
-        steps.append((order, jnp.where(later, first[1] + i - count, first[0] + i)))
+    for k in range(tiles - 1):
+        later = k >= count
+        tile = jnp.where(later, k - count, k)
+        steps.append((jnp.where(later, 1 - low, low), pl.multiple_of(tile * TILE, TILE)))
     return steps
 
 
 def forward_kernel(
     nlon,
-    cuts,
+    plan,
     ids_hbm,
     ids_row_hbm,
     beam_ref,
@@ -125,9 +147,9 @@
     leg_sems,
 ):
     degrees = leg_ref.shape[1]
+    upper = degrees // 2
     maps = harm_ref.shape[0]
-    tiles = degrees // LANES
-    rows = 2 * tiles
+    rows = harm_ref.shape[2]
     mids = 8
     slot = lax.axis_index("order") * ORD_DEV
     group = lax.axis_index("freq")
@@ -137,16 +159,24 @@
         pltpu.make_async_copy(beam_ref, beam_v, sems.at[2]),
         pltpu.make_async_copy(harm_ref, harm_v, sems.at[3]),
     ]
+
+    def upper_copy(order):
+        return pltpu.make_async_copy(
+            leg_ref.at[order, pl.ds(upper, upper), :], leg_v.at[pl.ds(0, upper), :], sems.at[4]
+        )
+
     for copy in copies:
         copy.start()
+    upper_copy(0).start()
     copies[0].wait()
-    steps = live_steps(ids_ref, slot, tiles)
+    steps = live_steps(ids_ref, slot, degrees)
+    fixed = upper // TILE
     leg_copies = []
-    for i, (order, tile) in enumerate(steps):
+    for k, (order, start) in enumerate(steps[fixed:]):
         copy = pltpu.make_async_copy(
-            leg_ref.at[order, pl.ds(pl.multiple_of(tile * LANES, LANES), LANES), :],
-            leg_v.at[pl.ds(i * LANES, LANES), :],
-            leg_sems.at[i],
+            leg_ref.at[order, pl.ds(start, TILE), :],
+            leg_v.at[pl.ds(upper + k * TILE, TILE), :],
+            leg_sems.at[k],
         )
         copy.start()
         leg_copies.append(copy)
@@ -159,25 +189,45 @@
         for o in range(ORD_DEV):
             wide[pl.ds((b * ORD_DEV + o) * rows, rows), :] = harm_v[b, o].astype(F32)
     lane = lane_ids((1, LANES))
-    blank = jnp.zeros((2 * maps, LANES), BF16)
-    for i, (order, tile) in enumerate(steps):
-        start = pl.multiple_of(tile * LANES, LANES)
-        live = lane + start >= ids_ref[slot + order]
-        shaping = jnp.where(live, own_beam[:, pl.ds(start, LANES)], 0.0)
-        at = pl.multiple_of(order * (2 * maps), 2 * maps)
-        cols = pl.ds(i * LANES, LANES)
-        lhs[pl.ds(2 * maps - at, 2 * maps), cols] = blank
-        for c in range(2):
-            values = wide[pl.ds(order * rows + tile * 2 + c, maps, stride=ORD_DEV * rows), :]
-            lhs[pl.ds(at + c * maps, maps), cols] = (values * shaping).astype(BF16)
-    table_rows(table_ref, small, fine, mids, range(0, small.shape[1], 16))
-    total = None
-    for lo, hi in zip(cuts[:-1], cuts[1:]):
-        for copy in leg_copies[lo:hi]:
-            copy.wait()
-        span = pl.ds(lo * LANES, (hi - lo) * LANES)
-        part = jnp.dot(lhs[:, span], leg_v[span, :], preferred_element_type=F32)
-        total = part if total is None else total + part
+    blank = jnp.zeros((2 * maps, TILE), BF16)
+
+    def prepare(some):
+        for i in some:
+            order, first = steps[i]
+            at = pl.multiple_of(order * (2 * maps), 2 * maps)
+            lhs[pl.ds(2 * maps - at, 2 * maps), pl.ds(i * TILE, TILE)] = blank
+            for t in range(TILE // LANES):
+                start = first + t * LANES
+                if not isinstance(start, int):
+                    start = pl.multiple_of(start, LANES)
+                live = lane + start >= ids_ref[slot + order]
+                shaping = jnp.where(live, own_beam[:, pl.ds(start, LANES)], 0.0)
+                for c in range(2):
+                    row = order * rows + start // LANES * 2 + c
+                    values = wide[pl.ds(row, maps, stride=ORD_DEV * rows), :]
+                    lhs[pl.ds(at + c * maps, maps), pl.ds(i * TILE + t * LANES, LANES)] = (
+                        values * shaping
+                    ).astype(BF16)
+
+    table_blocks = list(range(0, small.shape[1], 16))
+    prepare(range(fixed))
+    table_rows(table_ref, small, fine, mids, table_blocks[: plan[0]])
+    upper_copy(0).wait()
+
+    @pl.when(lower_slot(ids_ref, slot) == 1)
+    def _():
+        copy = upper_copy(1)
+        copy.start()
+        copy.wait()
+
+    total = jnp.dot(lhs[:, pl.ds(0, upper)], leg_v[pl.ds(0, upper), :], preferred_element_type=F32)
+    prepare(range(fixed, len(steps)))
+    table_rows(table_ref, small, fine, mids, table_blocks[plan[0] : plan[1]])
+    for copy in leg_copies:
+        copy.wait()
+    rest = pl.ds(upper, leg_v.shape[0] - upper)
+    total += jnp.dot(lhs[:, rest], leg_v[rest, :], preferred_element_type=F32)
+    table_rows(table_ref, small, fine, mids, table_blocks[plan[1] :])
     out_ref[...] = total.T.astype(BF16)
 
 
@@ -186,14 +236,13 @@
     maps = harm.shape[0]
     orders = order_ids.shape[0]
     ids_row = order_ids.reshape(1, -1)
-    steps = degrees // LANES + 1
-    cuts = (0, steps)
+    live = degrees + TILE
     return pl.pallas_call(
-        lambda *refs: forward_kernel(nlon, cuts, *refs),
+        lambda *refs: forward_kernel(nlon, (2, 5), *refs),
         name="forward",
         out_shape=(
             pltpu.VMEM((lats, ORD_DEV * 2 * maps), BF16),
-            pltpu.VMEM((steps * LANES, lats), BF16),
+            pltpu.VMEM((live, lats), BF16),
             pltpu.VMEM((2 * orders, nlon // 2), BF16),
             pltpu.VMEM((8 * ORD_DEV, LANES), F32),
         ),
@@ -205,13 +254,13 @@
             pltpu.VMEM((1, degrees), F32),
             pltpu.VMEM(harm.shape, BF16),
             pltpu.VMEM((maps * ORD_DEV * harm.shape[2], LANES), F32),
-            pltpu.VMEM((ORD_DEV * 2 * maps, steps * LANES), BF16),
+            pltpu.VMEM((ORD_DEV * 2 * maps, live), BF16),
             pltpu.VMEM((orders, orders), F32),
             pltpu.VMEM((2, orders, LANES), F32),
             pltpu.VMEM((2, orders, LANES), F32),
             pltpu.SMEM(order_ids.shape, jnp.int32),
-            pltpu.SemaphoreType.DMA((4,)),
-            pltpu.SemaphoreType.DMA((steps,)),
+            pltpu.SemaphoreType.DMA((5,)),
+            pltpu.SemaphoreType.DMA((degrees // TILE // 2 + 1,)),
         ],
         compiler_params=limits(16),
     )(*[off_chip(v) for v in (order_ids, ids_row, beam, harm, legendre)])
@@ -292,15 +341,19 @@
     )(on_chip(got), table, signs, on_chip(weight))
 
 
-def backward_kernel(cuts, ids_ref, beam_ref, got_ref, leg_ref, out_ref, mixed, terms):
+def backward_kernel(
+    cuts, ids_vmem, beam_ref, got_ref, leg_ref, out_ref, mixed, terms, result, blank, ids_ref, sems, zero_sems
+):
+    ids_copy = pltpu.make_async_copy(ids_vmem, ids_ref, sems.at[cuts[-1]])
+    ids_copy.start()
     lats = leg_ref.shape[1]
     groups, degrees = beam_ref.shape
-    tiles = degrees // LANES
     slot = lax.axis_index("order") * ORD_DEV
     span = got_ref.shape[0] // groups
     width = LANES // groups
     lows = lats // span
     own = width // (2 * ORD_DEV)
+    blank[...] = jnp.zeros_like(blank)
     blocks = [got_ref[pl.ds(f * span, span), :].astype(F32) for f in range(groups)]
     lane_group = lane_ids((span, LANES)) // width
     turned = [
@@ -312,7 +365,7 @@
             merged = jnp.where(lane_group == f, turned[f][(f - low) % groups], merged)
         mixed[pl.ds(low, span, stride=lows), :] = merged
     rows = mixed[...].T.astype(BF16)
-    lhs = jnp.concatenate(
+    rhs = jnp.concatenate(
         [
             rows[f * width + o * 2 * own : f * width + (o + 1) * 2 * own]
             for o in range(ORD_DEV)
@@ -320,44 +373,75 @@
         ],
         0,
     )
-    out_ref[...] = jnp.zeros_like(out_ref)
     lane = lane_ids((1, LANES))
-    steps = live_steps(ids_ref, slot, tiles)
+    ids_copy.wait()
+    steps = live_steps(ids_ref, slot, degrees)
+    per_tile = 2 * TILE // LANES
+    per_order = 2 * degrees // LANES
     half = groups * 2 * own
+
+    def out_rows(order, start):
+        return pl.ds(order * per_order + start // LANES * 2, per_tile)
+
+    copies = []
+    for k, (order, start) in enumerate(dead_steps(ids_ref, slot, degrees)):
+        copy = pltpu.make_async_copy(
+            blank, out_ref.at[:, out_rows(order, start), :], zero_sems.at[k]
+        )
+        copy.start()
+        copies.append(copy)
     for lo, hi in zip(cuts[:-1], cuts[1:]):
-        cols = pl.ds(lo * LANES, (hi - lo) * LANES)
+        cols = pl.ds(lo * TILE, (hi - lo) * TILE)
         terms[:, cols] = lax.dot_general(
-            lhs, leg_ref[cols, :], (((1,), (1,)), ((), ())), preferred_element_type=F32
-        )
+            leg_ref[cols, :], rhs, (((1,), (1,)), ((), ())), preferred_element_type=F32
+        ).T
         for i in range(lo, hi):
-            order, tile = steps[i]
-            start = pl.multiple_of(tile * LANES, LANES)
-            live = lane + start >= ids_ref[slot + order]
-            part = terms[pl.ds(pl.multiple_of(order * half, half), half), pl.ds(i * LANES, LANES)]
-            total = jnp.zeros((2 * own, LANES), F32)
-            for f in range(groups):
-                shaping = jnp.where(live, beam_ref[f : f + 1, pl.ds(start, LANES)], 0.0)
-                total += part[f * 2 * own : (f + 1) * 2 * own] * shaping
-            for c in range(2):
-                out_ref[:, order * 2 * tiles + tile * 2 + c, :] = total[c * own : (c + 1) * own]
+            order, first = steps[i]
+            for t in range(TILE // LANES):
+                start = first + t * LANES
+                if not isinstance(start, int):
+                    start = pl.multiple_of(start, LANES)
+                live = lane + start >= ids_ref[slot + order]
+                part = terms[
+                    pl.ds(pl.multiple_of(order * half, half), half), pl.ds(i * TILE + t * LANES, LANES)
+                ]
+                total = jnp.zeros((2 * own, LANES), F32)
+                for f in range(groups):
+                    shaping = jnp.where(live, beam_ref[f : f + 1, pl.ds(start, LANES)], 0.0)
+                    total += part[f * 2 * own : (f + 1) * 2 * own] * shaping
+                for c in range(2):
+                    result[i, :, t * 2 + c, :] = total[c * own : (c + 1) * own]
+            copy = pltpu.make_async_copy(
+                result.at[i], out_ref.at[:, out_rows(order, first), :], sems.at[i]
+            )
+            copy.start()
+            copies.append(copy)
+    for copy in copies:
+        copy.wait()
 
 
 def backward(order_ids, beam, got, legendre, own):
     degrees = beam.shape[1]
-    shape = (own, ORD_DEV * 2 * degrees // LANES, LANES)
-    cuts = (0, 33)
+    tiles = legendre.shape[0] // TILE
+    cuts = (0, 17)
+    per_tile = 2 * TILE // LANES
     return pl.pallas_call(
         lambda *refs: backward_kernel(cuts, *refs),
         name="backward",
-        out_shape=jax.ShapeDtypeStruct(shape, F32),
-        in_specs=[pl.BlockSpec(memory_space=pltpu.SMEM)] + [pl.BlockSpec(memory_space=pltpu.VMEM)] * 3,
-        out_specs=pl.BlockSpec(memory_space=pltpu.VMEM),
+        out_shape=jax.ShapeDtypeStruct((own, ORD_DEV * 2 * degrees // LANES, LANES), F32),
+        in_specs=[pl.BlockSpec(memory_space=pltpu.VMEM)] * 4,
+        out_specs=pl.BlockSpec(memory_space=pl.ANY),
         scratch_shapes=[
             pltpu.VMEM((legendre.shape[1], LANES), F32),
             pltpu.VMEM((LANES, legendre.shape[0]), F32),
+            pltpu.VMEM((tiles, own, per_tile, LANES), F32),
+            pltpu.VMEM((own, per_tile, LANES), F32),
+            pltpu.SMEM(order_ids.shape, jnp.int32),
+            pltpu.SemaphoreType.DMA((tiles + 1,)),
+            pltpu.SemaphoreType.DMA((degrees // TILE - 1,)),
         ],
         compiler_params=limits(8),
-    )(order_ids, on_chip(beam), on_chip(got), legendre)
+    )(on_chip(order_ids), on_chip(beam), on_chip(got), legendre)
 
 
 def on_device(harmonics, legendre, beam_window, order_ids, noise_weight):

time: 54.5 us -> 53.9 us (0.989)
  no operation moved by 1% of the time
where the time goes in v5:
time: 53.9 us; the launch traced here: 53.8 us
  blocking collectives  43.7 us (81%)
  Pallas kernels  10.1 us (19%)
    all_to_all x1, blocking collectives, on_device(): lax.all_to_all(columns, 'order', split_axis=0, concat_axis=0, tiled=True)  23.3 us
    all_to_all x1, blocking collectives, on_device(): lax.all_to_all(terms, ('freq', 'order'), split_axis=0, concat_axis=0, til...  20.4 us
    pallas_call x1, Pallas kernels, forward(): pl.pallas_call(lambda *refs: forward_kernel(nlon, (2, 5), *refs), name='f...  4.12 us
    pallas_call x1, Pallas kernels, backward(): pl.pallas_call(lambda *refs: backward_kernel(cuts, *refs), name='backward...  3.01 us
    pallas_call x1, Pallas kernels, pixels(): pl.pallas_call(lambda *refs: pixel_kernel(groups, chunk, scales, *refs),...  2.93 us

profile of v5, /device:TPU:1, one launch (start us, length us, event | category | flops | bytes accessed | tf_op | source)
XLA Modules:
  0.0 53.8 jit_solution(9032448934435834851)
XLA Ops:
  0.0 0.0 copy-start.1
  0.0 0.0 copy-start
  0.0 0.0 copy-start.2
  0.0 4.1 %forward.1 = (bf16[512,128]{1,0:T(8,128)(2,1)S(1)}, bf16[4352,512]{1,0:T(8,128)(2,1)S(1)}, bf16[256,4096]{1,0:T(8,128)(2,1)S(1)}, f32[16,128]{1,0:T(8,128)S(1)}) custom-call(s32[128]{0:T(128)} %refs_0_.3, s32[1,128]{1,0:T(1,128)} %bitcast.21, f32[4,4096]{1,0:T(4,128)} %refs_1_.1, bf16[32,2,64,128]{3,2,1,0:T(8,128)(2,1)} %bitcast.22, ...), custom_call_target="tpu_custom_call" | custom-call | tf_op jit(solution)/shard_map/forward/pallas_call | solution.py:240
  4.1 23.3 %all_to_all.10 = bf16[64,8,128]{2,1,0:T(8,128)(2,1)S(1)} all-to-all(bf16[64,8,128]{2,1,0:T(8,128)(2,1)S(1)} %bitcast.20), channel_id=1, replica_groups=mesh['freq'=4,'order'=64] {'order'}, dimensions={0} | all-to-all | bytes 262144 | tf_op jit(solution)/shard_map/all_to_all | solution.py:461
  27.4 0.0 copy-done.1
  27.4 2.9 %pixels.1 = bf16[512,128]{1,0:T(8,128)(2,1)S(1)} custom-call(bf16[512,128]{1,0:T(8,128)(2,1)S(1)} %bitcast.16, bf16[256,4096]{1,0:T(8,128)(2,1)S(1)} %get-tuple-element.10.refs_1_, f32[16,128]{1,0:T(8,128)S(1)} %get-tuple-element.11.refs_2_, f32[8,8192]{1,0:T(8,128)S(1)} %bitcast.19), custom_call_target="tpu_custom_call" | custom-call | tf_op jit(solution)/shard_map/pixels/pallas_call | solution.py:329
  30.3 20.4 %all_to_all.11 = bf16[256,2,128]{2,1,0:T(2,128)(2,1)S(1)} all-to-all(bf16[256,2,128]{2,1,0:T(2,128)(2,1)S(1)} %bitcast.17), channel_id=1, replica_groups=mesh['freq'=4,'order'=64] {'freq','order'}, dimensions={0} | all-to-all | bytes 262144 | tf_op jit(solution)/shard_map/all_to_all | solution.py:464
  50.8 0.0 copy-done
  50.8 0.0 copy-done.2
  50.8 3.0 %backward.1 = f32[8,128,128]{2,1,0:T(8,128)} custom-call(s32[128]{0:T(128)S(1)} %copy-done.2, f32[4,4096]{1,0:T(4,128)S(1)} %copy-done, bf16[512,128]{1,0:T(8,128)(2,1)S(1)} %bitcast.18, bf16[4352,512]{1,0:T(8,128)(2,1)S(1)} %get-tuple-element.12.refs_3_), custom_call_target="tpu_custom_call" | custom-call | tf_op jit(solution)/shard_map/backward/pallas_call | solution.py:428
Async XLA Ops:
  0.0 27.4 %copy-start.1 = (f32[1,8,8192]{2,1,0:T(8,128)S(1)}, f32[1,8,8192]{2,1,0:T(8,128)}, u32[]{:S(2)}) copy-start(f32[1,8,8192]{2,1,0:T(8,128)} %param.9) | copy-start | bytes 786436
  0.0 50.8 %copy-start = (f32[4,4096]{1,0:T(4,128)S(1)}, f32[4,4096]{1,0:T(4,128)}, u32[]{:S(2)}) copy-start(f32[4,4096]{1,0:T(4,128)} %refs_1_.1) | copy-start | bytes 196612
  0.0 50.8 %copy-start.2 = (s32[128]{0:T(128)S(1)}, s32[128]{0:T(128)}, u32[]{:S(2)}) copy-start(s32[128]{0:T(128)} %refs_0_.3) | copy-start | bytes 1540

commit v6 on v5

--- a/solution.py
+++ b/solution.py
@@ -36,10 +36,24 @@
     return first, second
 
 
+def cos_sin(turns, nlon):
+    quarter = nlon // 4
+    quadrant = (turns + quarter // 2) // quarter
+    x = (turns - quadrant * quarter).astype(F32) * (2.0 * math.pi / nlon)
+    y = x * x
+    cos = 1.0 + y * (-0.5 + y * (1.0 / 24 + y * (-1.0 / 720 + y * (1.0 / 40320))))
+    sin = x + x * y * (-1.0 / 6 + y * (1.0 / 120 + y * (-1.0 / 5040 + y * (1.0 / 362880))))
+    swap = (quadrant & 1) == 1
+    first = jnp.where(swap, sin, cos)
+    second = jnp.where(swap, cos, sin)
+    first = jnp.where(((quadrant + 1) & 2) == 2, -first, first)
+    second = jnp.where((quadrant & 2) == 2, -second, second)
+    return first, second
+
+
 def table_angles(nlon, ids_row, sign_ref, slots, small, fine, mids):
     rows = ids_row.shape[1]
     half = rows // ORD_DEV
-    unit = 2.0 * math.pi / nlon
     slots[...] = jnp.broadcast_to(ids_row.astype(F32), (rows, rows)).T
     lane = lane_ids((half, LANES))
     steps = jnp.where(lane < LANES // 2, lane * LANES, (lane - LANES // 2) * (mids * LANES))
@@ -47,13 +61,13 @@
         wide_ids = slots[pl.ds(o, half, stride=ORD_DEV), :]
         ids = wide_ids.astype(jnp.int32)
         factor = jnp.where((ids == 0) | (lane < LANES // 2), 1.0, 2.0)
-        angle = ((ids * steps) & (nlon - 1)).astype(F32) * unit
         part = pl.ds(o * half, half)
-        small[0, part, :] = factor * jnp.cos(angle)
-        small[1, part, :] = factor * jnp.sin(angle)
-        angle = ((ids * lane) & (nlon - 1)).astype(F32) * unit
-        fine[0, part, :] = jnp.cos(angle)
-        fine[1, part, :] = jnp.sin(angle)
+        cos, sin = cos_sin((ids * steps) & (nlon - 1), nlon)
+        small[0, part, :] = factor * cos
+        small[1, part, :] = factor * sin
+        cos, sin = cos_sin((ids * lane) & (nlon - 1), nlon)
+        fine[0, part, :] = cos
+        fine[1, part, :] = sin
         across = jnp.concatenate([wide_ids, wide_ids], 0).T[0:8]
         odd = across.astype(jnp.int32) & 1
         sign_ref[pl.ds(o * 8, 8), :] = (1 - 2 * odd).astype(F32)
@@ -89,6 +103,7 @@
 
 
 TILE = 2 * LANES
+PAD = 9
 
 
 def lower_slot(ids_ref, slot):
@@ -142,6 +157,7 @@
     slots,
     small,
     fine,
+    partial,
     ids_ref,
     sems,
     leg_sems,
@@ -187,7 +203,7 @@
     copies[3].wait()
     for b in range(maps):
         for o in range(ORD_DEV):
-            wide[pl.ds((b * ORD_DEV + o) * rows, rows), :] = harm_v[b, o].astype(F32)
+            wide[pl.ds(b * (ORD_DEV * rows + PAD) + o * rows, rows), :] = harm_v[b, o].astype(F32)
     lane = lane_ids((1, LANES))
     blank = jnp.zeros((2 * maps, TILE), BF16)
 
@@ -204,7 +220,7 @@
                 shaping = jnp.where(live, own_beam[:, pl.ds(start, LANES)], 0.0)
                 for c in range(2):
                     row = order * rows + start // LANES * 2 + c
-                    values = wide[pl.ds(row, maps, stride=ORD_DEV * rows), :]
+                    values = wide[pl.ds(row, maps, stride=ORD_DEV * rows + PAD), :]
                     lhs[pl.ds(at + c * maps, maps), pl.ds(i * TILE + t * LANES, LANES)] = (
                         values * shaping
                     ).astype(BF16)
@@ -220,13 +236,23 @@
         copy.start()
         copy.wait()
 
-    total = jnp.dot(lhs[:, pl.ds(0, upper)], leg_v[pl.ds(0, upper), :], preferred_element_type=F32)
+    partial[...] = jnp.dot(
+        lhs[:, pl.ds(0, upper)], leg_v[pl.ds(0, upper), :], preferred_element_type=F32
+    )
     prepare(range(fixed, len(steps)))
     table_rows(table_ref, small, fine, mids, table_blocks[plan[0] : plan[1]])
-    for copy in leg_copies:
-        copy.wait()
+
+    def arrived(k, carry):
+        pltpu.make_async_copy(
+            leg_ref.at[0, pl.ds(0, TILE), :],
+            leg_v.at[pl.ds(pl.multiple_of(upper + k * TILE, TILE), TILE), :],
+            leg_sems.at[k],
+        ).wait()
+        return carry
+
+    lax.fori_loop(0, len(leg_copies), arrived, 0)
     rest = pl.ds(upper, leg_v.shape[0] - upper)
-    total += jnp.dot(lhs[:, rest], leg_v[rest, :], preferred_element_type=F32)
+    total = partial[...] + jnp.dot(lhs[:, rest], leg_v[rest, :], preferred_element_type=F32)
     table_rows(table_ref, small, fine, mids, table_blocks[plan[1] :])
     out_ref[...] = total.T.astype(BF16)
 
@@ -238,7 +264,7 @@
     ids_row = order_ids.reshape(1, -1)
     live = degrees + TILE
     return pl.pallas_call(
-        lambda *refs: forward_kernel(nlon, (2, 5), *refs),
+        lambda *refs: forward_kernel(nlon, (8, 8), *refs),
         name="forward",
         out_shape=(
             pltpu.VMEM((lats, ORD_DEV * 2 * maps), BF16),
@@ -253,11 +279,12 @@
             pltpu.VMEM(beam.shape, F32),
             pltpu.VMEM((1, degrees), F32),
             pltpu.VMEM(harm.shape, BF16),
-            pltpu.VMEM((maps * ORD_DEV * harm.shape[2], LANES), F32),
+            pltpu.VMEM((maps * (ORD_DEV * harm.shape[2] + PAD), LANES), F32),
             pltpu.VMEM((ORD_DEV * 2 * maps, live), BF16),
             pltpu.VMEM((orders, orders), F32),
             pltpu.VMEM((2, orders, LANES), F32),
             pltpu.VMEM((2, orders, LANES), F32),
+            pltpu.VMEM((ORD_DEV * 2 * maps, lats), F32),
             pltpu.SMEM(order_ids.shape, jnp.int32),
             pltpu.SemaphoreType.DMA((5,)),
             pltpu.SemaphoreType.DMA((degrees // TILE // 2 + 1,)),
@@ -364,21 +391,12 @@
         for f in range(1, groups):
             merged = jnp.where(lane_group == f, turned[f][(f - low) % groups], merged)
         mixed[pl.ds(low, span, stride=lows), :] = merged
-    rows = mixed[...].T.astype(BF16)
-    rhs = jnp.concatenate(
-        [
-            rows[f * width + o * 2 * own : f * width + (o + 1) * 2 * own]
-            for o in range(ORD_DEV)
-            for f in range(groups)
-        ],
-        0,
-    )
+    rhs = mixed[...].astype(BF16)
     lane = lane_ids((1, LANES))
     ids_copy.wait()
     steps = live_steps(ids_ref, slot, degrees)
     per_tile = 2 * TILE // LANES
     per_order = 2 * degrees // LANES
-    half = groups * 2 * own
 
     def out_rows(order, start):
         return pl.ds(order * per_order + start // LANES * 2, per_tile)
@@ -392,9 +410,7 @@
         copies.append(copy)
     for lo, hi in zip(cuts[:-1], cuts[1:]):
         cols = pl.ds(lo * TILE, (hi - lo) * TILE)
-        terms[:, cols] = lax.dot_general(
-            leg_ref[cols, :], rhs, (((1,), (1,)), ((), ())), preferred_element_type=F32
-        ).T
+        terms[:, cols] = jnp.dot(leg_ref[cols, :], rhs, preferred_element_type=F32).T
         for i in range(lo, hi):
             order, first = steps[i]
             for t in range(TILE // LANES):
@@ -402,13 +418,12 @@
                 if not isinstance(start, int):
                     start = pl.multiple_of(start, LANES)
                 live = lane + start >= ids_ref[slot + order]
-                part = terms[
-                    pl.ds(pl.multiple_of(order * half, half), half), pl.ds(i * TILE + t * LANES, LANES)
-                ]
                 total = jnp.zeros((2 * own, LANES), F32)
                 for f in range(groups):
+                    at = pl.multiple_of(f * width + order * (2 * own), 2 * own)
+                    part = terms[pl.ds(at, 2 * own), pl.ds(i * TILE + t * LANES, LANES)]
                     shaping = jnp.where(live, beam_ref[f : f + 1, pl.ds(start, LANES)], 0.0)
-                    total += part[f * 2 * own : (f + 1) * 2 * own] * shaping
+                    total += part * shaping
                 for c in range(2):
                     result[i, :, t * 2 + c, :] = total[c * own : (c + 1) * own]
             copy = pltpu.make_async_copy(

time: 53.9 us -> 53.4 us (level)
  Pallas kernels: 10.1 us -> 9.45 us
    pallas_call x1, Pallas kernels: 4.12 us -> 3.54 us  [forward(): pl.pallas_call(lambda *refs: forward_kernel(nlon, (8, 8), *refs), name='f...]
where the time goes in v6:
time: 53.4 us; the launch traced here: 53.2 us
  blocking collectives  43.7 us (82%)
  Pallas kernels  9.45 us (18%)
    all_to_all x1, blocking collectives, on_device(): lax.all_to_all(columns, 'order', split_axis=0, concat_axis=0, tiled=True)  23.3 us
    all_to_all x1, blocking collectives, on_device(): lax.all_to_all(terms, ('freq', 'order'), split_axis=0, concat_axis=0, til...  20.5 us
    pallas_call x1, Pallas kernels, forward(): pl.pallas_call(lambda *refs: forward_kernel(nlon, (8, 8), *refs), name='f...  3.54 us
    pallas_call x1, Pallas kernels, backward(): pl.pallas_call(lambda *refs: backward_kernel(cuts, *refs), name='backward...  2.98 us
    pallas_call x1, Pallas kernels, pixels(): pl.pallas_call(lambda *refs: pixel_kernel(groups, chunk, scales, *refs),...  2.93 us

profile of v6, /device:TPU:1, one launch (start us, length us, event | category | flops | bytes accessed | tf_op | source)
XLA Modules:
  0.0 53.2 jit_solution(10290675124976126127)
XLA Ops:
  0.0 0.0 copy-start.1
  0.0 0.0 copy-start
  0.0 0.0 copy-start.2
  0.0 3.5 %forward.1 = (bf16[512,128]{1,0:T(8,128)(2,1)S(1)}, bf16[4352,512]{1,0:T(8,128)(2,1)S(1)}, bf16[256,4096]{1,0:T(8,128)(2,1)S(1)}, f32[16,128]{1,0:T(8,128)S(1)}) custom-call(s32[128]{0:T(128)} %refs_0_.3, s32[1,128]{1,0:T(1,128)} %bitcast.21, f32[4,4096]{1,0:T(4,128)} %refs_1_.1, bf16[32,2,64,128]{3,2,1,0:T(8,128)(2,1)} %bitcast.22, ...), custom_call_target="tpu_custom_call" | custom-call | tf_op jit(solution)/shard_map/forward/pallas_call | solution.py:266
  3.6 23.3 %all_to_all.10 = bf16[64,8,128]{2,1,0:T(8,128)(2,1)S(1)} all-to-all(bf16[64,8,128]{2,1,0:T(8,128)(2,1)S(1)} %bitcast.20), channel_id=1, replica_groups=mesh['freq'=4,'order'=64] {'order'}, dimensions={0} | all-to-all | bytes 262144 | tf_op jit(solution)/shard_map/all_to_all | solution.py:476
  26.8 0.0 copy-done.1
  26.8 2.9 %pixels.1 = bf16[512,128]{1,0:T(8,128)(2,1)S(1)} custom-call(bf16[512,128]{1,0:T(8,128)(2,1)S(1)} %bitcast.16, bf16[256,4096]{1,0:T(8,128)(2,1)S(1)} %get-tuple-element.10.refs_1_, f32[16,128]{1,0:T(8,128)S(1)} %get-tuple-element.11.refs_2_, f32[8,8192]{1,0:T(8,128)S(1)} %bitcast.19), custom_call_target="tpu_custom_call" | custom-call | tf_op jit(solution)/shard_map/pixels/pallas_call | solution.py:356
  29.7 20.5 %all_to_all.11 = bf16[256,2,128]{2,1,0:T(2,128)(2,1)S(1)} all-to-all(bf16[256,2,128]{2,1,0:T(2,128)(2,1)S(1)} %bitcast.17), channel_id=1, replica_groups=mesh['freq'=4,'order'=64] {'freq','order'}, dimensions={0} | all-to-all | bytes 262144 | tf_op jit(solution)/shard_map/all_to_all | solution.py:479
  50.2 0.0 copy-done
  50.2 0.0 copy-done.2
  50.2 3.0 %backward.1 = f32[8,128,128]{2,1,0:T(8,128)} custom-call(s32[128]{0:T(128)S(1)} %copy-done.2, f32[4,4096]{1,0:T(4,128)S(1)} %copy-done, bf16[512,128]{1,0:T(8,128)(2,1)S(1)} %bitcast.18, bf16[4352,512]{1,0:T(8,128)(2,1)S(1)} %get-tuple-element.12.refs_3_), custom_call_target="tpu_custom_call" | custom-call | tf_op jit(solution)/shard_map/backward/pallas_call | solution.py:443
Async XLA Ops:
  0.0 26.8 %copy-start.1 = (f32[1,8,8192]{2,1,0:T(8,128)S(1)}, f32[1,8,8192]{2,1,0:T(8,128)}, u32[]{:S(2)}) copy-start(f32[1,8,8192]{2,1,0:T(8,128)} %param.9) | copy-start | bytes 786436
  0.0 50.2 %copy-start = (f32[4,4096]{1,0:T(4,128)S(1)}, f32[4,4096]{1,0:T(4,128)}, u32[]{:S(2)}) copy-start(f32[4,4096]{1,0:T(4,128)} %refs_1_.1) | copy-start | bytes 196612
  0.0 50.2 %copy-start.2 = (s32[128]{0:T(128)S(1)}, s32[128]{0:T(128)}, u32[]{:S(2)}) copy-start(s32[128]{0:T(128)} %refs_0_.3) | copy-start | bytes 1540

commit v7 on v6

--- a/solution.py
+++ b/solution.py
@@ -164,8 +164,9 @@
 ):
     degrees = leg_ref.shape[1]
     upper = degrees // 2
-    maps = harm_ref.shape[0]
-    rows = harm_ref.shape[2]
+    groups = beam_ref.shape[0]
+    maps, _, rows, _ = harm_ref.shape
+    own = maps // groups
     mids = 8
     slot = lax.axis_index("order") * ORD_DEV
     group = lax.axis_index("freq")
@@ -173,7 +174,7 @@
         pltpu.make_async_copy(ids_hbm, ids_ref, sems.at[0]),
         pltpu.make_async_copy(ids_row_hbm, ids_row, sems.at[1]),
         pltpu.make_async_copy(beam_ref, beam_v, sems.at[2]),
-        pltpu.make_async_copy(harm_ref, harm_v, sems.at[3]),
+        pltpu.make_async_copy(harm_ref.at[pl.ds(group * own, own)], harm_v, sems.at[3]),
     ]
 
     def upper_copy(order):
@@ -199,9 +200,10 @@
     copies[1].wait()
     table_angles(nlon, ids_row[...], sign_ref, slots, small, fine, mids)
     copies[2].wait()
-    own_beam[...] = beam_v[pl.ds(group, 1), :]
+    for k in range(groups):
+        own_beam[k : k + 1, :] = beam_v[pl.ds(group ^ k, 1), :]
     copies[3].wait()
-    for b in range(maps):
+    for b in range(own):
         for o in range(ORD_DEV):
             wide[pl.ds(b * (ORD_DEV * rows + PAD) + o * rows, rows), :] = harm_v[b, o].astype(F32)
     lane = lane_ids((1, LANES))
@@ -220,10 +222,13 @@
                 shaping = jnp.where(live, own_beam[:, pl.ds(start, LANES)], 0.0)
                 for c in range(2):
                     row = order * rows + start // LANES * 2 + c
-                    values = wide[pl.ds(row, maps, stride=ORD_DEV * rows + PAD), :]
+                    values = wide[pl.ds(row, own, stride=ORD_DEV * rows + PAD), :]
+                    shaped = jnp.concatenate(
+                        [values * shaping[k : k + 1] for k in range(groups)], 0
+                    )
                     lhs[pl.ds(at + c * maps, maps), pl.ds(i * TILE + t * LANES, LANES)] = (
-                        values * shaping
-                    ).astype(BF16)
+                        shaped.astype(BF16)
+                    )
 
     table_blocks = list(range(0, small.shape[1], 16))
     prepare(range(fixed))
@@ -260,6 +265,7 @@
 def forward(order_ids, beam, harm, legendre, nlon):
     degrees, lats = legendre.shape[1:]
     maps = harm.shape[0]
+    own = maps // beam.shape[0]
     orders = order_ids.shape[0]
     ids_row = order_ids.reshape(1, -1)
     live = degrees + TILE
@@ -277,9 +283,9 @@
         scratch_shapes=[
             pltpu.VMEM(ids_row.shape, jnp.int32),
             pltpu.VMEM(beam.shape, F32),
-            pltpu.VMEM((1, degrees), F32),
-            pltpu.VMEM(harm.shape, BF16),
-            pltpu.VMEM((maps * (ORD_DEV * harm.shape[2] + PAD), LANES), F32),
+            pltpu.VMEM(beam.shape, F32),
+            pltpu.VMEM((own,) + harm.shape[1:], BF16),
+            pltpu.VMEM((own * (ORD_DEV * harm.shape[2] + PAD), LANES), F32),
             pltpu.VMEM((ORD_DEV * 2 * maps, live), BF16),
             pltpu.VMEM((orders, orders), F32),
             pltpu.VMEM((2, orders, LANES), F32),
@@ -294,12 +300,14 @@
 
 
 def pixel_kernel(
-    groups, chunk, scales, got_ref, table_ref, sign_ref, weight_ref, out_ref, wide, lhs, mixed
+    groups, chunk, scales, got_ref, table_ref, sign_ref, *refs
 ):
+    weight_refs, (out_ref, wide, lhs, mixed) = refs[:groups], refs[groups:]
     fwd_scale, back_scale = scales
-    rows = weight_ref.shape[0]
+    rows = weight_refs[0].shape[0]
     pairs = got_ref.shape[0] // rows
     maps = got_ref.shape[1] // (2 * ORD_DEV)
+    own = maps // groups
     size = rows * maps
     half = table_ref.shape[1]
     wide[...] = got_ref[...].astype(F32)
@@ -323,16 +331,20 @@
         field = jnp.dot(lhs[...], part, preferred_element_type=F32)
         pieces = []
         for h in range(2):
-            weight = weight_ref[:, pl.ds(h * half + j * chunk, chunk)] * fwd_scale
+            span = pl.ds(h * half + j * chunk, chunk)
+            weights = [ref[:, span] * fwd_scale for ref in weight_refs]
             for r in range(rows):
                 at = h * size + r * maps
-                pieces.append((field[at : at + maps] * weight[r : r + 1]).astype(BF16))
+                part_rows = [
+                    field[at + k * own : at + (k + 1) * own] * weights[k][r : r + 1]
+                    for k in range(groups)
+                ]
+                pieces.append(jnp.concatenate(part_rows, 0).astype(BF16))
         total += lax.dot_general(
             jnp.concatenate(pieces, 0), part, (((1,), (1,)), ((), ())), preferred_element_type=F32
         )
     sign = jnp.concatenate(signs, 1)
     total = (total[:size] + total[size:] * sign) * back_scale
-    own = maps // groups
     low_rows = rows // 2
     for f in range(groups):
         pieces = []
@@ -346,18 +358,19 @@
                 )
         turned = jnp.concatenate(pieces, 0).T
         for high in range(2):
-            mixed[pl.ds(f * 2 * pairs + high, pairs, stride=2), :] = turned[
+            mixed[pl.ds(f * 2 + high, pairs, stride=2 * groups), :] = turned[
                 high * pairs : (high + 1) * pairs
             ]
     out_ref[...] = mixed[...].astype(BF16)
 
 
-def pixels(got, table, signs, weight, groups, scales, chunk=256):
+def pixels(got, table, signs, weights, scales, chunk=256):
+    groups = len(weights)
     return pl.pallas_call(
         lambda *refs: pixel_kernel(groups, chunk, scales, *refs),
         name="pixels",
         out_shape=pltpu.VMEM(got.shape, BF16),
-        in_specs=[pl.BlockSpec(memory_space=pltpu.VMEM)] * 4,
+        in_specs=[pl.BlockSpec(memory_space=pltpu.VMEM)] * (3 + groups),
         out_specs=pl.BlockSpec(memory_space=pltpu.VMEM),
         scratch_shapes=[
             pltpu.VMEM(got.shape, F32),
@@ -365,11 +378,11 @@
             pltpu.VMEM(got.shape, F32),
         ],
         compiler_params=limits(8),
-    )(on_chip(got), table, signs, on_chip(weight))
+    )(on_chip(got), table, signs, *[on_chip(w) for w in weights])
 
 
 def backward_kernel(
-    cuts, ids_vmem, beam_ref, got_ref, leg_ref, out_ref, mixed, terms, result, blank, ids_ref, sems, zero_sems
+    cuts, ids_vmem, beam_ref, got_ref, leg_ref, out_ref, beam_v, wide, mixed, terms, result, blank, ids_ref, sems, zero_sems
 ):
     ids_copy = pltpu.make_async_copy(ids_vmem, ids_ref, sems.at[cuts[-1]])
     ids_copy.start()
@@ -381,16 +394,23 @@
     lows = lats // span
     own = width // (2 * ORD_DEV)
     blank[...] = jnp.zeros_like(blank)
-    blocks = [got_ref[pl.ds(f * span, span), :].astype(F32) for f in range(groups)]
-    lane_group = lane_ids((span, LANES)) // width
-    turned = [
-        [v if k == 0 else pltpu.roll(v, k * width, 1) for k in range(groups)] for v in blocks
-    ]
-    for low in range(lows):
-        merged = turned[0][(0 - low) % groups]
-        for f in range(1, groups):
-            merged = jnp.where(lane_group == f, turned[f][(f - low) % groups], merged)
-        mixed[pl.ds(low, span, stride=lows), :] = merged
+    group = lax.axis_index("freq")
+    for k in range(groups):
+        beam_v[k : k + 1, :] = beam_ref[pl.ds(group ^ k, 1), :]
+    wide[...] = got_ref[...].astype(F32)
+    pitch = 2 * groups
+    devices = got_ref.shape[0] // pitch
+    lane_group = lane_ids((devices, LANES)) // width
+    for high in range(2):
+        turned = []
+        for k in range(groups):
+            v = wide[pl.ds(k * 2 + high, devices, stride=pitch), :]
+            turned.append([v if n == 0 else pltpu.roll(v, n * width, 1) for n in range(groups)])
+        for low in range(lows):
+            merged = turned[0][(0 - low) % groups]
+            for k in range(1, groups):
+                merged = jnp.where(lane_group == k, turned[k][(k - low) % groups], merged)
+            mixed[pl.ds(high * lows + low, devices, stride=2 * lows), :] = merged
     rhs = mixed[...].astype(BF16)
     lane = lane_ids((1, LANES))
     ids_copy.wait()
@@ -422,7 +442,7 @@
                 for f in range(groups):
                     at = pl.multiple_of(f * width + order * (2 * own), 2 * own)
                     part = terms[pl.ds(at, 2 * own), pl.ds(i * TILE + t * LANES, LANES)]
-                    shaping = jnp.where(live, beam_ref[f : f + 1, pl.ds(start, LANES)], 0.0)
+                    shaping = jnp.where(live, beam_v[f : f + 1, pl.ds(start, LANES)], 0.0)
                     total += part * shaping
                 for c in range(2):
                     result[i, :, t * 2 + c, :] = total[c * own : (c + 1) * own]
@@ -447,6 +467,8 @@
         in_specs=[pl.BlockSpec(memory_space=pltpu.VMEM)] * 4,
         out_specs=pl.BlockSpec(memory_space=pl.ANY),
         scratch_shapes=[
+            pltpu.VMEM(beam.shape, F32),
+            pltpu.VMEM(got.shape, F32),
             pltpu.VMEM((legendre.shape[1], LANES), F32),
             pltpu.VMEM((LANES, legendre.shape[0]), F32),
             pltpu.VMEM((tiles, own, per_tile, LANES), F32),
@@ -471,12 +493,16 @@
     scales = (1.0 / math.sqrt(2.0 * orders_all), 1.0 / math.sqrt(1.0 * nlon))
     harm = harmonics.reshape(maps, ORD_DEV, 2, tiles, LANES).transpose(0, 1, 3, 2, 4)
     harm = harm.reshape(maps, ORD_DEV, -1, LANES)
+    weights = [noise_weight[0]]
+    for k in range(1, groups):
+        pairing = [(i, i ^ k) for i in range(groups)]
+        weights.append(lax.ppermute(noise_weight[0], "freq", pairing))
     columns, legendre, table, signs = forward(order_ids, beam_window, harm, legendre, nlon)
     columns = columns.reshape(pairs, lats // pairs, -1)
     got = lax.all_to_all(columns, "order", split_axis=0, concat_axis=0, tiled=True)
-    terms = pixels(got.reshape(lats, -1), table, signs, noise_weight[0], groups, scales)
-    terms = terms.reshape(groups * pairs, -1, LANES)
-    back = lax.all_to_all(terms, ("freq", "order"), split_axis=0, concat_axis=0, tiled=True)
+    terms = pixels(got.reshape(lats, -1), table, signs, weights, scales)
+    terms = terms.reshape(pairs, -1, LANES)
+    back = lax.all_to_all(terms, "order", split_axis=0, concat_axis=0, tiled=True)
     out = backward(order_ids, beam_window, back.reshape(-1, LANES), legendre, own)
     out = out.reshape(own, ORD_DEV, tiles, 2, LANES).transpose(0, 1, 3, 2, 4)
     return out.reshape(own, ORD_DEV, 2, degrees)

time: 53.4 us -> 51.9 us (0.972); the launches traced: 53.2 us -> 51.1 us
  blocking collectives: 43.7 us -> 35.3 us
  starting transfers between devices: 0 us -> 6.34 us
    ppermute x0 -> x3, starting transfers between devices: none -> 6.34 us  [on_device(): weights.append(lax.ppermute(noise_weight[0], 'freq', pairing))]
    all_to_all x1, blocking collectives: 20.5 us -> 14.6 us  [on_device(): lax.all_to_all(terms, 'order', split_axis=0, concat_axis=0, tiled=True)]
    all_to_all x1, blocking collectives: 23.3 us -> 20.7 us  [on_device(): lax.all_to_all(columns, 'order', split_axis=0, concat_axis=0, tiled=True)]
  transfers between devices with their start and end apart: 0 -> 3, of which waited for: 0 -> 0; matrix products, arithmetic and copies ran while one was open for 0% -> 0% of each run, Pallas kernels for 0% -> 6%
where the time goes in v7:
time: 51.9 us; the launch traced here: 51.1 us
  blocking collectives  35.3 us (68%)
  Pallas kernels  9.43 us (18%)
  starting transfers between devices  6.34 us (12%)
    all_to_all x1, blocking collectives, on_device(): lax.all_to_all(columns, 'order', split_axis=0, concat_axis=0, tiled=True)  20.7 us
    all_to_all x1, blocking collectives, on_device(): lax.all_to_all(terms, 'order', split_axis=0, concat_axis=0, tiled=True)  14.6 us
    ppermute x3, starting transfers between devices, on_device(): weights.append(lax.ppermute(noise_weight[0], 'freq', pairing))  6.34 us
    pallas_call x1, Pallas kernels, forward(): pl.pallas_call(lambda *refs: forward_kernel(nlon, (8, 8), *refs), name='f...  3.3 us
    pallas_call x1, Pallas kernels, backward(): pl.pallas_call(lambda *refs: backward_kernel(cuts, *refs), name='backward...  3.21 us
    pallas_call x1, Pallas kernels, pixels(): pl.pallas_call(lambda *refs: pixel_kernel(groups, chunk, scales, *refs),...  2.92 us
  transfers between devices with their start and end apart: 3, of which 0 were waited for; matrix products, arithmetic and copies ran while one was open for 0% of the time, Pallas kernels for 6%

profile of v7, /device:TPU:1, one launch (start us, length us, event | category | flops | bytes accessed | tf_op | source)
XLA Modules:
  0.0 51.1 jit_solution(6571865145331430306)
XLA Ops:
  0.0 3.2 %collective-permute-start = (f32[8,8192]{1,0:T(8,128)}, f32[8,8192]{1,0:T(8,128)S(1)}, u32[]{:S(2)}, u32[]{:S(2)}) collective-permute-start(f32[8,8192]{1,0:T(8,128)} %bitcast.19), channel_id=1, source_target_pairs={{0,64},{64,0},{128,192},{192,128},{1,65},{65,1},{129,193},{193,129... | collective-permute-start | bytes 786440 | tf_op jit(solution)/shard_map/ppermute | solution.py:499
  3.2 1.0 %collective-permute-start.1 = (f32[8,8192]{1,0:T(8,128)}, f32[8,8192]{1,0:T(8,128)S(1)}, u32[]{:S(2)}, u32[]{:S(2)}) collective-permute-start(f32[8,8192]{1,0:T(8,128)} %bitcast.20), channel_id=1, source_target_pairs={{0,128},{64,192},{128,0},{192,64},{1,129},{65,193},{129,1},{193,65... | collective-permute-start | bytes 786440 | tf_op jit(solution)/shard_map/ppermute | solution.py:499
  4.2 2.1 %collective-permute-start.2 = (f32[8,8192]{1,0:T(8,128)}, f32[8,8192]{1,0:T(8,128)S(1)}, u32[]{:S(2)}, u32[]{:S(2)}) collective-permute-start(f32[8,8192]{1,0:T(8,128)} %bitcast.21), channel_id=1, source_target_pairs={{0,192},{64,128},{128,64},{192,0},{1,193},{65,129},{129,65},{193,1... | collective-permute-start | bytes 786440 | tf_op jit(solution)/shard_map/ppermute | solution.py:499
  6.3 0.0 copy-start.1
  6.3 0.0 copy-start
  6.3 0.0 copy-start.2
  6.3 3.3 %forward.1 = (bf16[512,128]{1,0:T(8,128)(2,1)S(1)}, bf16[4352,512]{1,0:T(8,128)(2,1)S(1)}, bf16[256,4096]{1,0:T(8,128)(2,1)S(1)}, f32[16,128]{1,0:T(8,128)S(1)}) custom-call(s32[128]{0:T(128)} %refs_0_.3, s32[1,128]{1,0:T(1,128)} %bitcast.24, f32[4,4096]{1,0:T(4,128)} %refs_1_.1, bf16[32,2,64,128]{3,2,1,0:T(8,128)(2,1)} %bitcast.25, ...), custom_call_target="tpu_custom_call" | custom-call | tf_op jit(solution)/shard_map/forward/pallas_call | solution.py:272
  9.7 20.7 %all_to_all.10 = bf16[64,8,128]{2,1,0:T(8,128)(2,1)S(1)} all-to-all(bf16[64,8,128]{2,1,0:T(8,128)(2,1)S(1)} %bitcast.23), channel_id=1, replica_groups=mesh['freq'=4,'order'=64] {'order'}, dimensions={0} | all-to-all | bytes 262144 | tf_op jit(solution)/shard_map/all_to_all | solution.py:502
  30.3 0.0 collective-permute-done.refs_4_
  30.3 0.0 collective-permute-done.1.refs_5_
  30.3 0.0 collective-permute-done.2.refs_6_
  30.3 0.0 copy-done.1
  30.3 2.9 %pixels.1 = bf16[512,128]{1,0:T(8,128)(2,1)S(1)} custom-call(bf16[512,128]{1,0:T(8,128)(2,1)S(1)} %bitcast.17, bf16[256,4096]{1,0:T(8,128)(2,1)S(1)} %get-tuple-element.10.refs_1_, f32[16,128]{1,0:T(8,128)S(1)} %get-tuple-element.11.refs_2_, f32[8,8192]{1,0:T(8,128)S(1)} %bitcast.22, f32[8,8192]{1,0:T(8,128)S(1)} %collective-permute-done.refs_4_, ...), custom_call_target="tpu_custom_call" | custom-call | tf_op jit(solution)/shard_map/pixels/pallas_call | solution.py:369
  33.3 14.6 %all_to_all.11 = bf16[64,8,128]{2,1,0:T(8,128)(2,1)S(1)} all-to-all(bf16[64,8,128]{2,1,0:T(8,128)(2,1)S(1)} %bitcast.18), channel_id=1, replica_groups=mesh['freq'=4,'order'=64] {'order'}, dimensions={0} | all-to-all | bytes 262144 | tf_op jit(solution)/shard_map/all_to_all | solution.py:505
  47.9 0.0 copy-done
  47.9 0.0 copy-done.2
  47.9 3.2 %backward.1 = f32[8,128,128]{2,1,0:T(8,128)} custom-call(s32[128]{0:T(128)S(1)} %copy-done.2, f32[4,4096]{1,0:T(4,128)S(1)} %copy-done, bf16[512,128]{1,0:T(8,128)(2,1)S(1)} %bitcast.16, bf16[4352,512]{1,0:T(8,128)(2,1)S(1)} %get-tuple-element.12.refs_3_), custom_call_target="tpu_custom_call" | custom-call | tf_op jit(solution)/shard_map/backward/pallas_call | solution.py:463
Async XLA Ops:
  0.0 30.3 %collective-permute-start = (f32[8,8192]{1,0:T(8,128)}, f32[8,8192]{1,0:T(8,128)S(1)}, u32[]{:S(2)}, u32[]{:S(2)}) collective-permute-start(f32[8,8192]{1,0:T(8,128)} %bitcast.19), channel_id=1, source_target_pairs={{0,64},{64,0},{128,192},{192,128},{1,65},{65,1},{129,193},{193,129... | collective-permute-start | bytes 786440 | tf_op jit(solution)/shard_map/ppermute | solution.py:499
  3.2 27.1 %collective-permute-start.1 = (f32[8,8192]{1,0:T(8,128)}, f32[8,8192]{1,0:T(8,128)S(1)}, u32[]{:S(2)}, u32[]{:S(2)}) collective-permute-start(f32[8,8192]{1,0:T(8,128)} %bitcast.20), channel_id=1, source_target_pairs={{0,128},{64,192},{128,0},{192,64},{1,129},{65,193},{129,1},{193,65... | collective-permute-start | bytes 786440 | tf_op jit(solution)/shard_map/ppermute | solution.py:499
  4.2 26.1 %collective-permute-start.2 = (f32[8,8192]{1,0:T(8,128)}, f32[8,8192]{1,0:T(8,128)S(1)}, u32[]{:S(2)}, u32[]{:S(2)}) collective-permute-start(f32[8,8192]{1,0:T(8,128)} %bitcast.21), channel_id=1, source_target_pairs={{0,192},{64,128},{128,64},{192,0},{1,193},{65,129},{129,65},{193,1... | collective-permute-start | bytes 786440 | tf_op jit(solution)/shard_map/ppermute | solution.py:499
  6.3 24.0 %copy-start.1 = (f32[1,8,8192]{2,1,0:T(8,128)S(1)}, f32[1,8,8192]{2,1,0:T(8,128)}, u32[]{:S(2)}) copy-start(f32[1,8,8192]{2,1,0:T(8,128)} %param.9) | copy-start | bytes 786436
  6.3 41.5 %copy-start = (f32[4,4096]{1,0:T(4,128)S(1)}, f32[4,4096]{1,0:T(4,128)}, u32[]{:S(2)}) copy-start(f32[4,4096]{1,0:T(4,128)} %refs_1_.1) | copy-start | bytes 196612
  6.3 41.5 %copy-start.2 = (s32[128]{0:T(128)S(1)}, s32[128]{0:T(128)}, u32[]{:S(2)}) copy-start(s32[128]{0:T(128)} %refs_0_.3) | copy-start | bytes 1540

commit v8 on v7

--- a/solution.py
+++ b/solution.py
@@ -302,9 +302,9 @@
 def pixel_kernel(
     groups, chunk, scales, got_ref, table_ref, sign_ref, *refs
 ):
-    weight_refs, (out_ref, wide, lhs, mixed) = refs[:groups], refs[groups:]
+    weight_refs, (out_ref, wide, lhs, mixed) = refs[: groups // 2], refs[groups // 2 :]
     fwd_scale, back_scale = scales
-    rows = weight_refs[0].shape[0]
+    rows = weight_refs[0].shape[0] // 2
     pairs = got_ref.shape[0] // rows
     maps = got_ref.shape[1] // (2 * ORD_DEV)
     own = maps // groups
@@ -332,7 +332,9 @@
         pieces = []
         for h in range(2):
             span = pl.ds(h * half + j * chunk, chunk)
-            weights = [ref[:, span] * fwd_scale for ref in weight_refs]
+            weights = [
+                weight_refs[k // 2][pl.ds(k % 2 * rows, rows), span] * fwd_scale for k in range(groups)
+            ]
             for r in range(rows):
                 at = h * size + r * maps
                 part_rows = [
@@ -365,12 +367,12 @@
 
 
 def pixels(got, table, signs, weights, scales, chunk=256):
-    groups = len(weights)
+    groups = 2 * len(weights)
     return pl.pallas_call(
         lambda *refs: pixel_kernel(groups, chunk, scales, *refs),
         name="pixels",
         out_shape=pltpu.VMEM(got.shape, BF16),
-        in_specs=[pl.BlockSpec(memory_space=pltpu.VMEM)] * (3 + groups),
+        in_specs=[pl.BlockSpec(memory_space=pltpu.VMEM)] * (3 + len(weights)),
         out_specs=pl.BlockSpec(memory_space=pltpu.VMEM),
         scratch_shapes=[
             pltpu.VMEM(got.shape, F32),
@@ -493,11 +495,12 @@
     scales = (1.0 / math.sqrt(2.0 * orders_all), 1.0 / math.sqrt(1.0 * nlon))
     harm = harmonics.reshape(maps, ORD_DEV, 2, tiles, LANES).transpose(0, 1, 3, 2, 4)
     harm = harm.reshape(maps, ORD_DEV, -1, LANES)
-    weights = [noise_weight[0]]
-    for k in range(1, groups):
-        pairing = [(i, i ^ k) for i in range(groups)]
-        weights.append(lax.ppermute(noise_weight[0], "freq", pairing))
+    own_weight = noise_weight[0]
+    near = lax.ppermute(own_weight, "freq", [(i, i ^ 1) for i in range(groups)])
     columns, legendre, table, signs = forward(order_ids, beam_window, harm, legendre, nlon)
+    signs, near = lax.optimization_barrier((signs, near))
+    pair = jnp.concatenate([own_weight, near], 0)
+    weights = [pair, lax.ppermute(pair, "freq", [(i, i ^ 2) for i in range(groups)])]
     columns = columns.reshape(pairs, lats // pairs, -1)
     got = lax.all_to_all(columns, "order", split_axis=0, concat_axis=0, tiled=True)
     terms = pixels(got.reshape(lats, -1), table, signs, weights, scales)

time: 51.9 us -> 50.8 us (0.979)
  starting transfers between devices: 6.34 us -> 4.32 us
  blocking collectives: 35.3 us -> 36.6 us
    ppermute x3 -> x2, starting transfers between devices: 6.34 us -> 4.32 us  [the longest x1 3.2 us: on_device(): near = lax.ppermute(own_weight, 'freq', [(i, i ^ 1) for i in range(groups)])]
    all_to_all x1, blocking collectives: 20.7 us -> 21.5 us  [on_device(): lax.all_to_all(columns, 'order', split_axis=0, concat_axis=0, tiled=True)]
    all_to_all x1, blocking collectives: 14.6 us -> 15.1 us  [on_device(): lax.all_to_all(terms, 'order', split_axis=0, concat_axis=0, tiled=True)]
  transfers between devices with their start and end apart: 3 -> 2, of which waited for: 0 -> 0; matrix products, arithmetic and copies ran while one was open for 0% -> 0% of each run, Pallas kernels for 6% -> 6%
where the time goes in v8:
time: 50.8 us; the launch traced here: 50.4 us
  blocking collectives  36.6 us (72%)
  Pallas kernels  9.37 us (18%)
  starting transfers between devices  4.32 us (9%)
    all_to_all x1, blocking collectives, on_device(): lax.all_to_all(columns, 'order', split_axis=0, concat_axis=0, tiled=True)  21.5 us
    all_to_all x1, blocking collectives, on_device(): lax.all_to_all(terms, 'order', split_axis=0, concat_axis=0, tiled=True)  15.1 us
    pallas_call x1, Pallas kernels, forward(): pl.pallas_call(lambda *refs: forward_kernel(nlon, (8, 8), *refs), name='f...  3.24 us
    pallas_call x1, Pallas kernels, backward(): pl.pallas_call(lambda *refs: backward_kernel(cuts, *refs), name='backward...  3.21 us
    ppermute x1, starting transfers between devices, on_device(): near = lax.ppermute(own_weight, 'freq', [(i, i ^ 1) for i in range(groups)])  3.2 us
    pallas_call x1, Pallas kernels, pixels(): pl.pallas_call(lambda *refs: pixel_kernel(groups, chunk, scales, *refs),...  2.92 us
    ppermute x1, starting transfers between devices, on_device(): lax.ppermute(pair, 'freq', [(i, i ^ 2) for i in range(groups)])  1.12 us
  transfers between devices with their start and end apart: 2, of which 0 were waited for; matrix products, arithmetic and copies ran while one was open for 0% of the time, Pallas kernels for 6%

profile of v8, /device:TPU:1, one launch (start us, length us, event | category | flops | bytes accessed | tf_op | source)
XLA Modules:
  0.0 50.4 jit_solution(4631978808378260347)
XLA Ops:
  0.0 3.2 %collective-permute-start = (f32[8,8192]{1,0:T(8,128)}, f32[8,8192]{1,0:T(8,128)S(1)}, u32[]{:S(2)}, u32[]{:S(2)}) collective-permute-start(f32[8,8192]{1,0:T(8,128)} %bitcast.22), channel_id=1, source_target_pairs={{0,64},{64,0},{128,192},{192,128},{1,65},{65,1},{129,193},{193,129... | collective-permute-start | bytes 786440 | tf_op jit(solution)/shard_map/ppermute | solution.py:499
  3.2 0.0 copy-start.2
  3.2 3.2 %forward.1 = (bf16[512,128]{1,0:T(8,128)(2,1)S(1)}, bf16[4352,512]{1,0:T(8,128)(2,1)S(1)}, bf16[256,4096]{1,0:T(8,128)(2,1)S(1)}, f32[16,128]{1,0:T(8,128)S(1)}) custom-call(s32[128]{0:T(128)} %refs_0_.3, s32[1,128]{1,0:T(1,128)} %bitcast.20, f32[4,4096]{1,0:T(4,128)} %refs_1_.1, bf16[32,2,64,128]{3,2,1,0:T(8,128)(2,1)} %bitcast.21, ...), custom_call_target="tpu_custom_call" | custom-call | tf_op jit(solution)/shard_map/forward/pallas_call | solution.py:272
  6.5 0.0 copy-start
  6.5 0.0 copy-start.1
  6.5 0.0 collective-permute-done
  6.5 0.0 copy-done.2
  6.5 1.1 %collective-permute-start.1 = (f32[16,8192]{1,0:T(8,128)S(1)}, f32[16,8192]{1,0:T(8,128)S(1)}, u32[]{:S(2)}, u32[]{:S(2)}) collective-permute-start(f32[16,8192]{1,0:T(8,128)S(1)} %pad_maximum_fusion.refs_3_), channel_id=1, source_target_pairs={{0,128},{64,192},{128,0},{192,64},{1,129},{65,193},{129,1},{193,65... | collective-permute-start | bytes 1572872 | tf_op jit(solution)/shard_map/ppermute | solution.py:503
  7.7 21.5 %all_to_all.10 = bf16[64,8,128]{2,1,0:T(8,128)(2,1)S(1)} all-to-all(bf16[64,8,128]{2,1,0:T(8,128)(2,1)S(1)} %bitcast.19), channel_id=1, replica_groups=mesh['freq'=4,'order'=64] {'order'}, dimensions={0} | all-to-all | bytes 262144 | tf_op jit(solution)/shard_map/all_to_all | solution.py:505
  29.1 0.0 collective-permute-done.1.refs_4_
  29.1 2.9 %pixels.1 = bf16[512,128]{1,0:T(8,128)(2,1)S(1)} custom-call(bf16[512,128]{1,0:T(8,128)(2,1)S(1)} %bitcast.17, bf16[256,4096]{1,0:T(8,128)(2,1)S(1)} %get-tuple-element.12.refs_1_, f32[16,128]{1,0:T(8,128)S(1)} %get-tuple-element.14.refs_2_, f32[16,8192]{1,0:T(8,128)S(1)} %pad_maximum_fusion.refs_3_, f32[16,8192]{1,0:T(8,128)S(1)} %collective-permute-done.1.refs_4_), custom_call_target="tpu_custom_call" | custom-call | tf_op jit(solution)/shard_map/pixels/pallas_call | solution.py:371
  32.1 15.1 %all_to_all.11 = bf16[64,8,128]{2,1,0:T(8,128)(2,1)S(1)} all-to-all(bf16[64,8,128]{2,1,0:T(8,128)(2,1)S(1)} %bitcast.18), channel_id=1, replica_groups=mesh['freq'=4,'order'=64] {'order'}, dimensions={0} | all-to-all | bytes 262144 | tf_op jit(solution)/shard_map/all_to_all | solution.py:508
  47.2 0.0 copy-done
  47.2 0.0 copy-done.1
  47.2 3.2 %backward.1 = f32[8,128,128]{2,1,0:T(8,128)} custom-call(s32[128]{0:T(128)S(1)} %copy-done.1, f32[4,4096]{1,0:T(4,128)S(1)} %copy-done, bf16[512,128]{1,0:T(8,128)(2,1)S(1)} %bitcast.16, bf16[4352,512]{1,0:T(8,128)(2,1)S(1)} %get-tuple-element.16.refs_3_), custom_call_target="tpu_custom_call" | custom-call | tf_op jit(solution)/shard_map/backward/pallas_call | solution.py:465
  (1 shorter events, 0.0 us)
Async XLA Ops:
  0.0 6.5 %collective-permute-start = (f32[8,8192]{1,0:T(8,128)}, f32[8,8192]{1,0:T(8,128)S(1)}, u32[]{:S(2)}, u32[]{:S(2)}) collective-permute-start(f32[8,8192]{1,0:T(8,128)} %bitcast.22), channel_id=1, source_target_pairs={{0,64},{64,0},{128,192},{192,128},{1,65},{65,1},{129,193},{193,129... | collective-permute-start | bytes 786440 | tf_op jit(solution)/shard_map/ppermute | solution.py:499
  3.2 3.3 %copy-start.2 = (f32[1,8,8192]{2,1,0:T(8,128)S(1)}, f32[1,8,8192]{2,1,0:T(8,128)}, u32[]{:S(2)}) copy-start(f32[1,8,8192]{2,1,0:T(8,128)} %param.9) | copy-start | bytes 786436
  6.5 40.8 %copy-start = (f32[4,4096]{1,0:T(4,128)S(1)}, f32[4,4096]{1,0:T(4,128)}, u32[]{:S(2)}) copy-start(f32[4,4096]{1,0:T(4,128)} %refs_1_.1) | copy-start | bytes 196612
  6.5 40.7 %copy-start.1 = (s32[128]{0:T(128)S(1)}, s32[128]{0:T(128)}, u32[]{:S(2)}) copy-start(s32[128]{0:T(128)} %refs_0_.3) | copy-start | bytes 1540
  6.5 22.6 %collective-permute-start.1 = (f32[16,8192]{1,0:T(8,128)S(1)}, f32[16,8192]{1,0:T(8,128)S(1)}, u32[]{:S(2)}, u32[]{:S(2)}) collective-permute-start(f32[16,8192]{1,0:T(8,128)S(1)} %pad_maximum_fusion.refs_3_), channel_id=1, source_target_pairs={{0,128},{64,192},{128,0},{192,64},{1,129},{65,193},{129,1},{193,65... | collective-permute-start | bytes 1572872 | tf_op jit(solution)/shard_map/ppermute | solution.py:503

commit v9 on v8

--- a/solution.py
+++ b/solution.py
@@ -148,9 +148,9 @@
     leg_v,
     table_ref,
     sign_ref,
+    own_beam,
     ids_row,
     beam_v,
-    own_beam,
     harm_v,
     wide,
     lhs,
@@ -277,12 +277,12 @@
             pltpu.VMEM((live, lats), BF16),
             pltpu.VMEM((2 * orders, nlon // 2), BF16),
             pltpu.VMEM((8 * ORD_DEV, LANES), F32),
+            pltpu.VMEM(beam.shape, F32),
         ),
         in_specs=[pl.BlockSpec(memory_space=pl.ANY)] * 5,
-        out_specs=(pl.BlockSpec(memory_space=pltpu.VMEM),) * 4,
+        out_specs=(pl.BlockSpec(memory_space=pltpu.VMEM),) * 5,
         scratch_shapes=[
             pltpu.VMEM(ids_row.shape, jnp.int32),
-            pltpu.VMEM(beam.shape, F32),
             pltpu.VMEM(beam.shape, F32),
             pltpu.VMEM((own,) + harm.shape[1:], BF16),
             pltpu.VMEM((own * (ORD_DEV * harm.shape[2] + PAD), LANES), F32),
@@ -384,7 +384,7 @@
 
 
 def backward_kernel(
-    cuts, ids_vmem, beam_ref, got_ref, leg_ref, out_ref, beam_v, wide, mixed, terms, result, blank, ids_ref, sems, zero_sems
+    cuts, ids_vmem, beam_ref, got_ref, leg_ref, out_ref, wide, mixed, terms, result, blank, ids_ref, sems, zero_sems
 ):
     ids_copy = pltpu.make_async_copy(ids_vmem, ids_ref, sems.at[cuts[-1]])
     ids_copy.start()
@@ -396,9 +396,6 @@
     lows = lats // span
     own = width // (2 * ORD_DEV)
     blank[...] = jnp.zeros_like(blank)
-    group = lax.axis_index("freq")
-    for k in range(groups):
-        beam_v[k : k + 1, :] = beam_ref[pl.ds(group ^ k, 1), :]
     wide[...] = got_ref[...].astype(F32)
     pitch = 2 * groups
     devices = got_ref.shape[0] // pitch
@@ -444,7 +441,7 @@
                 for f in range(groups):
                     at = pl.multiple_of(f * width + order * (2 * own), 2 * own)
                     part = terms[pl.ds(at, 2 * own), pl.ds(i * TILE + t * LANES, LANES)]
-                    shaping = jnp.where(live, beam_v[f : f + 1, pl.ds(start, LANES)], 0.0)
+                    shaping = jnp.where(live, beam_ref[f : f + 1, pl.ds(start, LANES)], 0.0)
                     total += part * shaping
                 for c in range(2):
                     result[i, :, t * 2 + c, :] = total[c * own : (c + 1) * own]
@@ -469,7 +466,6 @@
         in_specs=[pl.BlockSpec(memory_space=pltpu.VMEM)] * 4,
         out_specs=pl.BlockSpec(memory_space=pl.ANY),
         scratch_shapes=[
-            pltpu.VMEM(beam.shape, F32),
             pltpu.VMEM(got.shape, F32),
             pltpu.VMEM((legendre.shape[1], LANES), F32),
             pltpu.VMEM((LANES, legendre.shape[0]), F32),
@@ -480,7 +476,7 @@
             pltpu.SemaphoreType.DMA((degrees // TILE - 1,)),
         ],
         compiler_params=limits(8),
-    )(on_chip(order_ids), on_chip(beam), on_chip(got), legendre)
+    )(on_chip(order_ids), beam, on_chip(got), legendre)
 
 
 def on_device(harmonics, legendre, beam_window, order_ids, noise_weight):
@@ -497,7 +493,9 @@
     harm = harm.reshape(maps, ORD_DEV, -1, LANES)
     own_weight = noise_weight[0]
     near = lax.ppermute(own_weight, "freq", [(i, i ^ 1) for i in range(groups)])
-    columns, legendre, table, signs = forward(order_ids, beam_window, harm, legendre, nlon)
+    columns, legendre, table, signs, beam = forward(
+        order_ids, beam_window, harm, legendre, nlon
+    )
     signs, near = lax.optimization_barrier((signs, near))
     pair = jnp.concatenate([own_weight, near], 0)
     weights = [pair, lax.ppermute(pair, "freq", [(i, i ^ 2) for i in range(groups)])]
@@ -506,7 +504,7 @@
     terms = pixels(got.reshape(lats, -1), table, signs, weights, scales)
     terms = terms.reshape(pairs, -1, LANES)
     back = lax.all_to_all(terms, "order", split_axis=0, concat_axis=0, tiled=True)
-    out = backward(order_ids, beam_window, back.reshape(-1, LANES), legendre, own)
+    out = backward(order_ids, beam, back.reshape(-1, LANES), legendre, own)
     out = out.reshape(own, ORD_DEV, tiles, 2, LANES).transpose(0, 1, 3, 2, 4)
     return out.reshape(own, ORD_DEV, 2, degrees)
 

time: 50.8 us -> 50.6 us (level)
  no operation moved by 1% of the time
where the time goes in v9:
time: 50.6 us; the launch traced here: 50.2 us
  blocking collectives  36.6 us (72%)
  Pallas kernels  9.15 us (18%)
  starting transfers between devices  4.32 us (9%)
    all_to_all x1, blocking collectives, on_device(): lax.all_to_all(columns, 'order', split_axis=0, concat_axis=0, tiled=True)  21.5 us
    all_to_all x1, blocking collectives, on_device(): lax.all_to_all(terms, 'order', split_axis=0, concat_axis=0, tiled=True)  15.1 us
    pallas_call x1, Pallas kernels, forward(): pl.pallas_call(lambda *refs: forward_kernel(nlon, (8, 8), *refs), name='f...  3.24 us
    ppermute x1, starting transfers between devices, on_device(): near = lax.ppermute(own_weight, 'freq', [(i, i ^ 1) for i in range(groups)])  3.2 us
    pallas_call x1, Pallas kernels, backward(): pl.pallas_call(lambda *refs: backward_kernel(cuts, *refs), name='backward...  3 us
    pallas_call x1, Pallas kernels, pixels(): pl.pallas_call(lambda *refs: pixel_kernel(groups, chunk, scales, *refs),...  2.92 us
    ppermute x1, starting transfers between devices, on_device(): lax.ppermute(pair, 'freq', [(i, i ^ 2) for i in range(groups)])  1.12 us
  transfers between devices with their start and end apart: 2, of which 0 were waited for; matrix products, arithmetic and copies ran while one was open for 0% of the time, Pallas kernels for 6%

profile of v9, /device:TPU:1, one launch (start us, length us, event | category | flops | bytes accessed | tf_op | source)
XLA Modules:
  0.0 50.2 jit_solution(4137934660493370929)
XLA Ops:
  0.0 3.2 %collective-permute-start = (f32[8,8192]{1,0:T(8,128)}, f32[8,8192]{1,0:T(8,128)S(1)}, u32[]{:S(2)}, u32[]{:S(2)}) collective-permute-start(f32[8,8192]{1,0:T(8,128)} %bitcast.22), channel_id=1, source_target_pairs={{0,64},{64,0},{128,192},{192,128},{1,65},{65,1},{129,193},{193,129... | collective-permute-start | bytes 786440 | tf_op jit(solution)/shard_map/ppermute | solution.py:495
  3.2 0.0 copy-start.1
  3.2 3.2 %forward.1 = (bf16[512,128]{1,0:T(8,128)(2,1)S(1)}, bf16[4352,512]{1,0:T(8,128)(2,1)S(1)}, bf16[256,4096]{1,0:T(8,128)(2,1)S(1)}, f32[16,128]{1,0:T(8,128)S(1)}, f32[4,4096]{1,0:T(4,128)S(1)}) custom-call(s32[128]{0:T(128)} %refs_0_.3, s32[1,128]{1,0:T(1,128)} %bitcast.20, f32[4,4096]{1,0:T(4,128)} %refs_2_.1, bf16[32,2,64,128]{3,2,1,0:T(8,128)(2,1)} %bitcast.21, ...), custom_call_target="tpu_custom_call" | custom-call | tf_op jit(solution)/shard_map/forward/pallas_call | solution.py:272
  6.5 0.0 copy-start
  6.5 0.0 collective-permute-done
  6.5 0.0 copy-done.1
  6.5 1.1 %collective-permute-start.1 = (f32[16,8192]{1,0:T(8,128)S(1)}, f32[16,8192]{1,0:T(8,128)S(1)}, u32[]{:S(2)}, u32[]{:S(2)}) collective-permute-start(f32[16,8192]{1,0:T(8,128)S(1)} %pad_maximum_fusion.refs_3_), channel_id=1, source_target_pairs={{0,128},{64,192},{128,0},{192,64},{1,129},{65,193},{129,1},{193,65... | collective-permute-start | bytes 1572872 | tf_op jit(solution)/shard_map/ppermute | solution.py:501
  7.7 21.5 %all_to_all.10 = bf16[64,8,128]{2,1,0:T(8,128)(2,1)S(1)} all-to-all(bf16[64,8,128]{2,1,0:T(8,128)(2,1)S(1)} %bitcast.19), channel_id=1, replica_groups=mesh['freq'=4,'order'=64] {'order'}, dimensions={0} | all-to-all | bytes 262144 | tf_op jit(solution)/shard_map/all_to_all | solution.py:503
  29.1 0.0 collective-permute-done.1.refs_4_
  29.1 2.9 %pixels.1 = bf16[512,128]{1,0:T(8,128)(2,1)S(1)} custom-call(bf16[512,128]{1,0:T(8,128)(2,1)S(1)} %bitcast.17, bf16[256,4096]{1,0:T(8,128)(2,1)S(1)} %get-tuple-element.14.refs_1_, f32[16,128]{1,0:T(8,128)S(1)} %get-tuple-element.16.refs_2_, f32[16,8192]{1,0:T(8,128)S(1)} %pad_maximum_fusion.refs_3_, f32[16,8192]{1,0:T(8,128)S(1)} %collective-permute-done.1.refs_4_), custom_call_target="tpu_custom_call" | custom-call | tf_op jit(solution)/shard_map/pixels/pallas_call | solution.py:371
  32.0 15.1 %all_to_all.11 = bf16[64,8,128]{2,1,0:T(8,128)(2,1)S(1)} all-to-all(bf16[64,8,128]{2,1,0:T(8,128)(2,1)S(1)} %bitcast.18), channel_id=1, replica_groups=mesh['freq'=4,'order'=64] {'order'}, dimensions={0} | all-to-all | bytes 262144 | tf_op jit(solution)/shard_map/all_to_all | solution.py:506
  47.2 0.0 copy-done
  47.2 3.0 %backward.1 = f32[8,128,128]{2,1,0:T(8,128)} custom-call(s32[128]{0:T(128)S(1)} %copy-done, f32[4,4096]{1,0:T(4,128)S(1)} %get-tuple-element.12.refs_1_, bf16[512,128]{1,0:T(8,128)(2,1)S(1)} %bitcast.16, bf16[4352,512]{1,0:T(8,128)(2,1)S(1)} %get-tuple-element.18.refs_3_), custom_call_target="tpu_custom_call" | custom-call | tf_op jit(solution)/shard_map/backward/pallas_call | solution.py:462
  (1 shorter events, 0.0 us)
Async XLA Ops:
  0.0 6.5 %collective-permute-start = (f32[8,8192]{1,0:T(8,128)}, f32[8,8192]{1,0:T(8,128)S(1)}, u32[]{:S(2)}, u32[]{:S(2)}) collective-permute-start(f32[8,8192]{1,0:T(8,128)} %bitcast.22), channel_id=1, source_target_pairs={{0,64},{64,0},{128,192},{192,128},{1,65},{65,1},{129,193},{193,129... | collective-permute-start | bytes 786440 | tf_op jit(solution)/shard_map/ppermute | solution.py:495
  3.2 3.3 %copy-start.1 = (f32[1,8,8192]{2,1,0:T(8,128)S(1)}, f32[1,8,8192]{2,1,0:T(8,128)}, u32[]{:S(2)}) copy-start(f32[1,8,8192]{2,1,0:T(8,128)} %param.9) | copy-start | bytes 786436
  6.5 40.7 %copy-start = (s32[128]{0:T(128)S(1)}, s32[128]{0:T(128)}, u32[]{:S(2)}) copy-start(s32[128]{0:T(128)} %refs_0_.3) | copy-start | bytes 1540
  6.5 22.6 %collective-permute-start.1 = (f32[16,8192]{1,0:T(8,128)S(1)}, f32[16,8192]{1,0:T(8,128)S(1)}, u32[]{:S(2)}, u32[]{:S(2)}) collective-permute-start(f32[16,8192]{1,0:T(8,128)S(1)} %pad_maximum_fusion.refs_3_), channel_id=1, source_target_pairs={{0,128},{64,192},{128,0},{192,64},{1,129},{65,193},{129,1},{193,65... | collective-permute-start | bytes 1572872 | tf_op jit(solution)/shard_map/ppermute | solution.py:501

commit v10 on v9

--- a/solution.py
+++ b/solution.py
@@ -396,9 +396,12 @@
     lows = lats // span
     own = width // (2 * ORD_DEV)
     blank[...] = jnp.zeros_like(blank)
-    wide[...] = got_ref[...].astype(F32)
-    pitch = 2 * groups
-    devices = got_ref.shape[0] // pitch
+    rows_per = 2 * groups
+    devices = got_ref.shape[0] // rows_per
+    pitch = rows_per + 1
+    values = got_ref[...].astype(F32)
+    for d in range(devices):
+        wide[pl.ds(d * pitch, rows_per), :] = values[d * rows_per : (d + 1) * rows_per]
     lane_group = lane_ids((devices, LANES)) // width
     for high in range(2):
         turned = []
@@ -421,12 +424,6 @@
         return pl.ds(order * per_order + start // LANES * 2, per_tile)
 
     copies = []
-    for k, (order, start) in enumerate(dead_steps(ids_ref, slot, degrees)):
-        copy = pltpu.make_async_copy(
-            blank, out_ref.at[:, out_rows(order, start), :], zero_sems.at[k]
-        )
-        copy.start()
-        copies.append(copy)
     for lo, hi in zip(cuts[:-1], cuts[1:]):
         cols = pl.ds(lo * TILE, (hi - lo) * TILE)
         terms[:, cols] = jnp.dot(leg_ref[cols, :], rhs, preferred_element_type=F32).T
@@ -450,6 +447,12 @@
             )
             copy.start()
             copies.append(copy)
+    for k, (order, start) in enumerate(dead_steps(ids_ref, slot, degrees)):
+        copy = pltpu.make_async_copy(
+            blank, out_ref.at[:, out_rows(order, start), :], zero_sems.at[k]
+        )
+        copy.start()
+        copies.append(copy)
     for copy in copies:
         copy.wait()
 
@@ -466,7 +469,7 @@
         in_specs=[pl.BlockSpec(memory_space=pltpu.VMEM)] * 4,
         out_specs=pl.BlockSpec(memory_space=pl.ANY),
         scratch_shapes=[
-            pltpu.VMEM(got.shape, F32),
+            pltpu.VMEM((got.shape[0] // 8 * 9, LANES), F32),
             pltpu.VMEM((legendre.shape[1], LANES), F32),
             pltpu.VMEM((LANES, legendre.shape[0]), F32),
             pltpu.VMEM((tiles, own, per_tile, LANES), F32),

time: 50.6 us -> 50.5 us (level)
  no operation moved by 1% of the time
where the time goes in v10:
time: 50.5 us; the launch traced here: 50.1 us
  blocking collectives  36.6 us (72%)
  Pallas kernels  9.11 us (18%)
  starting transfers between devices  4.32 us (9%)
    all_to_all x1, blocking collectives, on_device(): lax.all_to_all(columns, 'order', split_axis=0, concat_axis=0, tiled=True)  21.5 us
    all_to_all x1, blocking collectives, on_device(): lax.all_to_all(terms, 'order', split_axis=0, concat_axis=0, tiled=True)  15.1 us
    pallas_call x1, Pallas kernels, forward(): pl.pallas_call(lambda *refs: forward_kernel(nlon, (8, 8), *refs), name='f...  3.24 us
    ppermute x1, starting transfers between devices, on_device(): near = lax.ppermute(own_weight, 'freq', [(i, i ^ 1) for i in range(groups)])  3.2 us
    pallas_call x1, Pallas kernels, backward(): pl.pallas_call(lambda *refs: backward_kernel(cuts, *refs), name='backward...  2.96 us
    pallas_call x1, Pallas kernels, pixels(): pl.pallas_call(lambda *refs: pixel_kernel(groups, chunk, scales, *refs),...  2.92 us
    ppermute x1, starting transfers between devices, on_device(): lax.ppermute(pair, 'freq', [(i, i ^ 2) for i in range(groups)])  1.12 us
  transfers between devices with their start and end apart: 2, of which 0 were waited for; matrix products, arithmetic and copies ran while one was open for 0% of the time, Pallas kernels for 6%

profile of v10, /device:TPU:1, one launch (start us, length us, event | category | flops | bytes accessed | tf_op | source)
XLA Modules:
  0.0 50.1 jit_solution(16473533003744141923)
XLA Ops:
  0.0 3.2 %collective-permute-start = (f32[8,8192]{1,0:T(8,128)}, f32[8,8192]{1,0:T(8,128)S(1)}, u32[]{:S(2)}, u32[]{:S(2)}) collective-permute-start(f32[8,8192]{1,0:T(8,128)} %bitcast.22), channel_id=1, source_target_pairs={{0,64},{64,0},{128,192},{192,128},{1,65},{65,1},{129,193},{193,129... | collective-permute-start | bytes 786440 | tf_op jit(solution)/shard_map/ppermute | solution.py:498
  3.2 0.0 copy-start.1
  3.2 3.2 %forward.1 = (bf16[512,128]{1,0:T(8,128)(2,1)S(1)}, bf16[4352,512]{1,0:T(8,128)(2,1)S(1)}, bf16[256,4096]{1,0:T(8,128)(2,1)S(1)}, f32[16,128]{1,0:T(8,128)S(1)}, f32[4,4096]{1,0:T(4,128)S(1)}) custom-call(s32[128]{0:T(128)} %refs_0_.3, s32[1,128]{1,0:T(1,128)} %bitcast.20, f32[4,4096]{1,0:T(4,128)} %refs_2_.1, bf16[32,2,64,128]{3,2,1,0:T(8,128)(2,1)} %bitcast.21, ...), custom_call_target="tpu_custom_call" | custom-call | tf_op jit(solution)/shard_map/forward/pallas_call | solution.py:272
  6.5 0.0 copy-start
  6.5 0.0 collective-permute-done
  6.5 0.0 copy-done.1
  6.5 1.1 %collective-permute-start.1 = (f32[16,8192]{1,0:T(8,128)S(1)}, f32[16,8192]{1,0:T(8,128)S(1)}, u32[]{:S(2)}, u32[]{:S(2)}) collective-permute-start(f32[16,8192]{1,0:T(8,128)S(1)} %pad_maximum_fusion.refs_3_), channel_id=1, source_target_pairs={{0,128},{64,192},{128,0},{192,64},{1,129},{65,193},{129,1},{193,65... | collective-permute-start | bytes 1572872 | tf_op jit(solution)/shard_map/ppermute | solution.py:504
  7.7 21.5 %all_to_all.10 = bf16[64,8,128]{2,1,0:T(8,128)(2,1)S(1)} all-to-all(bf16[64,8,128]{2,1,0:T(8,128)(2,1)S(1)} %bitcast.19), channel_id=1, replica_groups=mesh['freq'=4,'order'=64] {'order'}, dimensions={0} | all-to-all | bytes 262144 | tf_op jit(solution)/shard_map/all_to_all | solution.py:506
  29.1 0.0 collective-permute-done.1.refs_4_
  29.1 2.9 %pixels.1 = bf16[512,128]{1,0:T(8,128)(2,1)S(1)} custom-call(bf16[512,128]{1,0:T(8,128)(2,1)S(1)} %bitcast.17, bf16[256,4096]{1,0:T(8,128)(2,1)S(1)} %get-tuple-element.14.refs_1_, f32[16,128]{1,0:T(8,128)S(1)} %get-tuple-element.16.refs_2_, f32[16,8192]{1,0:T(8,128)S(1)} %pad_maximum_fusion.refs_3_, f32[16,8192]{1,0:T(8,128)S(1)} %collective-permute-done.1.refs_4_), custom_call_target="tpu_custom_call" | custom-call | tf_op jit(solution)/shard_map/pixels/pallas_call | solution.py:371
  32.0 15.1 %all_to_all.11 = bf16[64,8,128]{2,1,0:T(8,128)(2,1)S(1)} all-to-all(bf16[64,8,128]{2,1,0:T(8,128)(2,1)S(1)} %bitcast.18), channel_id=1, replica_groups=mesh['freq'=4,'order'=64] {'order'}, dimensions={0} | all-to-all | bytes 262144 | tf_op jit(solution)/shard_map/all_to_all | solution.py:509
  47.2 0.0 copy-done
  47.2 3.0 %backward.1 = f32[8,128,128]{2,1,0:T(8,128)} custom-call(s32[128]{0:T(128)S(1)} %copy-done, f32[4,4096]{1,0:T(4,128)S(1)} %get-tuple-element.12.refs_1_, bf16[512,128]{1,0:T(8,128)(2,1)S(1)} %bitcast.16, bf16[4352,512]{1,0:T(8,128)(2,1)S(1)} %get-tuple-element.18.refs_3_), custom_call_target="tpu_custom_call" | custom-call | tf_op jit(solution)/shard_map/backward/pallas_call | solution.py:465
  (1 shorter events, 0.0 us)
Async XLA Ops:
  0.0 6.5 %collective-permute-start = (f32[8,8192]{1,0:T(8,128)}, f32[8,8192]{1,0:T(8,128)S(1)}, u32[]{:S(2)}, u32[]{:S(2)}) collective-permute-start(f32[8,8192]{1,0:T(8,128)} %bitcast.22), channel_id=1, source_target_pairs={{0,64},{64,0},{128,192},{192,128},{1,65},{65,1},{129,193},{193,129... | collective-permute-start | bytes 786440 | tf_op jit(solution)/shard_map/ppermute | solution.py:498
  3.2 3.3 %copy-start.1 = (f32[1,8,8192]{2,1,0:T(8,128)S(1)}, f32[1,8,8192]{2,1,0:T(8,128)}, u32[]{:S(2)}) copy-start(f32[1,8,8192]{2,1,0:T(8,128)} %param.9) | copy-start | bytes 786436
  6.5 40.7 %copy-start = (s32[128]{0:T(128)S(1)}, s32[128]{0:T(128)}, u32[]{:S(2)}) copy-start(s32[128]{0:T(128)} %refs_0_.3) | copy-start | bytes 1540
  6.5 22.6 %collective-permute-start.1 = (f32[16,8192]{1,0:T(8,128)S(1)}, f32[16,8192]{1,0:T(8,128)S(1)}, u32[]{:S(2)}, u32[]{:S(2)}) collective-permute-start(f32[16,8192]{1,0:T(8,128)S(1)} %pad_maximum_fusion.refs_3_), channel_id=1, source_target_pairs={{0,128},{64,192},{128,0},{192,64},{1,129},{65,193},{129,1},{193,65... | collective-permute-start | bytes 1572872 | tf_op jit(solution)/shard_map/ppermute | solution.py:504

commit v11 on v10

--- a/solution.py
+++ b/solution.py
@@ -270,7 +270,7 @@
     ids_row = order_ids.reshape(1, -1)
     live = degrees + TILE
     return pl.pallas_call(
-        lambda *refs: forward_kernel(nlon, (8, 8), *refs),
+        lambda *refs: forward_kernel(nlon, (4, 8), *refs),
         name="forward",
         out_shape=(
             pltpu.VMEM((lats, ORD_DEV * 2 * maps), BF16),

time: 50.5 us -> 50.5 us (level)
  no operation moved by 1% of the time
where the time goes in v11:
time: 50.5 us; the launch traced here: 50.1 us
  blocking collectives  36.6 us (72%)
  Pallas kernels  9.1 us (18%)
  starting transfers between devices  4.32 us (9%)
    all_to_all x1, blocking collectives, on_device(): lax.all_to_all(columns, 'order', split_axis=0, concat_axis=0, tiled=True)  21.5 us
    all_to_all x1, blocking collectives, on_device(): lax.all_to_all(terms, 'order', split_axis=0, concat_axis=0, tiled=True)  15.1 us
    pallas_call x1, Pallas kernels, forward(): pl.pallas_call(lambda *refs: forward_kernel(nlon, (4, 8), *refs), name='f...  3.24 us
    ppermute x1, starting transfers between devices, on_device(): near = lax.ppermute(own_weight, 'freq', [(i, i ^ 1) for i in range(groups)])  3.2 us
    pallas_call x1, Pallas kernels, backward(): pl.pallas_call(lambda *refs: backward_kernel(cuts, *refs), name='backward...  2.95 us
    pallas_call x1, Pallas kernels, pixels(): pl.pallas_call(lambda *refs: pixel_kernel(groups, chunk, scales, *refs),...  2.92 us
    ppermute x1, starting transfers between devices, on_device(): lax.ppermute(pair, 'freq', [(i, i ^ 2) for i in range(groups)])  1.12 us
  transfers between devices with their start and end apart: 2, of which 0 were waited for; matrix products, arithmetic and copies ran while one was open for 0% of the time, Pallas kernels for 6%

profile of v11, /device:TPU:1, one launch (start us, length us, event | category | flops | bytes accessed | tf_op | source)
XLA Modules:
  0.0 50.1 jit_solution(14141686504131286373)
XLA Ops:
  0.0 3.2 %collective-permute-start = (f32[8,8192]{1,0:T(8,128)}, f32[8,8192]{1,0:T(8,128)S(1)}, u32[]{:S(2)}, u32[]{:S(2)}) collective-permute-start(f32[8,8192]{1,0:T(8,128)} %bitcast.22), channel_id=1, source_target_pairs={{0,64},{64,0},{128,192},{192,128},{1,65},{65,1},{129,193},{193,129... | collective-permute-start | bytes 786440 | tf_op jit(solution)/shard_map/ppermute | solution.py:498
  3.2 0.0 copy-start.1
  3.2 3.2 %forward.1 = (bf16[512,128]{1,0:T(8,128)(2,1)S(1)}, bf16[4352,512]{1,0:T(8,128)(2,1)S(1)}, bf16[256,4096]{1,0:T(8,128)(2,1)S(1)}, f32[16,128]{1,0:T(8,128)S(1)}, f32[4,4096]{1,0:T(4,128)S(1)}) custom-call(s32[128]{0:T(128)} %refs_0_.3, s32[1,128]{1,0:T(1,128)} %bitcast.20, f32[4,4096]{1,0:T(4,128)} %refs_2_.1, bf16[32,2,64,128]{3,2,1,0:T(8,128)(2,1)} %bitcast.21, ...), custom_call_target="tpu_custom_call" | custom-call | tf_op jit(solution)/shard_map/forward/pallas_call | solution.py:272
  6.5 0.0 copy-start
  6.5 0.0 collective-permute-done
  6.5 0.0 copy-done.1
  6.5 1.1 %collective-permute-start.1 = (f32[16,8192]{1,0:T(8,128)S(1)}, f32[16,8192]{1,0:T(8,128)S(1)}, u32[]{:S(2)}, u32[]{:S(2)}) collective-permute-start(f32[16,8192]{1,0:T(8,128)S(1)} %pad_maximum_fusion.refs_3_), channel_id=1, source_target_pairs={{0,128},{64,192},{128,0},{192,64},{1,129},{65,193},{129,1},{193,65... | collective-permute-start | bytes 1572872 | tf_op jit(solution)/shard_map/ppermute | solution.py:504
  7.7 21.5 %all_to_all.10 = bf16[64,8,128]{2,1,0:T(8,128)(2,1)S(1)} all-to-all(bf16[64,8,128]{2,1,0:T(8,128)(2,1)S(1)} %bitcast.19), channel_id=1, replica_groups=mesh['freq'=4,'order'=64] {'order'}, dimensions={0} | all-to-all | bytes 262144 | tf_op jit(solution)/shard_map/all_to_all | solution.py:506
  29.1 0.0 collective-permute-done.1.refs_4_
  29.1 2.9 %pixels.1 = bf16[512,128]{1,0:T(8,128)(2,1)S(1)} custom-call(bf16[512,128]{1,0:T(8,128)(2,1)S(1)} %bitcast.17, bf16[256,4096]{1,0:T(8,128)(2,1)S(1)} %get-tuple-element.14.refs_1_, f32[16,128]{1,0:T(8,128)S(1)} %get-tuple-element.16.refs_2_, f32[16,8192]{1,0:T(8,128)S(1)} %pad_maximum_fusion.refs_3_, f32[16,8192]{1,0:T(8,128)S(1)} %collective-permute-done.1.refs_4_), custom_call_target="tpu_custom_call" | custom-call | tf_op jit(solution)/shard_map/pixels/pallas_call | solution.py:371
  32.0 15.1 %all_to_all.11 = bf16[64,8,128]{2,1,0:T(8,128)(2,1)S(1)} all-to-all(bf16[64,8,128]{2,1,0:T(8,128)(2,1)S(1)} %bitcast.18), channel_id=1, replica_groups=mesh['freq'=4,'order'=64] {'order'}, dimensions={0} | all-to-all | bytes 262144 | tf_op jit(solution)/shard_map/all_to_all | solution.py:509
  47.2 0.0 copy-done
  47.2 2.9 %backward.1 = f32[8,128,128]{2,1,0:T(8,128)} custom-call(s32[128]{0:T(128)S(1)} %copy-done, f32[4,4096]{1,0:T(4,128)S(1)} %get-tuple-element.12.refs_1_, bf16[512,128]{1,0:T(8,128)(2,1)S(1)} %bitcast.16, bf16[4352,512]{1,0:T(8,128)(2,1)S(1)} %get-tuple-element.18.refs_3_), custom_call_target="tpu_custom_call" | custom-call | tf_op jit(solution)/shard_map/backward/pallas_call | solution.py:465
  (1 shorter events, 0.0 us)
Async XLA Ops:
  0.0 6.5 %collective-permute-start = (f32[8,8192]{1,0:T(8,128)}, f32[8,8192]{1,0:T(8,128)S(1)}, u32[]{:S(2)}, u32[]{:S(2)}) collective-permute-start(f32[8,8192]{1,0:T(8,128)} %bitcast.22), channel_id=1, source_target_pairs={{0,64},{64,0},{128,192},{192,128},{1,65},{65,1},{129,193},{193,129... | collective-permute-start | bytes 786440 | tf_op jit(solution)/shard_map/ppermute | solution.py:498
  3.2 3.3 %copy-start.1 = (f32[1,8,8192]{2,1,0:T(8,128)S(1)}, f32[1,8,8192]{2,1,0:T(8,128)}, u32[]{:S(2)}) copy-start(f32[1,8,8192]{2,1,0:T(8,128)} %param.9) | copy-start | bytes 786436
  6.5 40.7 %copy-start = (s32[128]{0:T(128)S(1)}, s32[128]{0:T(128)}, u32[]{:S(2)}) copy-start(s32[128]{0:T(128)} %refs_0_.3) | copy-start | bytes 1540
  6.5 22.6 %collective-permute-start.1 = (f32[16,8192]{1,0:T(8,128)S(1)}, f32[16,8192]{1,0:T(8,128)S(1)}, u32[]{:S(2)}, u32[]{:S(2)}) collective-permute-start(f32[16,8192]{1,0:T(8,128)S(1)} %pad_maximum_fusion.refs_3_), channel_id=1, source_target_pairs={{0,128},{64,192},{128,0},{192,64},{1,129},{65,193},{129,1},{193,65... | collective-permute-start | bytes 1572872 | tf_op jit(solution)/shard_map/ppermute | solution.py:504
